TPU v7x, 256 devices: a whole 4x4x8 slice. The times are simulated.
256 devices in a mesh: seq: 16 (over z, core), rep: 16 (over x, y).
Axes of the slice: x: 4, y: 4, z: 8, core: 2. Of those that a mesh axis runs over, the one named last changes fastest.
Arguments:
- tokens: bfloat16 [65536, 1024], P(('rep', 'seq')), parts along dimension 0, may hold values from -16 to 16
- segments: int32 [65536], P(('rep', 'seq')), parts along dimension 0, may hold values from 0 to 3, never falling along the last dimension, each value on 1 to 2048 neighbouring positions
- qkv_weight: bfloat16 [1024, 3072], replicated, may hold values from -1 to 1
- out_weight: bfloat16 [1024, 1024], replicated, may hold values from -0.1875 to 0.1875
- out_bias: float32 [1024], replicated, may hold values from -3 to 3
- ln_gain: float32 [1024], replicated, may hold values from 0.1 to 1.9
- ln_bias: float32 [1024], replicated, may hold values from -3 to 3
Outputs:
- normed: bfloat16 [65536, 1024], P(('rep', 'seq')), parts along dimension 0
- kv_cache: bfloat16 [65536, 2048], P('rep', 'seq'), parts along dimension 0
There are 16 independent parts, one for each index of `rep`. A program takes and returns all parts, laid end to end along the dimension named above; an argument that names none is the same for every part. Nothing has to cross between parts.
Inputs may be any that keep to these rules, and one draw needn't show every extreme that they name: `segments`: each prompt is a contiguous run of 1 to 2048 tokens, numbers never falling, one prompt exactly 2048 tokens.
All inputs are finite; a program needn't handle non-finite values.
Results may differ from a plain program's by a relative error of at most 0.008.
Values may be sent and summed in bfloat16 or wider, within the bound.
A program may use at most 128 MiB of HBM per device.

v0:
```python
import math

import jax
import jax.numpy as jnp
from jax import lax
from jax.sharding import PartitionSpec as P

HEADS = 16
HEAD = 64


def shards(tokens, segments, qkv_weight, out_weight, out_bias, ln_gain, ln_bias):
    tok_rows, width = tokens.shape
    scale = 1.0 / math.sqrt(HEAD)
    all_seg = lax.all_gather(segments, "seq", axis=0, tiled=True)
    proj = jnp.dot(tokens, qkv_weight, preferred_element_type=jnp.float32).astype(jnp.bfloat16)
    grouped = proj.reshape(tok_rows, HEADS, 3, HEAD)
    key_value = grouped[:, :, 1:, :].reshape(tok_rows, 2 * width)
    kv_cache = lax.all_to_all(key_value, "seq", split_axis=1, concat_axis=0, tiled=True)
    queries = jnp.moveaxis(grouped[:, :, 0, :], 1, 0)
    piece = lax.all_gather(key_value, "seq", axis=0, tiled=True)
    top_now = jnp.full((HEADS, tok_rows), -1e30, jnp.float32)
    total_now = jnp.zeros((HEADS, tok_rows), jnp.float32)
    acc_now = jnp.zeros((HEADS, tok_rows, HEAD), jnp.float32)
    count_rows = piece.shape[0]
    kept = segments[:, None] == all_seg[None, :]
    split_piece = piece.reshape(count_rows, HEADS, 2, HEAD)
    keys = jnp.moveaxis(split_piece[:, :, 0, :], 1, 0)
    values = jnp.moveaxis(split_piece[:, :, 1, :], 1, 0)

    def per_head(items):
        query, key_h, value_h, top_h, total_h, acc_h = items
        score = jnp.dot(query, key_h.T, preferred_element_type=jnp.float32) * scale
        score = jnp.where(kept, score, -1e30)
        new_top = jnp.maximum(top_h, jnp.max(score, axis=1))
        weight = jnp.where(kept, jnp.exp(score - new_top[:, None]), 0.0)
        factor = jnp.exp(top_h - new_top)
        new_total = total_h * factor + jnp.sum(weight, axis=1)
        new_acc = acc_h * factor[:, None] + jnp.dot(
            weight.astype(jnp.bfloat16), value_h, preferred_element_type=jnp.float32
        )
        return (new_top, new_total, new_acc)

    top_all, total_all, acc_all = lax.map(
        per_head, (queries, keys, values, top_now, total_now, acc_now)
    )
    context = (acc_all / total_all[:, :, None]).astype(jnp.bfloat16)
    gathered_ctx = jnp.moveaxis(context, 0, 1).reshape(tok_rows, width)
    mixed = (
        jnp.dot(gathered_ctx, out_weight, preferred_element_type=jnp.float32)
        + out_bias
        + tokens.astype(jnp.float32)
    )
    mean = jnp.mean(mixed, axis=1, keepdims=True)
    centered = mixed - mean
    variance = jnp.mean(centered * centered, axis=1, keepdims=True)
    normed = centered / jnp.sqrt(variance + 1e-05) * ln_gain + ln_bias
    return (normed.astype(jnp.bfloat16), kv_cache)


def solution(mesh):
    in_specs = (P(("rep", "seq"), None), P(("rep", "seq")), P(), P(), P(), P(), P())
    out_specs = (P(("rep", "seq"), None), P("rep", "seq"))
    return jax.shard_map(shards, mesh=mesh, in_specs=in_specs, out_specs=out_specs, check_vma=False)
```

profile of v0, /device:TPU:1, one launch (start us, length us, event | category | flops | bytes accessed | tf_op | source)
XLA Modules:
  0.0 246.1 jit_solution(5084389880568863316)
XLA Ops:
  7.2 6.0 %convolution_convert_fusion = bf16[256,3072]{1,0:T(8,128)(2,1)} fusion(bf16[256,1024]{1,0:T(8,128)(2,1)} %param.9, bf16[1024,3072]{1,0:T(8,128)(2,1)} %param.11), kind=kOutput, calls=%fused_computation.24 | convolution fusion | flops 1611399168 | bytes 8388608 | tf_op jit(solution)/shard_map/dot_general | solution.py:16
  13.3 2.6 %copy.20 = bf16[256,3072]{0,1:T(8,128)(2,1)} copy(bf16[256,3072]{1,0:T(8,128)(2,1)} %convolution_convert_fusion) | data formatting | bytes 3145728 | tf_op jit(solution)/shard_map/convert_element_type | solution.py:16
  15.9 2.3 slice.17
  18.2 10.0 %all-to-all-start = ((bf16[256,16,128]{0,2,1:T(8,128)(2,1)}), bf16[256,16,128]{0,2,1:T(8,128)(2,1)S(1)}, u32[]{:S(2)}, u32[]{:S(2)}) async-start(bf16[256,16,128]{0,2,1:T(8,128)(2,1)} %bitcast.60), calls=%async_computation | async-start | bytes 2097152 | tf_op jit(solution)/shard_map/all_to_all | solution.py:19
  28.2 46.9 %all-gather = s32[16,1,256]{2,1,0:T(1,128)S(1)} all-gather(s32[1,1,256]{2,1,0:T(1,128)S(1)} %bitcast.68), channel_id=1, replica_groups=mesh['seq'=16,'rep'=16] {'seq'}, dimensions={0}, use_global_device_ids=true | all-gather | bytes 17408 | tf_op jit(solution)/shard_map/all_gather | solution.py:15
  75.1 1.9 slice_bitcast_fusion.2
  77.0 1.3 copy.24
  78.3 64.8 %all-gather.3.cloned.1.call-done = bf16[4096,2048]{0,1:T(8,128)(2,1)} async-done(((bf16[256,2048]{0,1:T(8,128)(2,1)}), bf16[4096,2048]{0,1:T(8,128)(2,1)}) %all-gather.3.cloned.1.call-update) | async-done | bytes 16777232 | tf_op jit(solution)/shard_map/all_gather | solution.py:21
  143.1 11.8 %slice_bitcast_fusion = (bf16[16,4096,64]{1,2,0:T(8,128)(2,1)}, bf16[16,4096,64]{1,2,0:T(8,128)(2,1)}) fusion(bf16[4096,16,2,64]{0,3,2,1:T(8,128)(2,1)} %bitcast.58), kind=kLoop, calls=%fused_computation.22 | loop fusion | bytes 33554432 | tf_op jit(solution)/shard_map/transpose | solution.py:29
  154.9 81.0 %while.13 = (s32[]{:T(128)}, f32[16,256]{1,0:T(8,128)S(1)}, f32[16,256,64]{1,2,0:T(8,128)S(1)}, bf16[16,256,64]{1,2,0:T(8,128)(2,1)}, bf16[16,4096,64]{1,2,0:T(8...) while((s32[]{:T(128)}, f32[16,256]{1,0:T(8,128)S(1)}, ...), condition=%wide.region_3.4_spmd.clone, body=%wide.region_0.3_spmd.clone.sunk | while | flops 281035520 | bytes 13797481 | solution.py:44
  154.9 2.0 fusion.40
  156.9 1.0 fusion.41
  157.9 2.0 fusion.42
  160.0 2.0 fusion.40
  163.0 2.0 fusion.42
  165.1 2.0 fusion.40
  167.0 1.0 fusion.41
  168.0 2.0 fusion.42
  170.1 2.0 fusion.40
  172.1 1.0 fusion.41
  173.1 2.0 fusion.42
  175.2 2.0 fusion.40
  178.2 2.0 fusion.42
  180.2 2.0 fusion.40
  182.2 1.0 fusion.41
  183.2 2.0 fusion.42
  185.3 2.0 fusion.40
  188.3 2.0 fusion.42
  190.4 2.0 fusion.40
  193.3 2.0 fusion.42
  195.4 2.0 fusion.40
  198.4 2.0 fusion.42
  200.5 2.0 fusion.40
  203.5 2.0 fusion.42
  205.5 2.0 fusion.40
  208.5 2.0 fusion.42
  210.6 2.0 fusion.40
  213.6 2.0 fusion.42
  215.7 2.0 fusion.40
  218.7 2.0 fusion.42
  220.7 2.0 fusion.40
  223.7 2.0 fusion.42
  225.8 2.0 fusion.40
  228.8 2.0 fusion.42
  230.9 2.0 fusion.40
  233.8 2.0 fusion.42
  236.1 1.9 fusion.28
  238.2 1.0 add_convert_fusion
  (81 shorter events, 13.4 us)
Async XLA Ops:
  7.2 228.9 %copy-start = (bf16[1024,1024]{1,0:T(8,128)(2,1)S(1)}, bf16[1024,1024]{1,0:T(8,128)(2,1)}, u32[]{:S(2)}) copy-start(bf16[1024,1024]{1,0:T(8,128)(2,1)} %param.12) | copy-start | bytes 6291460
  7.2 136.0 %all-gather.3.cloned.1.call-start = ((), (), s32[]{:S(2)}) async-start(), calls=%async_computation.1 | async-start | bytes 17825792 | tf_op jit(solution)/shard_map/all_gather | solution.py:21
  13.3 14.9 %copy-start.2 = (s32[256]{0:T(256)S(1)}, s32[256]{0:T(256)}, u32[]{:S(2)}) copy-start(s32[256]{0:T(256)} %param.10) | copy-start | bytes 3076
  18.2 58.8 %all-to-all-start = ((bf16[256,16,128]{0,2,1:T(8,128)(2,1)}), bf16[256,16,128]{0,2,1:T(8,128)(2,1)S(1)}, u32[]{:S(2)}, u32[]{:S(2)}) async-start(bf16[256,16,128]{0,2,1:T(8,128)(2,1)} %bitcast.60), calls=%async_computation | async-start | bytes 2097152 | tf_op jit(solution)/shard_map/all_to_all | solution.py:19
  143.1 11.8 %copy-start.1 = (f32[16,256,64]{1,2,0:T(8,128)S(1)}, f32[16,256,64]{1,2,0:T(8,128)}, u32[]{:S(2)}) copy-start(f32[16,256,64]{1,2,0:T(8,128)} %custom-call.1) | copy-start | bytes 3145732
  154.9 81.1 %copy-start.3 = (f32[1024]{0:T(1024)S(1)}, f32[1024]{0:T(1024)}, u32[]{:S(2)}) copy-start(f32[1024]{0:T(1024)} %param.13) | copy-start | bytes 12292
  235.9 2.3 copy-start.4
  235.9 2.3 copy-start.5
Sparse Core Ops, SparseCore 0:
  18.3 124.7 all-gather.2
where the time goes:
time: 248 us; the launch traced here: 246 us
  matrix products  71.4 us (29%)
  waiting for transfers between devices  64.8 us (26%)
  blocking collectives  46.9 us (19%)
  local copies, waits for them, and re-layouts  20.6 us (8%)
  other arithmetic  17.7 us (7%)
  between operations  14.1 us (6%)
  starting transfers between devices  10 us (4%)
    all_gather x1, waiting for transfers between devices, shards(): piece = lax.all_gather(key_value, 'seq', axis=0, tiled=True)  64.8 us
    all_gather x1, blocking collectives, shards(): all_seg = lax.all_gather(segments, 'seq', axis=0, tiled=True)  46.9 us
    dot_general x16, matrix products, per_head(): jnp.dot(weight.astype(jnp.bfloat16), value_h, preferred_element_type=jnp....  32.1 us
    dot_general x16, matrix products, per_head(): score = jnp.dot(query, key_h.T, preferred_element_type=jnp.float32) * scale  31.4 us
    reduce_sum x16, other arithmetic, per_head(): new_total = total_h * factor + jnp.sum(weight, axis=1)  16 us
    transpose x1, local copies, waits for them, and re-layouts, shards(): values = jnp.moveaxis(split_piece[:, :, 1, :], 1, 0)  11.8 us
    all_to_all x1, starting transfers between devices, shards(): lax.all_to_all(key_value, 'seq', split_axis=1, concat_axis=0, tiled=True)  9.98 us
    dot_general x1, matrix products, shards(): jnp.dot(tokens, qkv_weight, preferred_element_type=jnp.float32)  6.04 us
  transfers between devices with their start and end apart: 2, of which 1 were waited for; matrix products, arithmetic and copies ran while one was open for 1% of the time, Pallas kernels for 0%

commit v1 on v0

v1 whole, which is shorter than its diff:
```python
import math

import jax
import jax.numpy as jnp
from jax import lax
from jax.sharding import PartitionSpec as P

HEADS = 16
HEAD = 64
Q_CHUNK = 512


def shards(tokens, segments, qkv_weight, out_weight, out_bias, ln_gain, ln_bias):
    tok_rows, width = tokens.shape
    scale = 1.0 / math.sqrt(HEAD)
    all_seg = lax.all_gather(segments, "seq", axis=0, tiled=True)
    proj = jnp.dot(tokens, qkv_weight, preferred_element_type=jnp.float32).astype(jnp.bfloat16)
    grouped = proj.reshape(tok_rows, HEADS, 3 * HEAD)
    mine = lax.all_to_all(grouped, "seq", split_axis=1, concat_axis=0, tiled=True)
    count_rows = mine.shape[0]
    mine = mine.reshape(count_rows, 3 * HEAD)
    kv_cache = mine[:, HEAD:]
    query = mine[:, :HEAD]
    key_h = mine[:, HEAD:2 * HEAD]
    value_h = mine[:, 2 * HEAD:]
    chunks = count_rows // Q_CHUNK

    def per_chunk(items):
        q_c, seg_c = items
        kept = seg_c[:, None] == all_seg[None, :]
        score = jnp.dot(q_c, key_h.T, preferred_element_type=jnp.float32) * scale
        score = jnp.where(kept, score, -1e30)
        top = jnp.max(score, axis=1, keepdims=True)
        weight = jnp.where(kept, jnp.exp(score - top), 0.0)
        total = jnp.sum(weight, axis=1, keepdims=True)
        acc = jnp.dot(weight.astype(jnp.bfloat16), value_h, preferred_element_type=jnp.float32)
        return (acc / total).astype(jnp.bfloat16)

    context = lax.map(
        per_chunk,
        (query.reshape(chunks, Q_CHUNK, HEAD), all_seg.reshape(chunks, Q_CHUNK)),
    ).reshape(count_rows, 1, HEAD)
    gathered_ctx = lax.all_to_all(context, "seq", split_axis=0, concat_axis=1, tiled=True)
    gathered_ctx = gathered_ctx.reshape(tok_rows, width)
    mixed = (
        jnp.dot(gathered_ctx, out_weight, preferred_element_type=jnp.float32)
        + out_bias
        + tokens.astype(jnp.float32)
    )
    mean = jnp.mean(mixed, axis=1, keepdims=True)
    centered = mixed - mean
    variance = jnp.mean(centered * centered, axis=1, keepdims=True)
    normed = centered / jnp.sqrt(variance + 1e-05) * ln_gain + ln_bias
    return (normed.astype(jnp.bfloat16), kv_cache)


def solution(mesh):
    in_specs = (P(("rep", "seq"), None), P(("rep", "seq")), P(), P(), P(), P(), P())
    out_specs = (P(("rep", "seq"), None), P("rep", "seq"))
    return jax.shard_map(shards, mesh=mesh, in_specs=in_specs, out_specs=out_specs, check_vma=False)
```

time: 248 us -> 215 us (0.87)
  waiting for transfers between devices: 64.8 us -> 14.7 us
  other arithmetic: 17.7 us -> 45.8 us
  matrix products: 71.4 us -> 57.2 us
  between operations: 14.1 us -> 0.8 us
  local copies, waits for them, and re-layouts: 20.6 us -> 31.1 us
  starting transfers between devices: 10 us -> 15.9 us
    all_gather x1 -> x0, waiting for transfers between devices: 64.8 us -> none  [shards(): piece = lax.all_gather(key_value, 'seq', axis=0, tiled=True)]
    reshape x0 -> x1, other arithmetic: none -> 23.5 us  [shards(): context = lax.map(per_chunk, (query.reshape(chunks, Q_CHUNK, HEAD), all_s...]
    all_to_all x1 -> x2, waiting for transfers between devices: 0.01 us -> 14.7 us  [the longest x1 14.7 us: shards(): lax.all_to_all(context, 'seq', split_axis=0, concat_axis=1, tiled=True)]
    dot_general x32 -> x16, matrix products: 63.5 us -> 49.3 us  [the longest x8 26.4 us: per_chunk(): jnp.dot(weight.astype(jnp.bfloat16), value_h, preferred_element_type=jnp....]
    transpose x2 -> x0, local copies, waits for them, and re-layouts: 13.7 us -> none  [the longest x1 11.8 us: shards(): values = jnp.moveaxis(split_piece[:, :, 1, :], 1, 0)]
    unnamed x12 -> x17, local copies, waits for them, and re-layouts: 0.03 us -> 11.2 us
    all_to_all x1 -> x2, starting transfers between devices: 9.98 us -> 15.9 us  [the longest x1 9.97 us: shards(): lax.all_to_all(grouped, 'seq', split_axis=1, concat_axis=0, tiled=True)]
    reshape x0 -> x4, local copies, waits for them, and re-layouts: none -> 5.19 us  [the longest x3 5.18 us: shards(): context = lax.map(per_chunk, (query.reshape(chunks, Q_CHUNK, HEAD), all_s...]
where the time goes in v1:
time: 215 us; the launch traced here: 214 us
  matrix products  57.2 us (27%)
  blocking collectives  48.2 us (22%)
  other arithmetic  45.8 us (21%)
  local copies, waits for them, and re-layouts  31.1 us (14%)
  starting transfers between devices  15.9 us (7%)
  waiting for transfers between devices  14.7 us (7%)
    all_gather x1, blocking collectives, shards(): all_seg = lax.all_gather(segments, 'seq', axis=0, tiled=True)  48.2 us
    dot_general x8, matrix products, per_chunk(): jnp.dot(weight.astype(jnp.bfloat16), value_h, preferred_element_type=jnp....  26.4 us
    reshape x1, other arithmetic, shards(): context = lax.map(per_chunk, (query.reshape(chunks, Q_CHUNK, HEAD), all_s...  23.5 us
    dot_general x8, matrix products, per_chunk(): score = jnp.dot(q_c, key_h.T, preferred_element_type=jnp.float32) * scale  22.9 us
    reduce_sum x8, other arithmetic, per_chunk(): total = jnp.sum(weight, axis=1, keepdims=True)  21 us
    all_to_all x1, waiting for transfers between devices, shards(): lax.all_to_all(context, 'seq', split_axis=0, concat_axis=1, tiled=True)  14.7 us
    unnamed x17, local copies, waits for them, and re-layouts  11.2 us
    all_to_all x1, starting transfers between devices, shards(): lax.all_to_all(grouped, 'seq', split_axis=1, concat_axis=0, tiled=True)  9.97 us
  transfers between devices with their start and end apart: 2, of which 1 were waited for; matrix products, arithmetic and copies ran while one was open for 1% of the time, Pallas kernels for 0%

profile of v1, /device:TPU:1, one launch (start us, length us, event | category | flops | bytes accessed | tf_op | source)
XLA Modules:
  0.0 213.7 jit_solution(3142455166517597984)
XLA Ops:
  0.7 6.0 %convolution_convert_fusion = bf16[256,3072]{1,0:T(8,128)(2,1)} fusion(bf16[256,1024]{1,0:T(8,128)(2,1)} %param.9, bf16[1024,3072]{1,0:T(8,128)(2,1)} %param.11), kind=kOutput, calls=%fused_computation.18 | convolution fusion | flops 1611399168 | bytes 8388608 | tf_op jit(solution)/shard_map/dot_general | solution.py:17
  6.7 2.6 %copy.21 = bf16[256,3072]{0,1:T(8,128)(2,1)} copy(bf16[256,3072]{1,0:T(8,128)(2,1)} %convolution_convert_fusion) | data formatting | bytes 3145728 | tf_op jit(solution)/shard_map/convert_element_type | solution.py:17
  9.3 10.0 %all-to-all-start = ((bf16[256,16,192]{0,2,1:T(8,128)(2,1)}), bf16[256,16,192]{0,2,1:T(8,128)(2,1)}, u32[]{:S(2)}, u32[]{:S(2)}) async-start(bf16[256,16,192]{0,2,1:T(8,128)(2,1)} %bitcast.51), calls=%async_computation | async-start | bytes 3145728 | tf_op jit(solution)/shard_map/all_to_all | solution.py:19
  19.3 48.2 %all-gather = s32[16,1,256]{2,1,0:T(1,128)S(1)} all-gather(s32[1,1,256]{2,1,0:T(1,128)S(1)} %bitcast.60), channel_id=1, replica_groups=mesh['seq'=16,'rep'=16] {'seq'}, dimensions={0}, use_global_device_ids=true | all-gather | bytes 17408 | tf_op jit(solution)/shard_map/all_gather | solution.py:16
  67.5 1.6 copy.34
  69.1 1.1 copy-done.1
  70.2 0.9 fusion.25
  71.2 2.4 %copy.25 = bf16[4096,64]{1,0:T(8,128)(2,1)} copy(bf16[4096,64]{0,1:T(8,128)(2,1)} %get-tuple-element.74) | data formatting | bytes 1048576 | tf_op jit(solution)/shard_map/while | solution.py:39
  73.6 1.3 copy.24
  74.9 1.3 copy.31
  76.2 70.4 %while.10 = (s32[]{:T(128)}, bf16[8,512,64]{1,2,0:T(8,128)(2,1)}, s32[8,512]{1,0:T(8,128)S(1)}, s32[4096]{0:T(1024)S(1)}, bf16[8,512,64]{2,1,0:T(8,128)(2,1)}, /...) while((s32[]{:T(128)}, bf16[8,512,64]{1,2,0:T(8,128)(2,1)}, s32[8,512]{1,0:T(8,128)S(1)}, ...), condition=%wide.region_3.4_spmd, body=%wide.region_0.3_spmd.sunk | while | flops 570489856 | bytes 29102212 | solution.py:39
  76.3 2.9 %fusion.42 = (f32[512]{0:T(512)S(1)}, f32[512,4096]{1,0:T(8,128)S(1)}) fusion(s32[4096]{0:T(1024)S(1)} %get-tuple-element.145, s32[512]{0:T(512)S(1)} %bitcast.57, bf16[4096,64]{1,0:T(8,128)(2,1)} %get-tuple-element.147, bf16[8,512,64]{2,1,0:T(8,128)(2,1)} %get-tuple-element.146, s32[]{:T(128)S(6)} %copy.40), kind=kOutput, calls=%fused_computation.2.clone.1 | convolution fusion | flops 276823552 | bytes 9588740 | tf_op jit(solution)/shard_map/while/body/eval_jaxpr/dot_general | solution.py:31
  79.1 2.6 %fusion.43 = f32[512]{0:T(512)S(1)} fusion(f32[512,4096]{1,0:T(8,128)S(1)} %get-tuple-element.124, f32[512]{0:T(512)S(1)} %get-tuple-element.125, s32[4096]{0:T(1024)S(1)} %get-tuple-element.145, s32[512]{0:T(512)S(1)} %bitcast.58), kind=kLoop, calls=%fused_computation.3.clone.1 | loop fusion | flops 12582400 | bytes 8411136 | tf_op jit(solution)/shard_map/while/body/eval_jaxpr/reduce_sum | solution.py:35
  81.8 3.3 %fusion.44 = bf16[8,512,64]{1,2,0:T(8,128)(2,1)} fusion(bf16[8,512,64]{1,2,0:T(8,128)(2,1)} %get-tuple-element.135, s32[]{:T(128)S(6)} %copy.40, bf16[4096,64]{1,0:T(8,128)(2,1)S(1)} %copy-done.2, f32[512,4096]{1,0:T(8,128)S(1)} %get-tuple-element.124, f32[512]{0:T(512)S(1)} %get-tuple-element.125, s32[4096]{0:T(1024)S(1)} %get-tuple-element.145, ...), kind=kOutput, calls=%fused_computation.9.clone.1 | convolution fusion | flops 281083904 | bytes 9000964 | tf_op jit(solution)/shard_map/while/body/eval_jaxpr/dot_general | solution.py:36
  85.1 2.9 %fusion.42 = (f32[512]{0:T(512)S(1)}, f32[512,4096]{1,0:T(8,128)S(1)}) fusion(s32[4096]{0:T(1024)S(1)} %get-tuple-element.145, s32[512]{0:T(512)S(1)} %bitcast.57, bf16[4096,64]{1,0:T(8,128)(2,1)} %get-tuple-element.147, bf16[8,512,64]{2,1,0:T(8,128)(2,1)} %get-tuple-element.146, s32[]{:T(128)S(6)} %copy.40), kind=kOutput, calls=%fused_computation.2.clone.1 | convolution fusion | flops 276823552 | bytes 9588740 | tf_op jit(solution)/shard_map/while/body/eval_jaxpr/dot_general | solution.py:31
  87.9 2.6 %fusion.43 = f32[512]{0:T(512)S(1)} fusion(f32[512,4096]{1,0:T(8,128)S(1)} %get-tuple-element.124, f32[512]{0:T(512)S(1)} %get-tuple-element.125, s32[4096]{0:T(1024)S(1)} %get-tuple-element.145, s32[512]{0:T(512)S(1)} %bitcast.58), kind=kLoop, calls=%fused_computation.3.clone.1 | loop fusion | flops 12582400 | bytes 8411136 | tf_op jit(solution)/shard_map/while/body/eval_jaxpr/reduce_sum | solution.py:35
  90.6 3.3 %fusion.44 = bf16[8,512,64]{1,2,0:T(8,128)(2,1)} fusion(bf16[8,512,64]{1,2,0:T(8,128)(2,1)} %get-tuple-element.135, s32[]{:T(128)S(6)} %copy.40, bf16[4096,64]{1,0:T(8,128)(2,1)S(1)} %copy-done.2, f32[512,4096]{1,0:T(8,128)S(1)} %get-tuple-element.124, f32[512]{0:T(512)S(1)} %get-tuple-element.125, s32[4096]{0:T(1024)S(1)} %get-tuple-element.145, ...), kind=kOutput, calls=%fused_computation.9.clone.1 | convolution fusion | flops 281083904 | bytes 9000964 | tf_op jit(solution)/shard_map/while/body/eval_jaxpr/dot_general | solution.py:36
  93.9 2.9 %fusion.42 = (f32[512]{0:T(512)S(1)}, f32[512,4096]{1,0:T(8,128)S(1)}) fusion(s32[4096]{0:T(1024)S(1)} %get-tuple-element.145, s32[512]{0:T(512)S(1)} %bitcast.57, bf16[4096,64]{1,0:T(8,128)(2,1)} %get-tuple-element.147, bf16[8,512,64]{2,1,0:T(8,128)(2,1)} %get-tuple-element.146, s32[]{:T(128)S(6)} %copy.40), kind=kOutput, calls=%fused_computation.2.clone.1 | convolution fusion | flops 276823552 | bytes 9588740 | tf_op jit(solution)/shard_map/while/body/eval_jaxpr/dot_general | solution.py:31
  96.7 2.6 %fusion.43 = f32[512]{0:T(512)S(1)} fusion(f32[512,4096]{1,0:T(8,128)S(1)} %get-tuple-element.124, f32[512]{0:T(512)S(1)} %get-tuple-element.125, s32[4096]{0:T(1024)S(1)} %get-tuple-element.145, s32[512]{0:T(512)S(1)} %bitcast.58), kind=kLoop, calls=%fused_computation.3.clone.1 | loop fusion | flops 12582400 | bytes 8411136 | tf_op jit(solution)/shard_map/while/body/eval_jaxpr/reduce_sum | solution.py:35
  99.4 3.3 %fusion.44 = bf16[8,512,64]{1,2,0:T(8,128)(2,1)} fusion(bf16[8,512,64]{1,2,0:T(8,128)(2,1)} %get-tuple-element.135, s32[]{:T(128)S(6)} %copy.40, bf16[4096,64]{1,0:T(8,128)(2,1)S(1)} %copy-done.2, f32[512,4096]{1,0:T(8,128)S(1)} %get-tuple-element.124, f32[512]{0:T(512)S(1)} %get-tuple-element.125, s32[4096]{0:T(1024)S(1)} %get-tuple-element.145, ...), kind=kOutput, calls=%fused_computation.9.clone.1 | convolution fusion | flops 281083904 | bytes 9000964 | tf_op jit(solution)/shard_map/while/body/eval_jaxpr/dot_general | solution.py:36
  102.7 2.9 %fusion.42 = (f32[512]{0:T(512)S(1)}, f32[512,4096]{1,0:T(8,128)S(1)}) fusion(s32[4096]{0:T(1024)S(1)} %get-tuple-element.145, s32[512]{0:T(512)S(1)} %bitcast.57, bf16[4096,64]{1,0:T(8,128)(2,1)} %get-tuple-element.147, bf16[8,512,64]{2,1,0:T(8,128)(2,1)} %get-tuple-element.146, s32[]{:T(128)S(6)} %copy.40), kind=kOutput, calls=%fused_computation.2.clone.1 | convolution fusion | flops 276823552 | bytes 9588740 | tf_op jit(solution)/shard_map/while/body/eval_jaxpr/dot_general | solution.py:31
  105.5 2.6 %fusion.43 = f32[512]{0:T(512)S(1)} fusion(f32[512,4096]{1,0:T(8,128)S(1)} %get-tuple-element.124, f32[512]{0:T(512)S(1)} %get-tuple-element.125, s32[4096]{0:T(1024)S(1)} %get-tuple-element.145, s32[512]{0:T(512)S(1)} %bitcast.58), kind=kLoop, calls=%fused_computation.3.clone.1 | loop fusion | flops 12582400 | bytes 8411136 | tf_op jit(solution)/shard_map/while/body/eval_jaxpr/reduce_sum | solution.py:35
  108.2 3.3 %fusion.44 = bf16[8,512,64]{1,2,0:T(8,128)(2,1)} fusion(bf16[8,512,64]{1,2,0:T(8,128)(2,1)} %get-tuple-element.135, s32[]{:T(128)S(6)} %copy.40, bf16[4096,64]{1,0:T(8,128)(2,1)S(1)} %copy-done.2, f32[512,4096]{1,0:T(8,128)S(1)} %get-tuple-element.124, f32[512]{0:T(512)S(1)} %get-tuple-element.125, s32[4096]{0:T(1024)S(1)} %get-tuple-element.145, ...), kind=kOutput, calls=%fused_computation.9.clone.1 | convolution fusion | flops 281083904 | bytes 9000964 | tf_op jit(solution)/shard_map/while/body/eval_jaxpr/dot_general | solution.py:36
  111.5 2.9 %fusion.42 = (f32[512]{0:T(512)S(1)}, f32[512,4096]{1,0:T(8,128)S(1)}) fusion(s32[4096]{0:T(1024)S(1)} %get-tuple-element.145, s32[512]{0:T(512)S(1)} %bitcast.57, bf16[4096,64]{1,0:T(8,128)(2,1)} %get-tuple-element.147, bf16[8,512,64]{2,1,0:T(8,128)(2,1)} %get-tuple-element.146, s32[]{:T(128)S(6)} %copy.40), kind=kOutput, calls=%fused_computation.2.clone.1 | convolution fusion | flops 276823552 | bytes 9588740 | tf_op jit(solution)/shard_map/while/body/eval_jaxpr/dot_general | solution.py:31
  114.3 2.6 %fusion.43 = f32[512]{0:T(512)S(1)} fusion(f32[512,4096]{1,0:T(8,128)S(1)} %get-tuple-element.124, f32[512]{0:T(512)S(1)} %get-tuple-element.125, s32[4096]{0:T(1024)S(1)} %get-tuple-element.145, s32[512]{0:T(512)S(1)} %bitcast.58), kind=kLoop, calls=%fused_computation.3.clone.1 | loop fusion | flops 12582400 | bytes 8411136 | tf_op jit(solution)/shard_map/while/body/eval_jaxpr/reduce_sum | solution.py:35
  117.0 3.3 %fusion.44 = bf16[8,512,64]{1,2,0:T(8,128)(2,1)} fusion(bf16[8,512,64]{1,2,0:T(8,128)(2,1)} %get-tuple-element.135, s32[]{:T(128)S(6)} %copy.40, bf16[4096,64]{1,0:T(8,128)(2,1)S(1)} %copy-done.2, f32[512,4096]{1,0:T(8,128)S(1)} %get-tuple-element.124, f32[512]{0:T(512)S(1)} %get-tuple-element.125, s32[4096]{0:T(1024)S(1)} %get-tuple-element.145, ...), kind=kOutput, calls=%fused_computation.9.clone.1 | convolution fusion | flops 281083904 | bytes 9000964 | tf_op jit(solution)/shard_map/while/body/eval_jaxpr/dot_general | solution.py:36
  120.3 2.9 %fusion.42 = (f32[512]{0:T(512)S(1)}, f32[512,4096]{1,0:T(8,128)S(1)}) fusion(s32[4096]{0:T(1024)S(1)} %get-tuple-element.145, s32[512]{0:T(512)S(1)} %bitcast.57, bf16[4096,64]{1,0:T(8,128)(2,1)} %get-tuple-element.147, bf16[8,512,64]{2,1,0:T(8,128)(2,1)} %get-tuple-element.146, s32[]{:T(128)S(6)} %copy.40), kind=kOutput, calls=%fused_computation.2.clone.1 | convolution fusion | flops 276823552 | bytes 9588740 | tf_op jit(solution)/shard_map/while/body/eval_jaxpr/dot_general | solution.py:31
  123.1 2.6 %fusion.43 = f32[512]{0:T(512)S(1)} fusion(f32[512,4096]{1,0:T(8,128)S(1)} %get-tuple-element.124, f32[512]{0:T(512)S(1)} %get-tuple-element.125, s32[4096]{0:T(1024)S(1)} %get-tuple-element.145, s32[512]{0:T(512)S(1)} %bitcast.58), kind=kLoop, calls=%fused_computation.3.clone.1 | loop fusion | flops 12582400 | bytes 8411136 | tf_op jit(solution)/shard_map/while/body/eval_jaxpr/reduce_sum | solution.py:35
  125.8 3.3 %fusion.44 = bf16[8,512,64]{1,2,0:T(8,128)(2,1)} fusion(bf16[8,512,64]{1,2,0:T(8,128)(2,1)} %get-tuple-element.135, s32[]{:T(128)S(6)} %copy.40, bf16[4096,64]{1,0:T(8,128)(2,1)S(1)} %copy-done.2, f32[512,4096]{1,0:T(8,128)S(1)} %get-tuple-element.124, f32[512]{0:T(512)S(1)} %get-tuple-element.125, s32[4096]{0:T(1024)S(1)} %get-tuple-element.145, ...), kind=kOutput, calls=%fused_computation.9.clone.1 | convolution fusion | flops 281083904 | bytes 9000964 | tf_op jit(solution)/shard_map/while/body/eval_jaxpr/dot_general | solution.py:36
  129.1 2.9 %fusion.42 = (f32[512]{0:T(512)S(1)}, f32[512,4096]{1,0:T(8,128)S(1)}) fusion(s32[4096]{0:T(1024)S(1)} %get-tuple-element.145, s32[512]{0:T(512)S(1)} %bitcast.57, bf16[4096,64]{1,0:T(8,128)(2,1)} %get-tuple-element.147, bf16[8,512,64]{2,1,0:T(8,128)(2,1)} %get-tuple-element.146, s32[]{:T(128)S(6)} %copy.40), kind=kOutput, calls=%fused_computation.2.clone.1 | convolution fusion | flops 276823552 | bytes 9588740 | tf_op jit(solution)/shard_map/while/body/eval_jaxpr/dot_general | solution.py:31
  131.9 2.6 %fusion.43 = f32[512]{0:T(512)S(1)} fusion(f32[512,4096]{1,0:T(8,128)S(1)} %get-tuple-element.124, f32[512]{0:T(512)S(1)} %get-tuple-element.125, s32[4096]{0:T(1024)S(1)} %get-tuple-element.145, s32[512]{0:T(512)S(1)} %bitcast.58), kind=kLoop, calls=%fused_computation.3.clone.1 | loop fusion | flops 12582400 | bytes 8411136 | tf_op jit(solution)/shard_map/while/body/eval_jaxpr/reduce_sum | solution.py:35
  134.6 3.3 %fusion.44 = bf16[8,512,64]{1,2,0:T(8,128)(2,1)} fusion(bf16[8,512,64]{1,2,0:T(8,128)(2,1)} %get-tuple-element.135, s32[]{:T(128)S(6)} %copy.40, bf16[4096,64]{1,0:T(8,128)(2,1)S(1)} %copy-done.2, f32[512,4096]{1,0:T(8,128)S(1)} %get-tuple-element.124, f32[512]{0:T(512)S(1)} %get-tuple-element.125, s32[4096]{0:T(1024)S(1)} %get-tuple-element.145, ...), kind=kOutput, calls=%fused_computation.9.clone.1 | convolution fusion | flops 281083904 | bytes 9000964 | tf_op jit(solution)/shard_map/while/body/eval_jaxpr/dot_general | solution.py:36
  137.9 2.9 %fusion.42 = (f32[512]{0:T(512)S(1)}, f32[512,4096]{1,0:T(8,128)S(1)}) fusion(s32[4096]{0:T(1024)S(1)} %get-tuple-element.145, s32[512]{0:T(512)S(1)} %bitcast.57, bf16[4096,64]{1,0:T(8,128)(2,1)} %get-tuple-element.147, bf16[8,512,64]{2,1,0:T(8,128)(2,1)} %get-tuple-element.146, s32[]{:T(128)S(6)} %copy.40), kind=kOutput, calls=%fused_computation.2.clone.1 | convolution fusion | flops 276823552 | bytes 9588740 | tf_op jit(solution)/shard_map/while/body/eval_jaxpr/dot_general | solution.py:31
  140.7 2.6 %fusion.43 = f32[512]{0:T(512)S(1)} fusion(f32[512,4096]{1,0:T(8,128)S(1)} %get-tuple-element.124, f32[512]{0:T(512)S(1)} %get-tuple-element.125, s32[4096]{0:T(1024)S(1)} %get-tuple-element.145, s32[512]{0:T(512)S(1)} %bitcast.58), kind=kLoop, calls=%fused_computation.3.clone.1 | loop fusion | flops 12582400 | bytes 8411136 | tf_op jit(solution)/shard_map/while/body/eval_jaxpr/reduce_sum | solution.py:35
  143.4 3.3 %fusion.44 = bf16[8,512,64]{1,2,0:T(8,128)(2,1)} fusion(bf16[8,512,64]{1,2,0:T(8,128)(2,1)} %get-tuple-element.135, s32[]{:T(128)S(6)} %copy.40, bf16[4096,64]{1,0:T(8,128)(2,1)S(1)} %copy-done.2, f32[512,4096]{1,0:T(8,128)S(1)} %get-tuple-element.124, f32[512]{0:T(512)S(1)} %get-tuple-element.125, s32[4096]{0:T(1024)S(1)} %get-tuple-element.145, ...), kind=kOutput, calls=%fused_computation.9.clone.1 | convolution fusion | flops 281083904 | bytes 9000964 | tf_op jit(solution)/shard_map/while/body/eval_jaxpr/dot_general | solution.py:36
  146.7 1.5 copy.32
  148.2 3.2 %reshape.53 = bf16[4096,1,64]{2,1,0:T(2,128)(2,1)} reshape(bf16[8,512,64]{2,1,0:T(8,128)(2,1)S(1)} %copy.32) | data formatting | bytes 1048576 | tf_op jit(solution)/shard_map/reshape | solution.py:42
  151.3 0.5 broadcast.45
  151.9 23.5 %reduce.1 = bf16[4096,64]{1,0:T(8,128)(2,1)S(1)} reduce(bf16[4096,1,64]{2,1,0:T(2,128)(2,1)} %reshape.53, bf16[]{:T(256)} %broadcast.45), dimensions={1}, to_apply=%reshape.53.reduce_sub_computation | reduce | bytes 1048578 | tf_op jit(solution)/shard_map/reshape | solution.py:42
  175.3 1.5 reshape.55
  176.8 5.9 %all-to-all-start.1 = ((bf16[16,2,8192]{2,1,0:T(2,128)(2,1)}), bf16[16,2,8192]{2,1,0:T(2,128)(2,1)}, u32[]{:S(2)}, u32[]{:S(2)}) async-start(bf16[16,2,8192]{2,1,0:T(2,128)(2,1)} %reshape.55), calls=%async_computation.1 | async-start | bytes 1048576 | tf_op jit(solution)/shard_map/all_to_all | solution.py:43
  182.8 1.3 slice.19
  184.1 1.3 copy.30
  185.4 14.7 %all-to-all-done.1 = bf16[16,2,8192]{2,1,0:T(2,128)(2,1)} async-done(((bf16[16,2,8192]{2,1,0:T(2,128)(2,1)}), bf16[16,2,8192]{2,1,0:T(2,128)(2,1)}, u32[]{:S(2)}, u32[]{:S(2)}) %all-to-all-start.1) | async-done | bytes 524320 | tf_op jit(solution)/shard_map/all_to_all | solution.py:43
  200.1 5.5 %reshape.56 = bf16[4096,1,64]{2,1,0:T(2,128)(2,1)} reshape(bf16[16,2,8192]{2,1,0:T(2,128)(2,1)} %all-to-all-done.1) | data formatting | bytes 1048576
  205.6 4.6 %copy.28 = bf16[4096,1,64]{0,2,1:T(8,128)(2,1)S(1)} copy(bf16[4096,1,64]{2,1,0:T(2,128)(2,1)} %reshape.56) | data formatting | bytes 1048576 | tf_op jit(solution)/shard_map/all_to_all | solution.py:43
  210.5 1.9 fusion.26
  212.7 1.0 add_convert_fusion
  (44 shorter events, 0.7 us)
Async XLA Ops:
  0.6 209.9 %copy-start = (bf16[1024,1024]{1,0:T(8,128)(2,1)S(1)}, bf16[1024,1024]{1,0:T(8,128)(2,1)}, u32[]{:S(2)}) copy-start(bf16[1024,1024]{1,0:T(8,128)(2,1)} %param.12) | copy-start | bytes 6291460
  0.6 18.6 %copy-start.6 = (s32[256]{0:T(256)S(1)}, s32[256]{0:T(256)}, u32[]{:S(2)}) copy-start(s32[256]{0:T(256)} %param.10) | copy-start | bytes 3076
  9.3 58.2 %all-to-all-start = ((bf16[256,16,192]{0,2,1:T(8,128)(2,1)}), bf16[256,16,192]{0,2,1:T(8,128)(2,1)}, u32[]{:S(2)}, u32[]{:S(2)}) async-start(bf16[256,16,192]{0,2,1:T(8,128)(2,1)} %bitcast.51), calls=%async_computation | async-start | bytes 3145728 | tf_op jit(solution)/shard_map/all_to_all | solution.py:19
  69.1 1.2 copy-start.1
  76.2 5.5 %copy-start.2 = (bf16[4096,64]{1,0:T(8,128)(2,1)S(1)}, bf16[4096,64]{1,0:T(8,128)(2,1)}, u32[]{:S(2)}) copy-start(bf16[4096,64]{1,0:T(8,128)(2,1)} %get-tuple-element.148) | copy-start | bytes 1572868 | tf_op jit(solution)/shard_map/while
  85.1 5.5 %copy-start.2 = (bf16[4096,64]{1,0:T(8,128)(2,1)S(1)}, bf16[4096,64]{1,0:T(8,128)(2,1)}, u32[]{:S(2)}) copy-start(bf16[4096,64]{1,0:T(8,128)(2,1)} %get-tuple-element.148) | copy-start | bytes 1572868 | tf_op jit(solution)/shard_map/while
  93.9 5.5 %copy-start.2 = (bf16[4096,64]{1,0:T(8,128)(2,1)S(1)}, bf16[4096,64]{1,0:T(8,128)(2,1)}, u32[]{:S(2)}) copy-start(bf16[4096,64]{1,0:T(8,128)(2,1)} %get-tuple-element.148) | copy-start | bytes 1572868 | tf_op jit(solution)/shard_map/while
  102.7 5.5 %copy-start.2 = (bf16[4096,64]{1,0:T(8,128)(2,1)S(1)}, bf16[4096,64]{1,0:T(8,128)(2,1)}, u32[]{:S(2)}) copy-start(bf16[4096,64]{1,0:T(8,128)(2,1)} %get-tuple-element.148) | copy-start | bytes 1572868 | tf_op jit(solution)/shard_map/while
  111.5 5.5 %copy-start.2 = (bf16[4096,64]{1,0:T(8,128)(2,1)S(1)}, bf16[4096,64]{1,0:T(8,128)(2,1)}, u32[]{:S(2)}) copy-start(bf16[4096,64]{1,0:T(8,128)(2,1)} %get-tuple-element.148) | copy-start | bytes 1572868 | tf_op jit(solution)/shard_map/while
  120.3 5.5 %copy-start.2 = (bf16[4096,64]{1,0:T(8,128)(2,1)S(1)}, bf16[4096,64]{1,0:T(8,128)(2,1)}, u32[]{:S(2)}) copy-start(bf16[4096,64]{1,0:T(8,128)(2,1)} %get-tuple-element.148) | copy-start | bytes 1572868 | tf_op jit(solution)/shard_map/while
  129.1 5.5 %copy-start.2 = (bf16[4096,64]{1,0:T(8,128)(2,1)S(1)}, bf16[4096,64]{1,0:T(8,128)(2,1)}, u32[]{:S(2)}) copy-start(bf16[4096,64]{1,0:T(8,128)(2,1)} %get-tuple-element.148) | copy-start | bytes 1572868 | tf_op jit(solution)/shard_map/while
  137.9 5.5 %copy-start.2 = (bf16[4096,64]{1,0:T(8,128)(2,1)S(1)}, bf16[4096,64]{1,0:T(8,128)(2,1)}, u32[]{:S(2)}) copy-start(bf16[4096,64]{1,0:T(8,128)(2,1)} %get-tuple-element.148) | copy-start | bytes 1572868 | tf_op jit(solution)/shard_map/while
  151.9 58.6 %copy-start.3 = (f32[1024]{0:T(1024)S(1)}, f32[1024]{0:T(1024)}, u32[]{:S(2)}) copy-start(f32[1024]{0:T(1024)} %param.13) | copy-start | bytes 12292
  176.8 23.2 %all-to-all-start.1 = ((bf16[16,2,8192]{2,1,0:T(2,128)(2,1)}), bf16[16,2,8192]{2,1,0:T(2,128)(2,1)}, u32[]{:S(2)}, u32[]{:S(2)}) async-start(bf16[16,2,8192]{2,1,0:T(2,128)(2,1)} %reshape.55), calls=%async_computation.1 | async-start | bytes 1048576 | tf_op jit(solution)/shard_map/all_to_all | solution.py:43
  182.8 29.9 %copy-start.4 = (f32[1024]{0:T(1024)S(1)}, f32[1024]{0:T(1024)}, u32[]{:S(2)}) copy-start(f32[1024]{0:T(1024)} %param.15) | copy-start | bytes 12292
  182.8 29.9 %copy-start.5 = (f32[1024]{0:T(1024)S(1)}, f32[1024]{0:T(1024)}, u32[]{:S(2)}) copy-start(f32[1024]{0:T(1024)} %param.14) | copy-start | bytes 12292

commit v2 on v1

--- a/solution.py
+++ b/solution.py
@@ -3,11 +3,79 @@
 import jax
 import jax.numpy as jnp
 from jax import lax
+from jax.experimental import pallas as pl
+from jax.experimental.pallas import tpu as pltpu
 from jax.sharding import PartitionSpec as P
 
 HEADS = 16
 HEAD = 64
-Q_CHUNK = 512
+BQ = 512
+BK = 512
+INTERPRET = False
+
+
+def attn_kernel(lo_ref, hi_ref, q_ref, k_ref, v_ref, sq_ref, sk_ref, o_ref):
+    i = pl.program_id(0)
+    q = q_ref[...]
+    sq = sq_ref[...]
+
+    def body(j, carry):
+        m, l, acc = carry
+        k = k_ref[j]
+        v = v_ref[j]
+        sk = sk_ref[j]
+        s = lax.dot_general(q, k, (((1,), (1,)), ((), ())), preferred_element_type=jnp.float32)
+        s = jnp.where(sq == sk, s, -jnp.inf)
+        m_new = jnp.maximum(m, jnp.max(s, axis=1, keepdims=True))
+        m_safe = jnp.where(m_new == -jnp.inf, 0.0, m_new)
+        p = jnp.exp(s - m_safe)
+        alpha = jnp.exp(m - m_safe)
+        l = alpha * l + jnp.sum(p, axis=1, keepdims=True)
+        acc = alpha * acc + jnp.dot(p.astype(jnp.bfloat16), v, preferred_element_type=jnp.float32)
+        return m_new, l, acc
+
+    m0 = jnp.full((BQ, 1), -jnp.inf, jnp.float32)
+    l0 = jnp.zeros((BQ, 1), jnp.float32)
+    acc0 = jnp.zeros((BQ, HEAD), jnp.float32)
+    _, l, acc = lax.fori_loop(lo_ref[i], hi_ref[i], body, (m0, l0, acc0))
+    o_ref[...] = (acc / l).astype(o_ref.dtype)
+
+
+def attention(query, key_h, value_h, seg):
+    rows = query.shape[0]
+    nq, nk = rows // BQ, rows // BK
+    first = seg[::BQ]
+    last = seg[BQ - 1::BQ]
+    start = jnp.sum((seg[None, :] < first[:, None]).astype(jnp.int32), axis=1)
+    end = jnp.sum((seg[None, :] <= last[:, None]).astype(jnp.int32), axis=1)
+    lo = start // BK
+    hi = (end + BK - 1) // BK
+    grid_spec = pltpu.PrefetchScalarGridSpec(
+        num_scalar_prefetch=2,
+        grid=(nq,),
+        in_specs=[
+            pl.BlockSpec((BQ, HEAD), lambda i, lo, hi: (i, 0)),
+            pl.BlockSpec((nk, BK, HEAD), lambda i, lo, hi: (0, 0, 0)),
+            pl.BlockSpec((nk, BK, HEAD), lambda i, lo, hi: (0, 0, 0)),
+            pl.BlockSpec((BQ, 1), lambda i, lo, hi: (i, 0)),
+            pl.BlockSpec((nk, 1, BK), lambda i, lo, hi: (0, 0, 0)),
+        ],
+        out_specs=pl.BlockSpec((BQ, HEAD), lambda i, lo, hi: (i, 0)),
+    )
+    return pl.pallas_call(
+        attn_kernel,
+        grid_spec=grid_spec,
+        out_shape=jax.ShapeDtypeStruct((rows, HEAD), jnp.bfloat16),
+        interpret=INTERPRET,
+    )(
+        lo,
+        hi,
+        query,
+        key_h.reshape(nk, BK, HEAD),
+        value_h.reshape(nk, BK, HEAD),
+        seg.reshape(rows, 1),
+        seg.reshape(nk, 1, BK),
+    )
 
 
 def shards(tokens, segments, qkv_weight, out_weight, out_bias, ln_gain, ln_bias):
@@ -20,26 +88,10 @@
     count_rows = mine.shape[0]
     mine = mine.reshape(count_rows, 3 * HEAD)
     kv_cache = mine[:, HEAD:]
-    query = mine[:, :HEAD]
+    query = mine[:, :HEAD] * jnp.asarray(scale, jnp.bfloat16)
     key_h = mine[:, HEAD:2 * HEAD]
     value_h = mine[:, 2 * HEAD:]
-    chunks = count_rows // Q_CHUNK
-
-    def per_chunk(items):
-        q_c, seg_c = items
-        kept = seg_c[:, None] == all_seg[None, :]
-        score = jnp.dot(q_c, key_h.T, preferred_element_type=jnp.float32) * scale
-        score = jnp.where(kept, score, -1e30)
-        top = jnp.max(score, axis=1, keepdims=True)
-        weight = jnp.where(kept, jnp.exp(score - top), 0.0)
-        total = jnp.sum(weight, axis=1, keepdims=True)
-        acc = jnp.dot(weight.astype(jnp.bfloat16), value_h, preferred_element_type=jnp.float32)
-        return (acc / total).astype(jnp.bfloat16)
-
-    context = lax.map(
-        per_chunk,
-        (query.reshape(chunks, Q_CHUNK, HEAD), all_seg.reshape(chunks, Q_CHUNK)),
-    ).reshape(count_rows, 1, HEAD)
+    context = attention(query, key_h, value_h, all_seg).reshape(count_rows, 1, HEAD)
     gathered_ctx = lax.all_to_all(context, "seq", split_axis=0, concat_axis=1, tiled=True)
     gathered_ctx = gathered_ctx.reshape(tok_rows, width)
     mixed = (

time: 215 us -> 155 us (0.72)
  matrix products: 57.2 us -> 6.86 us
  other arithmetic: 45.8 us -> 8.88 us
  Pallas kernels: 0 us -> 34.7 us
  local copies, waits for them, and re-layouts: 31.1 us -> 21.9 us
    dot_general x16 -> x0, matrix products: 49.3 us -> none  [the longest x8 26.4 us: per_chunk(): jnp.dot(weight.astype(jnp.bfloat16), value_h, preferred_element_type=jnp....]
    pallas_call x0 -> x1, Pallas kernels: none -> 34.7 us  [attention(): pl.pallas_call(attn_kernel, grid_spec=grid_spec, out_shape=jax.ShapeDtype...]
    reduce_sum x8 -> x1, other arithmetic: 21 us -> 0.24 us  [attention(): end = jnp.sum((seg[None, :] <= last[:, None]).astype(jnp.int32), axis=1)]
    reshape x1, other arithmetic: 23.5 us -> 2.85 us  [shards(): attention(query, key_h, value_h, all_seg).reshape(count_rows, 1, HEAD)]
    unnamed x17, local copies, waits for them, and re-layouts: 11.2 us -> 5.23 us
    while x19 -> x0, local copies, waits for them, and re-layouts: 5.1 us -> none  [the longest x3 5.07 us: shards(): lax.map(per_chunk, (query.reshape(chunks, Q_CHUNK, HEAD), all_seg.reshape...]
    slice x0 -> x1, other arithmetic: none -> 3.93 us  [shards(): value_h = mine[:, 2 * HEAD:]]
    all_to_all x0 -> x1, local copies, waits for them, and re-layouts: none -> 3.71 us  [shards(): lax.all_to_all(grouped, 'seq', split_axis=1, concat_axis=0, tiled=True)]
  transfers between devices with their start and end apart: 2 -> 2, of which waited for: 1 -> 1; matrix products, arithmetic and copies ran while one was open for 1% -> 4% of each run, Pallas kernels for 0% -> 0%
where the time goes in v2:
time: 155 us; the launch traced here: 152 us
  blocking collectives  48.2 us (31%)
  Pallas kernels  34.7 us (22%)
  local copies, waits for them, and re-layouts  21.9 us (14%)
  starting transfers between devices  16 us (10%)
  waiting for transfers between devices  14.3 us (9%)
  other arithmetic  8.88 us (6%)
  matrix products  6.86 us (4%)
    all_gather x1, blocking collectives, shards(): all_seg = lax.all_gather(segments, 'seq', axis=0, tiled=True)  48.2 us
    pallas_call x1, Pallas kernels, attention(): pl.pallas_call(attn_kernel, grid_spec=grid_spec, out_shape=jax.ShapeDtype...  34.7 us
    all_to_all x1, waiting for transfers between devices, shards(): lax.all_to_all(context, 'seq', split_axis=0, concat_axis=1, tiled=True)  14.3 us
    all_to_all x1, starting transfers between devices, shards(): lax.all_to_all(grouped, 'seq', split_axis=1, concat_axis=0, tiled=True)  10.1 us
    dot_general x1, matrix products, shards(): jnp.dot(tokens, qkv_weight, preferred_element_type=jnp.float32)  6.04 us
    all_to_all x1, starting transfers between devices, shards(): lax.all_to_all(context, 'seq', split_axis=0, concat_axis=1, tiled=True)  5.92 us
    unnamed x17, local copies, waits for them, and re-layouts  5.23 us
    all_to_all x2, local copies, waits for them, and re-layouts, shards(): lax.all_to_all(context, 'seq', split_axis=0, concat_axis=1, tiled=True)  4.8 us
  transfers between devices with their start and end apart: 2, of which 1 were waited for; matrix products, arithmetic and copies ran while one was open for 4% of the time, Pallas kernels for 0%

profile of v2, /device:TPU:1, one launch (start us, length us, event | category | flops | bytes accessed | tf_op | source)
XLA Modules:
  0.0 151.6 jit_solution(2155656422399580249)
XLA Ops:
  0.6 0.0 copy-start
  0.6 6.0 %convolution_convert_fusion = bf16[256,3072]{1,0:T(8,128)(2,1)} fusion(bf16[256,1024]{1,0:T(8,128)(2,1)} %param.7, bf16[1024,3072]{1,0:T(8,128)(2,1)} %param.9), kind=kOutput, calls=%fused_computation | convolution fusion | flops 1611399168 | bytes 8388608 | tf_op jit(solution)/shard_map/dot_general | solution.py:85
  6.7 2.6 %copy.24 = bf16[256,3072]{0,1:T(8,128)(2,1)} copy(bf16[256,3072]{1,0:T(8,128)(2,1)} %convolution_convert_fusion) | data formatting | bytes 3145728 | tf_op jit(solution)/shard_map/convert_element_type | solution.py:85
  9.3 0.0 copy-start.6
  9.3 10.1 %all-to-all-start = ((bf16[256,16,192]{0,2,1:T(8,128)(2,1)}), bf16[256,16,192]{0,2,1:T(8,128)(2,1)}, u32[]{:S(2)}, u32[]{:S(2)}) async-start(bf16[256,16,192]{0,2,1:T(8,128)(2,1)} %bitcast.27), calls=%async_computation | async-start | bytes 3145728 | tf_op jit(solution)/shard_map/all_to_all | solution.py:87
  19.4 0.0 copy-done.6
  19.4 48.2 %all-gather = s32[16,1,256]{2,1,0:T(1,128)S(1)} all-gather(s32[1,1,256]{2,1,0:T(1,128)S(1)} %bitcast.39), channel_id=1, replica_groups=mesh['seq'=16,'rep'=16] {'seq'}, dimensions={0}, use_global_device_ids=true | all-gather | bytes 17408 | tf_op jit(solution)/shard_map/all_gather | solution.py:84
  67.6 0.0 copy-start.2
  67.6 0.1 slice.19
  67.6 0.1 slice.18
  67.7 2.0 %copy.26.sq_ref = s32[4096,1]{1,0:T(8,128)} copy(s32[4096,1]{0,1:T(1,128)S(1)} %bitcast.36) | data formatting | bytes 32768 | tf_op jit(solution)/shard_map/reshape | solution.py:76
  69.7 0.2 convert_reduce_fusion
  69.9 0.6 and_select_fusion
  70.5 0.0 all-to-all-done
  70.5 3.7 %copy.25 = bf16[16,256,1,192]{3,1,0,2:T(8,128)(2,1)} copy(bf16[16,256,1,192]{1,3,0,2:T(8,128)(2,1)} %bitcast.4) | data formatting | bytes 3145728 | tf_op jit(solution)/shard_map/all_to_all | solution.py:87
  74.2 0.0 copy-done.2
  74.2 3.9 %fusion.1 = (bf16[4096,64]{1,0:T(8,128)(2,1)}, bf16[4096,64]{1,0:T(8,128)(2,1)}, bf16[4096,64]{1,0:T(8,128)(2,1)}) fusion(bf16[4096,192]{1,0:T(8,128)(2,1)} %bitcast.25), kind=kLoop, calls=%fused_computation.18 | loop fusion | flops 262144 | bytes 3145728 | tf_op jit(solution)/shard_map/slice | solution.py:93
  78.2 34.7 %shard_map.86 = bf16[4096,64]{1,0:T(8,128)(2,1)} custom-call(s32[8]{0:T(128)} %get-tuple-element.10.lo_ref, s32[8]{0:T(128)} %get-tuple-element.9.hi_ref, bf16[4096,64]{1,0:T(8,128)(2,1)} %get-tuple-element.6.q_ref, bf16[8,512,64]{2,1,0:T(8,128)(2,1)} %bitcast.30, bf16[8,512,64]{2,1,0:T(8,128)(2,1)} %bitcast.29, s32[4096,1]{1,0:T(8,128)} %copy.26.sq_ref, ...), custom_call_target="tpu_custom_call" | custom-call | tf_op jit(solution)/shard_map/pallas_call | solution.py:65
  112.9 0.5 broadcast.59
  113.4 2.8 %reduce = bf16[4096,64]{1,0:T(8,128)(2,1)S(1)} reduce(bf16[4096,1,64]{2,0,1:T(8,128)(2,1)} %bitcast.28, bf16[]{:T(256)} %broadcast.59), dimensions={1}, to_apply=%copy.27.reduce_sub_computation | reduce | bytes 1048578 | tf_op jit(solution)/shard_map/reshape | solution.py:94
  116.2 1.5 reshape.60
  117.7 5.9 %all-to-all-start.1 = ((bf16[16,2,8192]{2,1,0:T(2,128)(2,1)}), bf16[16,2,8192]{2,1,0:T(2,128)(2,1)S(1)}, u32[]{:S(2)}, u32[]{:S(2)}) async-start(bf16[16,2,8192]{2,1,0:T(2,128)(2,1)} %reshape.60), calls=%async_computation.1 | async-start | bytes 1048576 | tf_op jit(solution)/shard_map/all_to_all | solution.py:95
  123.7 2.9 %slice.27 = bf16[4096,128]{1,0:T(8,128)(2,1)} slice(bf16[4096,192]{1,0:T(8,128)(2,1)} %bitcast.26), slice={[0:4096], [64:192]} | slice | bytes 2097152 | tf_op jit(solution)/shard_map/slice | solution.py:90
  126.6 14.3 %all-to-all-done.1 = bf16[16,2,8192]{2,1,0:T(2,128)(2,1)S(1)} async-done(((bf16[16,2,8192]{2,1,0:T(2,128)(2,1)}), bf16[16,2,8192]{2,1,0:T(2,128)(2,1)S(1)}, u32[]{:S(2)}, u32[]{:S(2)}) %all-to-all-start.1) | async-done | bytes 524320 | tf_op jit(solution)/shard_map/all_to_all | solution.py:95
  140.9 3.6 %reshape.61 = bf16[4096,1,64]{2,1,0:T(2,128)(2,1)} reshape(bf16[16,2,8192]{2,1,0:T(2,128)(2,1)S(1)} %all-to-all-done.1) | data formatting | bytes 1048576
  144.4 0.0 copy-start.1
  144.5 0.0 copy-start.3
  144.5 4.6 %copy.28 = bf16[4096,1,64]{0,2,1:T(8,128)(2,1)S(1)} copy(bf16[4096,1,64]{2,1,0:T(2,128)(2,1)} %reshape.61) | data formatting | bytes 1048576 | tf_op jit(solution)/shard_map/all_to_all | solution.py:95
  149.1 0.1 copy.30
  149.2 0.2 copy.29
  149.4 0.0 copy-done
  149.4 0.0 copy-done.1
  149.4 0.0 copy-done.3
  149.4 0.0 copy-start.4
  149.4 0.0 copy-start.5
  149.4 0.8 fusion.2
  150.3 0.3 multiply_reduce_fusion
  150.5 0.0 copy-done.4
  150.5 0.0 copy-done.5
  150.6 1.0 add_convert_fusion
  (2 shorter events, 0.0 us)
Async XLA Ops:
  0.6 148.8 %copy-start = (bf16[1024,1024]{1,0:T(8,128)(2,1)S(1)}, bf16[1024,1024]{1,0:T(8,128)(2,1)}, u32[]{:S(2)}) copy-start(bf16[1024,1024]{1,0:T(8,128)(2,1)} %param.10) | copy-start | bytes 6291460
  9.3 10.1 %copy-start.6 = (s32[256]{0:T(256)S(1)}, s32[256]{0:T(256)}, u32[]{:S(2)}) copy-start(s32[256]{0:T(256)} %param.8) | copy-start | bytes 3076
  9.3 61.2 %all-to-all-start = ((bf16[256,16,192]{0,2,1:T(8,128)(2,1)}), bf16[256,16,192]{0,2,1:T(8,128)(2,1)}, u32[]{:S(2)}, u32[]{:S(2)}) async-start(bf16[256,16,192]{0,2,1:T(8,128)(2,1)} %bitcast.27), calls=%async_computation | async-start | bytes 3145728 | tf_op jit(solution)/shard_map/all_to_all | solution.py:87
  67.6 6.7 %copy-start.2 = (s32[16,1,256]{2,1,0:T(1,128)}, s32[16,1,256]{2,1,0:T(1,128)S(1)}, u32[]{:S(2)}) copy-start(s32[16,1,256]{2,1,0:T(1,128)S(1)} %all-gather) | copy-start | bytes 49156
  117.7 23.1 %all-to-all-start.1 = ((bf16[16,2,8192]{2,1,0:T(2,128)(2,1)}), bf16[16,2,8192]{2,1,0:T(2,128)(2,1)S(1)}, u32[]{:S(2)}, u32[]{:S(2)}) async-start(bf16[16,2,8192]{2,1,0:T(2,128)(2,1)} %reshape.60), calls=%async_computation.1 | async-start | bytes 1048576 | tf_op jit(solution)/shard_map/all_to_all | solution.py:95
  144.4 4.9 %copy-start.1 = (bf16[256,1024]{1,0:T(8,128)(2,1)S(1)}, bf16[256,1024]{1,0:T(8,128)(2,1)}, u32[]{:S(2)}) copy-start(bf16[256,1024]{1,0:T(8,128)(2,1)} %param.7) | copy-start | bytes 1572868
  144.5 5.0 %copy-start.3 = (f32[1024]{0:T(1024)S(1)}, f32[1024]{0:T(1024)}, u32[]{:S(2)}) copy-start(f32[1024]{0:T(1024)} %param.11) | copy-start | bytes 12292
  149.4 1.1 copy-start.4
  149.4 1.1 copy-start.5

commit v3 on v2

v3 whole, which is shorter than its diff:
```python
import math

import jax
import jax.numpy as jnp
from jax import lax
from jax.experimental import pallas as pl
from jax.experimental.pallas import tpu as pltpu
from jax.sharding import PartitionSpec as P

HEADS = 16
HEAD = 64
SEGS = 4
BQ = 256
BK = 256
INTERPRET = False


def seg_of(x, b1, b2, b3):
    return (x >= b1).astype(jnp.int32) + (x >= b2).astype(jnp.int32) + (x >= b3).astype(jnp.int32)


def attn_kernel(lo_ref, hi_ref, bnd_ref, q_ref, kv_ref, o_ref):
    i = pl.program_id(0)
    b1, b2, b3 = bnd_ref[0], bnd_ref[1], bnd_ref[2]
    q0 = i * BQ
    scale = 1.0 / math.sqrt(HEAD)
    q = q_ref[0, :, 2 * HEAD:] * jnp.asarray(scale, jnp.bfloat16)
    rows = q0 + lax.broadcasted_iota(jnp.int32, (BQ, 1), 0)
    sq = seg_of(rows, b1, b2, b3)
    q_first = seg_of(q0, b1, b2, b3)
    q_last = seg_of(q0 + BQ - 1, b1, b2, b3)

    def tile(j, carry, masked):
        m, l, acc = carry
        kv = kv_ref[j]
        s = lax.dot_general(q, kv[:, :HEAD], (((1,), (1,)), ((), ())), preferred_element_type=jnp.float32)
        if masked:
            cols = j * BK + lax.broadcasted_iota(jnp.int32, (1, BK), 1)
            s = jnp.where(sq == seg_of(cols, b1, b2, b3), s, -jnp.inf)
        m_new = jnp.maximum(m, jnp.max(s, axis=1, keepdims=True))
        m_safe = jnp.where(m_new == -jnp.inf, 0.0, m_new)
        p = jnp.exp(s - m_safe)
        alpha = jnp.exp(m - m_safe)
        l = alpha * l + jnp.sum(p, axis=1, keepdims=True)
        acc = alpha * acc + jnp.dot(p.astype(jnp.bfloat16), kv[:, :2 * HEAD], preferred_element_type=jnp.float32)
        return m_new, l, acc

    def body(j, carry):
        k_first = seg_of(j * BK, b1, b2, b3)
        k_last = seg_of(j * BK + BK - 1, b1, b2, b3)
        inside = (q_first == q_last) & (k_first == k_last) & (q_first == k_first)
        return lax.cond(
            inside,
            lambda c: tile(j, c, False),
            lambda c: tile(j, c, True),
            carry,
        )

    m0 = jnp.full((BQ, 1), -jnp.inf, jnp.float32)
    l0 = jnp.zeros((BQ, 1), jnp.float32)
    acc0 = jnp.zeros((BQ, 2 * HEAD), jnp.float32)
    _, l, acc = lax.fori_loop(lo_ref[i], hi_ref[i], body, (m0, l0, acc0))
    out = pltpu.roll(acc / l, HEAD, 1)
    o_ref[...] = out[:, :HEAD].astype(o_ref.dtype)


def attention(mine, counts):
    nk = mine.shape[0]
    rows = nk * BK
    nq = rows // BQ
    b1, b2, b3 = counts[1], counts[2], counts[3]
    bounds = jnp.concatenate([jnp.zeros((1,), jnp.int32), counts[1:], jnp.full((1,), rows, jnp.int32)])
    starts = jnp.arange(nq, dtype=jnp.int32) * BQ
    first = seg_of(starts, b1, b2, b3)
    last = seg_of(starts + BQ - 1, b1, b2, b3)
    lo = bounds[first] // BK
    hi = (bounds[last + 1] + BK - 1) // BK
    grid_spec = pltpu.PrefetchScalarGridSpec(
        num_scalar_prefetch=3,
        grid=(nq,),
        in_specs=[
            pl.BlockSpec((1, BQ, 3 * HEAD), lambda i, lo, hi, bnd: (i, 0, 0)),
            pl.BlockSpec((nk, BK, 3 * HEAD), lambda i, lo, hi, bnd: (0, 0, 0)),
        ],
        out_specs=pl.BlockSpec((BQ, HEAD), lambda i, lo, hi, bnd: (i, 0)),
    )
    return pl.pallas_call(
        attn_kernel,
        grid_spec=grid_spec,
        out_shape=jax.ShapeDtypeStruct((rows, HEAD), jnp.bfloat16),
        interpret=INTERPRET,
    )(lo, hi, counts[1:], mine.reshape(nq, BQ, 3 * HEAD), mine)


def shards(tokens, segments, qkv_weight, out_weight, out_bias, ln_gain, ln_bias):
    tok_rows, width = tokens.shape
    groups = lax.axis_size("seq")
    levels = jnp.arange(SEGS + 1, dtype=jnp.int32)
    local = jnp.sum((segments[None, :] < levels[:, None]).astype(jnp.int32), axis=1)
    counts = lax.psum(local, "seq")
    proj = jnp.dot(tokens, qkv_weight, preferred_element_type=jnp.float32).astype(jnp.bfloat16)
    grouped = proj.reshape(tok_rows, HEADS, 3, HEAD)
    payload = jnp.concatenate([grouped[:, :, 1], grouped[:, :, 2], grouped[:, :, 0]], axis=-1)
    payload = jnp.moveaxis(payload, 1, 0)
    mine = lax.all_to_all(payload, "seq", split_axis=0, concat_axis=0, tiled=True)
    kv_cache = mine[:, :, :2 * HEAD].reshape(groups * tok_rows, 2 * HEAD)
    context = attention(mine.reshape(groups * tok_rows // BK, BK, 3 * HEAD), counts)
    ctx = lax.all_to_all(context.reshape(groups, tok_rows, HEAD), "seq", split_axis=0, concat_axis=0, tiled=True)
    mixed = (
        jnp.einsum("htc,hcd->td", ctx, out_weight.reshape(HEADS, HEAD, width), preferred_element_type=jnp.float32)
        + out_bias
        + tokens.astype(jnp.float32)
    )
    mean = jnp.mean(mixed, axis=1, keepdims=True)
    centered = mixed - mean
    variance = jnp.mean(centered * centered, axis=1, keepdims=True)
    normed = centered / jnp.sqrt(variance + 1e-05) * ln_gain + ln_bias
    return (normed.astype(jnp.bfloat16), kv_cache)


def solution(mesh):
    in_specs = (P(("rep", "seq"), None), P(("rep", "seq")), P(), P(), P(), P(), P())
    out_specs = (P(("rep", "seq"), None), P("rep", "seq"))
    return jax.shard_map(shards, mesh=mesh, in_specs=in_specs, out_specs=out_specs, check_vma=False)
```

time: 155 us -> 178 us (1.15)
  the two profiles are of different devices: /device:TPU:1 before, /device:TPU:23 now
where the time goes in v3:
time: 178 us
  Pallas kernels  75.7 us (43%)
  blocking collectives  42.9 us (24%)
  starting transfers between devices  16.2 us (9%)
  waiting for transfers between devices  14.9 us (8%)
  local copies, waits for them, and re-layouts  14.4 us (8%)
  matrix products  6.87 us (4%)
  other arithmetic  5.75 us (3%)
    pallas_call x1, Pallas kernels, attention(): pl.pallas_call(attn_kernel, grid_spec=grid_spec, out_shape=jax.ShapeDtype...  75.7 us
    psum x1, blocking collectives, shards(): counts = lax.psum(local, 'seq')  42.9 us
    all_to_all x1, waiting for transfers between devices, shards(): lax.all_to_all(context.reshape(groups, tok_rows, HEAD), 'seq', split_axis...  14.9 us
    all_to_all x1, starting transfers between devices, shards(): lax.all_to_all(payload, 'seq', split_axis=0, concat_axis=0, tiled=True)  9.28 us
    all_to_all x1, starting transfers between devices, shards(): lax.all_to_all(context.reshape(groups, tok_rows, HEAD), 'seq', split_axis...  6.88 us
    dot_general x1, matrix products, shards(): jnp.dot(tokens, qkv_weight, preferred_element_type=jnp.float32)  6.05 us
    all_to_all x1, local copies, waits for them, and re-layouts, shards(): lax.all_to_all(payload, 'seq', split_axis=0, concat_axis=0, tiled=True)  3.69 us
  transfers between devices with their start and end apart: 2, of which 1 were waited for; matrix products, arithmetic and copies ran while one was open for 4% of the time, Pallas kernels for 0%

profile of v3, /device:TPU:23, one launch (start us, length us, event | category | flops | bytes accessed | tf_op | source)
XLA Modules:
  0.0 177.5 jit_solution(8468996640200582948)
XLA Ops:
  0.6 0.0 copy-start
  0.6 6.1 %convolution_convert_fusion = bf16[256,3072]{1,0:T(8,128)(2,1)} fusion(bf16[256,1024]{1,0:T(8,128)(2,1)} %param.7, bf16[1024,3072]{1,0:T(8,128)(2,1)} %param.9), kind=kOutput, calls=%fused_computation.2 | convolution fusion | flops 1611399168 | bytes 8388608 | tf_op jit(solution)/shard_map/dot_general | solution.py:101
  6.7 2.6 %copy.28 = bf16[256,3072]{0,1:T(8,128)(2,1)} copy(bf16[256,3072]{1,0:T(8,128)(2,1)} %convolution_convert_fusion) | data formatting | bytes 3145728 | tf_op jit(solution)/shard_map/convert_element_type | solution.py:101
  9.3 1.5 slice_bitcast_fusion.2
  10.8 1.3 maximum_bitcast_fusion
  12.0 0.0 copy-start.6
  12.0 9.3 %all-to-all-start = ((bf16[16,256,192]{1,2,0:T(8,128)(2,1)}), bf16[16,256,192]{1,2,0:T(8,128)(2,1)}, u32[]{:S(2)}, u32[]{:S(2)}) async-start(bf16[16,256,192]{1,2,0:T(8,128)(2,1)} %maximum_bitcast_fusion), calls=%async_computation | async-start | bytes 3145728 | tf_op jit(solution)/shard_map/all_to_all | solution.py:105
  21.3 0.0 copy-done.6
  21.3 0.1 convert_reduce_fusion
  21.4 42.9 %psum.7 = s32[5]{0:T(128)S(1)} all-reduce(s32[5]{0:T(128)S(1)} %convert_reduce_fusion), channel_id=1, replica_groups=mesh['seq'=16,'rep'=16] {'seq'}, use_global_device_ids=true, to_apply=%region_1.0 | all-reduce | flops 5 | bytes 40 | tf_op jit(solution)/shard_map/psum | solution.py:100
  64.4 0.1 slice.25.bnd_ref
  64.4 0.0 copy-start.5
  64.4 0.1 pad_add_fusion
  64.5 0.6 fusion.8
  65.1 1.8 %fusion.6 = (s32[16]{0:T(128)S(1)}, s32[16]{0:T(128)S(1)}) fusion(s32[]{:T(128)} %bitcast.2, s32[]{:T(128)} %bitcast.1, s32[]{:T(128)} %bitcast), kind=kLoop, calls=%fused_computation.37 | loop fusion | flops 400 | bytes 140 | tf_op jit(solution)/shard_map/select_n | solution.py:76
  67.0 0.7 gather_fusion.1
  67.6 0.7 gather_fusion
  68.3 0.6 and_select_fusion.hi_ref
  68.9 0.5 and_select_fusion.1.lo_ref
  69.4 0.0 all-to-all-done
  69.4 3.7 %copy.31.q_ref.kv_ref = bf16[16,256,192]{2,1,0:T(8,128)(2,1)} copy(bf16[16,256,192]{1,2,0:T(8,128)(2,1)} %all-to-all-done) | data formatting | bytes 3145728 | tf_op jit(solution)/shard_map/all_to_all | solution.py:105
  73.1 0.0 copy-done.5
  73.1 75.7 %shard_map.86 = bf16[4096,64]{1,0:T(8,128)(2,1)} custom-call(s32[16]{0:T(128)} %and_select_fusion.1.lo_ref, s32[16]{0:T(128)} %and_select_fusion.hi_ref, s32[4]{0:T(128)} %copy-done.5, bf16[16,256,192]{2,1,0:T(8,128)(2,1)} %copy.31.q_ref.kv_ref, bf16[16,256,192]{2,1,0:T(8,128)(2,1)} %copy.31.q_ref.kv_ref), custom_call_target="tpu_custom_call" | custom-call | tf_op jit(solution)/shard_map/pallas_call | solution.py:87
  148.8 0.0 copy-start.1
  148.9 0.0 copy-start.2
  148.9 2.4 %copy.33 = bf16[16,256,64]{1,2,0:T(8,128)(2,1)} copy(bf16[16,256,64]{2,1,0:T(8,128)(2,1)} %bitcast.35) | data formatting | bytes 1048576 | tf_op jit(solution)/shard_map/reshape | solution.py:108
  151.3 6.9 %all-to-all-start.1 = ((bf16[16,256,64]{1,2,0:T(8,128)(2,1)}), bf16[16,256,64]{1,2,0:T(8,128)(2,1)S(1)}, u32[]{:S(2)}, u32[]{:S(2)}) async-start(bf16[16,256,64]{1,2,0:T(8,128)(2,1)} %copy.33), calls=%async_computation.1 | async-start | bytes 1048576 | tf_op jit(solution)/shard_map/all_to_all | solution.py:108
  158.1 2.3 %slice.40 = bf16[16,256,128]{2,1,0:T(8,128)(2,1)} slice(bf16[16,256,192]{2,1,0:T(8,128)(2,1)} %copy.31.q_ref.kv_ref), slice={[0:16], [0:256], [0:128]} | slice | bytes 2097152 | tf_op jit(solution)/shard_map/slice | solution.py:106
  160.4 14.9 %all-to-all-done.1 = bf16[16,256,64]{1,2,0:T(8,128)(2,1)S(1)} async-done(((bf16[16,256,64]{1,2,0:T(8,128)(2,1)}), bf16[16,256,64]{1,2,0:T(8,128)(2,1)S(1)}, u32[]{:S(2)}, u32[]{:S(2)}) %all-to-all-start.1) | async-done | bytes 524320 | tf_op jit(solution)/shard_map/all_to_all | solution.py:108
  175.3 0.0 copy-done
  175.3 0.0 copy-done.1
  175.3 0.0 copy-done.2
  175.4 0.0 copy-start.3
  175.4 0.0 copy-start.4
  175.4 0.8 fusion.9
  176.2 0.3 multiply_reduce_fusion
  176.5 0.0 copy-done.3
  176.5 0.0 copy-done.4
  176.5 1.0 add_convert_fusion
  (4 shorter events, 0.0 us)
Async XLA Ops:
  0.6 174.7 %copy-start = (bf16[1024,1024]{1,0:T(8,128)(2,1)S(1)}, bf16[1024,1024]{1,0:T(8,128)(2,1)}, u32[]{:S(2)}) copy-start(bf16[1024,1024]{1,0:T(8,128)(2,1)} %param.10) | copy-start | bytes 6291460
  12.0 9.3 %copy-start.6 = (s32[256]{0:T(256)S(1)}, s32[256]{0:T(256)}, u32[]{:S(2)}) copy-start(s32[256]{0:T(256)} %param.8) | copy-start | bytes 3076
  12.0 57.4 %all-to-all-start = ((bf16[16,256,192]{1,2,0:T(8,128)(2,1)}), bf16[16,256,192]{1,2,0:T(8,128)(2,1)}, u32[]{:S(2)}, u32[]{:S(2)}) async-start(bf16[16,256,192]{1,2,0:T(8,128)(2,1)} %maximum_bitcast_fusion), calls=%async_computation | async-start | bytes 3145728 | tf_op jit(solution)/shard_map/all_to_all | solution.py:105
  64.4 8.7 %copy-start.5 = (s32[4]{0:T(128)}, s32[4]{0:T(128)S(1)}, u32[]{:S(2)}) copy-start(s32[4]{0:T(128)S(1)} %slice.25.bnd_ref) | copy-start | bytes 52
  148.8 26.5 %copy-start.1 = (bf16[256,1024]{1,0:T(8,128)(2,1)S(1)}, bf16[256,1024]{1,0:T(8,128)(2,1)}, u32[]{:S(2)}) copy-start(bf16[256,1024]{1,0:T(8,128)(2,1)} %param.7) | copy-start | bytes 1572868
  148.9 26.5 %copy-start.2 = (f32[1024]{0:T(1024)S(1)}, f32[1024]{0:T(1024)}, u32[]{:S(2)}) copy-start(f32[1024]{0:T(1024)} %param.11) | copy-start | bytes 12292
  151.3 24.1 %all-to-all-start.1 = ((bf16[16,256,64]{1,2,0:T(8,128)(2,1)}), bf16[16,256,64]{1,2,0:T(8,128)(2,1)S(1)}, u32[]{:S(2)}, u32[]{:S(2)}) async-start(bf16[16,256,64]{1,2,0:T(8,128)(2,1)} %copy.33), calls=%async_computation.1 | async-start | bytes 1048576 | tf_op jit(solution)/shard_map/all_to_all | solution.py:108
  175.4 1.1 copy-start.3
  175.4 1.1 copy-start.4

commit v4 on v3

--- a/solution.py
+++ b/solution.py
@@ -10,8 +10,8 @@
 HEADS = 16
 HEAD = 64
 SEGS = 4
-BQ = 256
-BK = 256
+BQ = 512
+BK = 512
 INTERPRET = False
 
 
@@ -27,34 +27,20 @@
     q = q_ref[0, :, 2 * HEAD:] * jnp.asarray(scale, jnp.bfloat16)
     rows = q0 + lax.broadcasted_iota(jnp.int32, (BQ, 1), 0)
     sq = seg_of(rows, b1, b2, b3)
-    q_first = seg_of(q0, b1, b2, b3)
-    q_last = seg_of(q0 + BQ - 1, b1, b2, b3)
 
-    def tile(j, carry, masked):
+    def body(j, carry):
         m, l, acc = carry
-        kv = kv_ref[j]
+        kv = kv_ref[j, :, :2 * HEAD]
         s = lax.dot_general(q, kv[:, :HEAD], (((1,), (1,)), ((), ())), preferred_element_type=jnp.float32)
-        if masked:
-            cols = j * BK + lax.broadcasted_iota(jnp.int32, (1, BK), 1)
-            s = jnp.where(sq == seg_of(cols, b1, b2, b3), s, -jnp.inf)
+        cols = j * BK + lax.broadcasted_iota(jnp.int32, (1, BK), 1)
+        s = jnp.where(sq == seg_of(cols, b1, b2, b3), s, -jnp.inf)
         m_new = jnp.maximum(m, jnp.max(s, axis=1, keepdims=True))
         m_safe = jnp.where(m_new == -jnp.inf, 0.0, m_new)
         p = jnp.exp(s - m_safe)
         alpha = jnp.exp(m - m_safe)
         l = alpha * l + jnp.sum(p, axis=1, keepdims=True)
-        acc = alpha * acc + jnp.dot(p.astype(jnp.bfloat16), kv[:, :2 * HEAD], preferred_element_type=jnp.float32)
+        acc = alpha * acc + jnp.dot(p.astype(jnp.bfloat16), kv, preferred_element_type=jnp.float32)
         return m_new, l, acc
-
-    def body(j, carry):
-        k_first = seg_of(j * BK, b1, b2, b3)
-        k_last = seg_of(j * BK + BK - 1, b1, b2, b3)
-        inside = (q_first == q_last) & (k_first == k_last) & (q_first == k_first)
-        return lax.cond(
-            inside,
-            lambda c: tile(j, c, False),
-            lambda c: tile(j, c, True),
-            carry,
-        )
 
     m0 = jnp.full((BQ, 1), -jnp.inf, jnp.float32)
     l0 = jnp.zeros((BQ, 1), jnp.float32)

time: 178 us -> 136 us (0.76)
  the two profiles are of different devices: /device:TPU:23 before, /device:TPU:1 now
where the time goes in v4:
time: 136 us; the launch traced here: 135 us
  blocking collectives  42.9 us (32%)
  Pallas kernels  31.1 us (23%)
  starting transfers between devices  17 us (12%)
  local copies, waits for them, and re-layouts  14.7 us (11%)
  waiting for transfers between devices  14.7 us (11%)
  matrix products  8.1 us (6%)
  other arithmetic  5.82 us (4%)
    psum x1, blocking collectives, shards(): counts = lax.psum(local, 'seq')  42.9 us
    pallas_call x1, Pallas kernels, attention(): pl.pallas_call(attn_kernel, grid_spec=grid_spec, out_shape=jax.ShapeDtype...  31.1 us
    all_to_all x1, waiting for transfers between devices, shards(): lax.all_to_all(context.reshape(groups, tok_rows, HEAD), 'seq', split_axis...  14.7 us
    all_to_all x1, starting transfers between devices, shards(): lax.all_to_all(payload, 'seq', split_axis=0, concat_axis=0, tiled=True)  10.1 us
    all_to_all x1, starting transfers between devices, shards(): lax.all_to_all(context.reshape(groups, tok_rows, HEAD), 'seq', split_axis...  6.88 us
    dot_general x1, matrix products, shards(): jnp.dot(tokens, qkv_weight, preferred_element_type=jnp.float32)  6.06 us
    all_to_all x1, local copies, waits for them, and re-layouts, shards(): lax.all_to_all(payload, 'seq', split_axis=0, concat_axis=0, tiled=True)  3.7 us
  transfers between devices with their start and end apart: 2, of which 1 were waited for; matrix products, arithmetic and copies ran while one was open for 6% of the time, Pallas kernels for 0%

profile of v4, /device:TPU:1, one launch (start us, length us, event | category | flops | bytes accessed | tf_op | source)
XLA Modules:
  0.0 135.1 jit_solution(6117133192489393156)
XLA Ops:
  0.6 0.0 copy-start
  0.6 6.1 %convolution_convert_fusion = bf16[256,3072]{1,0:T(8,128)(2,1)} fusion(bf16[256,1024]{1,0:T(8,128)(2,1)} %param.7, bf16[1024,3072]{1,0:T(8,128)(2,1)} %param.9), kind=kOutput, calls=%fused_computation.2 | convolution fusion | flops 1611399168 | bytes 8388608 | tf_op jit(solution)/shard_map/dot_general | solution.py:87
  6.7 2.6 %copy.24 = bf16[256,3072]{0,1:T(8,128)(2,1)} copy(bf16[256,3072]{1,0:T(8,128)(2,1)} %convolution_convert_fusion) | data formatting | bytes 3145728 | tf_op jit(solution)/shard_map/convert_element_type | solution.py:87
  9.3 1.5 %slice_bitcast_fusion.2 = (bf16[256,16,64]{0,2,1:T(8,128)(2,1)S(1)}, bf16[256,16,64]{0,2,1:T(8,128)(2,1)S(1)}, bf16[256,16,64]{0,2,1:T(8,128)(2,1)S(1)}) fusion(bf16[256,16,3,64]{0,3,2,1:T(8,128)(2,1)} %bitcast.37), kind=kLoop, calls=%fused_computation.11 | loop fusion | bytes 3145728 | tf_op jit(solution)/shard_map/squeeze | solution.py:89
  10.8 1.3 maximum_bitcast_fusion
  12.0 0.0 copy-start.5
  12.0 10.1 %all-to-all-start = ((bf16[16,256,192]{1,2,0:T(8,128)(2,1)}), bf16[16,256,192]{1,2,0:T(8,128)(2,1)}, u32[]{:S(2)}, u32[]{:S(2)}) async-start(bf16[16,256,192]{1,2,0:T(8,128)(2,1)} %maximum_bitcast_fusion), calls=%async_computation | async-start | bytes 3145728 | tf_op jit(solution)/shard_map/all_to_all | solution.py:91
  22.1 0.0 copy-done.5
  22.2 0.1 convert_reduce_fusion
  22.3 42.9 %psum.7 = s32[5]{0:T(128)S(1)} all-reduce(s32[5]{0:T(128)S(1)} %convert_reduce_fusion), channel_id=1, replica_groups=mesh['seq'=16,'rep'=16] {'seq'}, use_global_device_ids=true, to_apply=%region_1.0 | all-reduce | flops 5 | bytes 40 | tf_op jit(solution)/shard_map/psum | solution.py:86
  65.2 0.1 slice.25.bnd_ref
  65.3 0.0 copy-start.4
  65.3 0.1 pad_add_fusion
  65.4 0.7 fusion.8
  66.0 1.9 %fusion.6 = (s32[8]{0:T(128)S(1)}, s32[8]{0:T(128)S(1)}) fusion(s32[]{:T(128)} %bitcast.2, s32[]{:T(128)} %bitcast.1, s32[]{:T(128)} %bitcast), kind=kLoop, calls=%fused_computation.37 | loop fusion | flops 200 | bytes 76 | tf_op jit(solution)/shard_map/select_n | solution.py:62
  68.0 0.6 gather_fusion
  68.6 0.6 gather_fusion.1
  69.3 0.5 and_select_fusion.1.lo_ref
  69.8 0.6 and_select_fusion.hi_ref
  70.4 0.0 all-to-all-done
  70.4 3.7 %copy.27 = bf16[16,256,192]{2,1,0:T(8,128)(2,1)} copy(bf16[16,256,192]{1,2,0:T(8,128)(2,1)} %all-to-all-done) | data formatting | bytes 3145728 | tf_op jit(solution)/shard_map/all_to_all | solution.py:91
  74.1 0.0 copy-done.4
  74.1 31.1 %shard_map.86 = bf16[4096,64]{1,0:T(8,128)(2,1)} custom-call(s32[8]{0:T(128)} %and_select_fusion.1.lo_ref, s32[8]{0:T(128)} %and_select_fusion.hi_ref, s32[4]{0:T(128)} %copy-done.4, bf16[8,512,192]{2,1,0:T(8,128)(2,1)} %bitcast.35, bf16[8,512,192]{2,1,0:T(8,128)(2,1)} %bitcast.36), custom_call_target="tpu_custom_call" | custom-call | tf_op jit(solution)/shard_map/pallas_call | solution.py:73
  105.1 2.3 %copy.28 = bf16[16,256,64]{1,2,0:T(8,128)(2,1)} copy(bf16[16,256,64]{2,1,0:T(8,128)(2,1)} %bitcast.38) | data formatting | bytes 1048576 | tf_op jit(solution)/shard_map/reshape | solution.py:94
  107.5 6.9 %all-to-all-start.1 = ((bf16[16,256,64]{1,2,0:T(8,128)(2,1)}), bf16[16,256,64]{1,2,0:T(8,128)(2,1)}, u32[]{:S(2)}, u32[]{:S(2)}) async-start(bf16[16,256,64]{1,2,0:T(8,128)(2,1)} %copy.28), calls=%async_computation.1 | async-start | bytes 1048576 | tf_op jit(solution)/shard_map/all_to_all | solution.py:94
  114.4 0.0 copy-start.1
  114.4 1.3 slice.40
  115.7 1.3 copy.29
  117.0 14.7 %all-to-all-done.1 = bf16[16,256,64]{1,2,0:T(8,128)(2,1)} async-done(((bf16[16,256,64]{1,2,0:T(8,128)(2,1)}), bf16[16,256,64]{1,2,0:T(8,128)(2,1)}, u32[]{:S(2)}, u32[]{:S(2)}) %all-to-all-start.1) | async-done | bytes 524320 | tf_op jit(solution)/shard_map/all_to_all | solution.py:94
  131.7 0.0 copy-done
  131.7 0.0 copy-done.1
  131.7 0.0 copy-start.2
  131.7 0.0 copy-start.3
  131.7 2.0 %fusion.9 = (f32[256]{0:T(256)S(1)}, f32[256,1024]{1,0:T(8,128)S(1)}) fusion(bf16[256,1024]{1,0:T(8,128)(2,1)} %param.7, f32[1024]{0:T(1024)S(1)} %copy-done.1, bf16[16,256,64]{1,2,0:T(8,128)(2,1)} %all-to-all-done.1, bf16[16,64,1024]{2,1,0:T(8,128)(2,1)S(1)} %bitcast.34), kind=kOutput, calls=%fused_computation.43 | convolution fusion | flops 537919232 | bytes 4199424 | tf_op jit(solution)/shard_map/htc,hcd->td/dot_general | solution.py:96
  133.8 0.3 multiply_reduce_fusion
  134.0 0.0 copy-done.2
  134.0 0.0 copy-done.3
  134.0 1.0 add_convert_fusion
  (4 shorter events, 0.0 us)
Async XLA Ops:
  0.6 131.1 %copy-start = (bf16[1024,1024]{1,0:T(8,128)(2,1)S(1)}, bf16[1024,1024]{1,0:T(8,128)(2,1)}, u32[]{:S(2)}) copy-start(bf16[1024,1024]{1,0:T(8,128)(2,1)} %param.10) | copy-start | bytes 6291460
  12.0 10.1 %copy-start.5 = (s32[256]{0:T(256)S(1)}, s32[256]{0:T(256)}, u32[]{:S(2)}) copy-start(s32[256]{0:T(256)} %param.8) | copy-start | bytes 3076
  12.0 58.3 %all-to-all-start = ((bf16[16,256,192]{1,2,0:T(8,128)(2,1)}), bf16[16,256,192]{1,2,0:T(8,128)(2,1)}, u32[]{:S(2)}, u32[]{:S(2)}) async-start(bf16[16,256,192]{1,2,0:T(8,128)(2,1)} %maximum_bitcast_fusion), calls=%async_computation | async-start | bytes 3145728 | tf_op jit(solution)/shard_map/all_to_all | solution.py:91
  65.3 8.8 %copy-start.4 = (s32[4]{0:T(128)}, s32[4]{0:T(128)S(1)}, u32[]{:S(2)}) copy-start(s32[4]{0:T(128)S(1)} %slice.25.bnd_ref) | copy-start | bytes 52
  107.5 24.2 %all-to-all-start.1 = ((bf16[16,256,64]{1,2,0:T(8,128)(2,1)}), bf16[16,256,64]{1,2,0:T(8,128)(2,1)}, u32[]{:S(2)}, u32[]{:S(2)}) async-start(bf16[16,256,64]{1,2,0:T(8,128)(2,1)} %copy.28), calls=%async_computation.1 | async-start | bytes 1048576 | tf_op jit(solution)/shard_map/all_to_all | solution.py:94
  114.4 17.3 %copy-start.1 = (f32[1024]{0:T(1024)S(1)}, f32[1024]{0:T(1024)}, u32[]{:S(2)}) copy-start(f32[1024]{0:T(1024)} %param.11) | copy-start | bytes 12292
  131.7 2.3 %copy-start.2 = (f32[1024]{0:T(1024)S(1)}, f32[1024]{0:T(1024)}, u32[]{:S(2)}) copy-start(f32[1024]{0:T(1024)} %param.13) | copy-start | bytes 12292
  131.7 2.3 %copy-start.3 = (f32[1024]{0:T(1024)S(1)}, f32[1024]{0:T(1024)}, u32[]{:S(2)}) copy-start(f32[1024]{0:T(1024)} %param.12) | copy-start | bytes 12292

commit v5 on v4

--- a/solution.py
+++ b/solution.py
@@ -84,6 +84,7 @@
     levels = jnp.arange(SEGS + 1, dtype=jnp.int32)
     local = jnp.sum((segments[None, :] < levels[:, None]).astype(jnp.int32), axis=1)
     counts = lax.psum(local, "seq")
+    counts, tokens = lax.optimization_barrier((counts, tokens))
     proj = jnp.dot(tokens, qkv_weight, preferred_element_type=jnp.float32).astype(jnp.bfloat16)
     grouped = proj.reshape(tok_rows, HEADS, 3, HEAD)
     payload = jnp.concatenate([grouped[:, :, 1], grouped[:, :, 2], grouped[:, :, 0]], axis=-1)

time: 136 us -> 138 us (1.015)
  the two profiles are of different devices: /device:TPU:1 before, /device:TPU:21 now
where the time goes in v5:
time: 138 us; the launch traced here: 137 us
  waiting for transfers between devices  48.3 us (35%)
  Pallas kernels  33.9 us (25%)
  local copies, waits for them, and re-layouts  14.7 us (11%)
  blocking collectives  13.9 us (10%)
  starting transfers between devices  11.4 us (8%)
  matrix products  7.96 us (6%)
  other arithmetic  6.58 us (5%)
    pallas_call x1, Pallas kernels, attention(): pl.pallas_call(attn_kernel, grid_spec=grid_spec, out_shape=jax.ShapeDtype...  33.9 us
    all_to_all x1, waiting for transfers between devices, shards(): lax.all_to_all(payload, 'seq', split_axis=0, concat_axis=0, tiled=True)  33.6 us
    all_to_all x1, waiting for transfers between devices, shards(): lax.all_to_all(context.reshape(groups, tok_rows, HEAD), 'seq', split_axis...  14.7 us
    psum x1, blocking collectives, shards(): counts = lax.psum(local, 'seq')  13.9 us
    all_to_all x1, starting transfers between devices, shards(): lax.all_to_all(payload, 'seq', split_axis=0, concat_axis=0, tiled=True)  7.23 us
    dot_general x1, matrix products, shards(): jnp.dot(tokens, qkv_weight, preferred_element_type=jnp.float32)  5.92 us
    all_to_all x1, starting transfers between devices, shards(): lax.all_to_all(context.reshape(groups, tok_rows, HEAD), 'seq', split_axis...  4.13 us
    all_to_all x1, local copies, waits for them, and re-layouts, shards(): lax.all_to_all(payload, 'seq', split_axis=0, concat_axis=0, tiled=True)  3.7 us
  transfers between devices with their start and end apart: 2, of which 2 were waited for; matrix products, arithmetic and copies ran while one was open for 6% of the time, Pallas kernels for 0%

profile of v5, /device:TPU:21, one launch (start us, length us, event | category | flops | bytes accessed | tf_op | source)
XLA Modules:
  0.0 137.4 jit_solution(2933560517809683606)
XLA Ops:
  0.6 0.0 copy-start
  0.6 0.9 convert_reduce_fusion
  1.6 13.9 %psum.7 = s32[5]{0:T(128)S(1)} all-reduce(s32[5]{0:T(128)S(1)} %convert_reduce_fusion), channel_id=1, replica_groups=mesh['seq'=16,'rep'=16] {'seq'}, use_global_device_ids=true, to_apply=%region_1.0 | all-reduce | flops 5 | bytes 40 | tf_op jit(solution)/shard_map/psum | solution.py:86
  15.5 5.9 %convolution_convert_fusion = bf16[256,3072]{1,0:T(8,128)(2,1)} fusion(bf16[256,1024]{1,0:T(8,128)(2,1)} %param.7, bf16[1024,3072]{1,0:T(8,128)(2,1)} %param.9), kind=kOutput, calls=%fused_computation.2 | convolution fusion | flops 1611399168 | bytes 8388608 | tf_op jit(solution)/shard_map/dot_general | solution.py:88
  21.4 2.6 %copy.24 = bf16[256,3072]{0,1:T(8,128)(2,1)} copy(bf16[256,3072]{1,0:T(8,128)(2,1)} %convolution_convert_fusion) | data formatting | bytes 3145728 | tf_op jit(solution)/shard_map/convert_element_type | solution.py:88
  24.0 1.5 %slice_bitcast_fusion.2 = (bf16[256,16,64]{0,2,1:T(8,128)(2,1)S(1)}, bf16[256,16,64]{0,2,1:T(8,128)(2,1)S(1)}, bf16[256,16,64]{0,2,1:T(8,128)(2,1)S(1)}) fusion(bf16[256,16,3,64]{0,3,2,1:T(8,128)(2,1)} %bitcast.37), kind=kLoop, calls=%fused_computation.11 | loop fusion | bytes 3145728 | tf_op jit(solution)/shard_map/squeeze | solution.py:90
  25.4 1.3 maximum_bitcast_fusion
  26.7 7.2 %all-to-all-start = ((bf16[16,256,192]{1,2,0:T(8,128)(2,1)}), bf16[16,256,192]{1,2,0:T(8,128)(2,1)}, u32[]{:S(2)}, u32[]{:S(2)}) async-start(bf16[16,256,192]{1,2,0:T(8,128)(2,1)} %maximum_bitcast_fusion), calls=%async_computation | async-start | bytes 3145728 | tf_op jit(solution)/shard_map/all_to_all | solution.py:92
  33.9 0.1 slice.25.bnd_ref
  34.0 0.0 copy-start.4
  34.0 0.1 pad_add_fusion
  34.1 0.6 fusion.8
  34.7 1.9 %fusion.6 = (s32[8]{0:T(128)S(1)}, s32[8]{0:T(128)S(1)}) fusion(s32[]{:T(128)} %bitcast.2, s32[]{:T(128)} %bitcast.1, s32[]{:T(128)} %bitcast), kind=kLoop, calls=%fused_computation.37 | loop fusion | flops 200 | bytes 76 | tf_op jit(solution)/shard_map/select_n | solution.py:62
  36.7 0.6 gather_fusion
  37.3 0.6 gather_fusion.1
  38.0 0.5 and_select_fusion.1.lo_ref
  38.5 0.5 and_select_fusion.hi_ref
  39.0 33.6 %all-to-all-done = bf16[16,256,192]{1,2,0:T(8,128)(2,1)} async-done(((bf16[16,256,192]{1,2,0:T(8,128)(2,1)}), bf16[16,256,192]{1,2,0:T(8,128)(2,1)}, u32[]{:S(2)}, u32[]{:S(2)}) %all-to-all-start) | async-done | bytes 1572896 | tf_op jit(solution)/shard_map/all_to_all | solution.py:92
  72.6 3.7 %copy.27 = bf16[16,256,192]{2,1,0:T(8,128)(2,1)} copy(bf16[16,256,192]{1,2,0:T(8,128)(2,1)} %all-to-all-done) | data formatting | bytes 3145728 | tf_op jit(solution)/shard_map/all_to_all | solution.py:92
  76.3 0.0 copy-done.4
  76.3 33.9 %shard_map.86 = bf16[4096,64]{1,0:T(8,128)(2,1)} custom-call(s32[8]{0:T(128)} %and_select_fusion.1.lo_ref, s32[8]{0:T(128)} %and_select_fusion.hi_ref, s32[4]{0:T(128)} %copy-done.4, bf16[8,512,192]{2,1,0:T(8,128)(2,1)} %bitcast.35, bf16[8,512,192]{2,1,0:T(8,128)(2,1)} %bitcast.36), custom_call_target="tpu_custom_call" | custom-call | tf_op jit(solution)/shard_map/pallas_call | solution.py:73
  110.2 2.3 %copy.28 = bf16[16,256,64]{1,2,0:T(8,128)(2,1)} copy(bf16[16,256,64]{2,1,0:T(8,128)(2,1)} %bitcast.38) | data formatting | bytes 1048576 | tf_op jit(solution)/shard_map/reshape | solution.py:95
  112.5 4.1 %all-to-all-start.1 = ((bf16[16,256,64]{1,2,0:T(8,128)(2,1)}), bf16[16,256,64]{1,2,0:T(8,128)(2,1)}, u32[]{:S(2)}, u32[]{:S(2)}) async-start(bf16[16,256,64]{1,2,0:T(8,128)(2,1)} %copy.28), calls=%async_computation.1 | async-start | bytes 1048576 | tf_op jit(solution)/shard_map/all_to_all | solution.py:95
  116.7 0.0 copy-start.1
  116.7 1.3 slice.40
  118.0 1.3 copy.29
  119.3 14.7 %all-to-all-done.1 = bf16[16,256,64]{1,2,0:T(8,128)(2,1)} async-done(((bf16[16,256,64]{1,2,0:T(8,128)(2,1)}), bf16[16,256,64]{1,2,0:T(8,128)(2,1)}, u32[]{:S(2)}, u32[]{:S(2)}) %all-to-all-start.1) | async-done | bytes 524320 | tf_op jit(solution)/shard_map/all_to_all | solution.py:95
  134.0 0.0 copy-done
  134.0 0.0 copy-done.1
  134.0 0.0 copy-start.2
  134.0 0.0 copy-start.3
  134.0 2.0 %fusion.9 = (f32[256]{0:T(256)S(1)}, f32[256,1024]{1,0:T(8,128)S(1)}) fusion(bf16[256,1024]{1,0:T(8,128)(2,1)} %param.7, f32[1024]{0:T(1024)S(1)} %copy-done.1, bf16[16,256,64]{1,2,0:T(8,128)(2,1)} %all-to-all-done.1, bf16[16,64,1024]{2,1,0:T(8,128)(2,1)S(1)} %bitcast.34), kind=kOutput, calls=%fused_computation.43 | convolution fusion | flops 537919232 | bytes 4199424 | tf_op jit(solution)/shard_map/htc,hcd->td/dot_general | solution.py:97
  136.1 0.3 multiply_reduce_fusion
  136.3 0.0 copy-done.2
  136.3 0.0 copy-done.3
  136.3 1.0 add_convert_fusion
  (4 shorter events, 0.0 us)
Async XLA Ops:
  0.6 133.4 %copy-start = (bf16[1024,1024]{1,0:T(8,128)(2,1)S(1)}, bf16[1024,1024]{1,0:T(8,128)(2,1)}, u32[]{:S(2)}) copy-start(bf16[1024,1024]{1,0:T(8,128)(2,1)} %param.10) | copy-start | bytes 6291460
  26.7 45.9 %all-to-all-start = ((bf16[16,256,192]{1,2,0:T(8,128)(2,1)}), bf16[16,256,192]{1,2,0:T(8,128)(2,1)}, u32[]{:S(2)}, u32[]{:S(2)}) async-start(bf16[16,256,192]{1,2,0:T(8,128)(2,1)} %maximum_bitcast_fusion), calls=%async_computation | async-start | bytes 3145728 | tf_op jit(solution)/shard_map/all_to_all | solution.py:92
  34.0 42.3 %copy-start.4 = (s32[4]{0:T(128)}, s32[4]{0:T(128)S(1)}, u32[]{:S(2)}) copy-start(s32[4]{0:T(128)S(1)} %slice.25.bnd_ref) | copy-start | bytes 52
  112.5 21.4 %all-to-all-start.1 = ((bf16[16,256,64]{1,2,0:T(8,128)(2,1)}), bf16[16,256,64]{1,2,0:T(8,128)(2,1)}, u32[]{:S(2)}, u32[]{:S(2)}) async-start(bf16[16,256,64]{1,2,0:T(8,128)(2,1)} %copy.28), calls=%async_computation.1 | async-start | bytes 1048576 | tf_op jit(solution)/shard_map/all_to_all | solution.py:95
  116.7 17.3 %copy-start.1 = (f32[1024]{0:T(1024)S(1)}, f32[1024]{0:T(1024)}, u32[]{:S(2)}) copy-start(f32[1024]{0:T(1024)} %param.11) | copy-start | bytes 12292
  134.0 2.3 %copy-start.2 = (f32[1024]{0:T(1024)S(1)}, f32[1024]{0:T(1024)}, u32[]{:S(2)}) copy-start(f32[1024]{0:T(1024)} %param.13) | copy-start | bytes 12292
  134.0 2.3 %copy-start.3 = (f32[1024]{0:T(1024)S(1)}, f32[1024]{0:T(1024)}, u32[]{:S(2)}) copy-start(f32[1024]{0:T(1024)} %param.12) | copy-start | bytes 12292

commit v6 on v4

--- a/solution.py
+++ b/solution.py
@@ -19,12 +19,16 @@
     return (x >= b1).astype(jnp.int32) + (x >= b2).astype(jnp.int32) + (x >= b3).astype(jnp.int32)
 
 
-def attn_kernel(lo_ref, hi_ref, bnd_ref, q_ref, kv_ref, o_ref):
+def attn_kernel(cnt_ref, q_ref, kv_ref, o_ref):
     i = pl.program_id(0)
-    b1, b2, b3 = bnd_ref[0], bnd_ref[1], bnd_ref[2]
+    b1, b2, b3 = cnt_ref[1], cnt_ref[2], cnt_ref[3]
     q0 = i * BQ
+    first = seg_of(q0, b1, b2, b3)
+    last = seg_of(q0 + BQ - 1, b1, b2, b3)
+    lo = cnt_ref[first] // BK
+    hi = (cnt_ref[last + 1] + BK - 1) // BK
     scale = 1.0 / math.sqrt(HEAD)
-    q = q_ref[0, :, 2 * HEAD:] * jnp.asarray(scale, jnp.bfloat16)
+    q = q_ref[0, :, 2 * HEAD:3 * HEAD] * jnp.asarray(scale, jnp.bfloat16)
     rows = q0 + lax.broadcasted_iota(jnp.int32, (BQ, 1), 0)
     sq = seg_of(rows, b1, b2, b3)
 
@@ -45,52 +49,46 @@
     m0 = jnp.full((BQ, 1), -jnp.inf, jnp.float32)
     l0 = jnp.zeros((BQ, 1), jnp.float32)
     acc0 = jnp.zeros((BQ, 2 * HEAD), jnp.float32)
-    _, l, acc = lax.fori_loop(lo_ref[i], hi_ref[i], body, (m0, l0, acc0))
+    _, l, acc = lax.fori_loop(lo, hi, body, (m0, l0, acc0))
     out = pltpu.roll(acc / l, HEAD, 1)
     o_ref[...] = out[:, :HEAD].astype(o_ref.dtype)
 
 
 def attention(mine, counts):
-    nk = mine.shape[0]
+    nk, _, feat = mine.shape
     rows = nk * BK
     nq = rows // BQ
-    b1, b2, b3 = counts[1], counts[2], counts[3]
-    bounds = jnp.concatenate([jnp.zeros((1,), jnp.int32), counts[1:], jnp.full((1,), rows, jnp.int32)])
-    starts = jnp.arange(nq, dtype=jnp.int32) * BQ
-    first = seg_of(starts, b1, b2, b3)
-    last = seg_of(starts + BQ - 1, b1, b2, b3)
-    lo = bounds[first] // BK
-    hi = (bounds[last + 1] + BK - 1) // BK
     grid_spec = pltpu.PrefetchScalarGridSpec(
-        num_scalar_prefetch=3,
+        num_scalar_prefetch=1,
         grid=(nq,),
         in_specs=[
-            pl.BlockSpec((1, BQ, 3 * HEAD), lambda i, lo, hi, bnd: (i, 0, 0)),
-            pl.BlockSpec((nk, BK, 3 * HEAD), lambda i, lo, hi, bnd: (0, 0, 0)),
+            pl.BlockSpec((1, BQ, feat), lambda i, cnt: (i, 0, 0)),
+            pl.BlockSpec((nk, BK, feat), lambda i, cnt: (0, 0, 0)),
         ],
-        out_specs=pl.BlockSpec((BQ, HEAD), lambda i, lo, hi, bnd: (i, 0)),
+        out_specs=pl.BlockSpec((BQ, HEAD), lambda i, cnt: (i, 0)),
     )
     return pl.pallas_call(
         attn_kernel,
         grid_spec=grid_spec,
         out_shape=jax.ShapeDtypeStruct((rows, HEAD), jnp.bfloat16),
         interpret=INTERPRET,
-    )(lo, hi, counts[1:], mine.reshape(nq, BQ, 3 * HEAD), mine)
+    )(counts, mine.reshape(nq, BQ, feat), mine)
 
 
 def shards(tokens, segments, qkv_weight, out_weight, out_bias, ln_gain, ln_bias):
     tok_rows, width = tokens.shape
     groups = lax.axis_size("seq")
-    levels = jnp.arange(SEGS + 1, dtype=jnp.int32)
-    local = jnp.sum((segments[None, :] < levels[:, None]).astype(jnp.int32), axis=1)
-    counts = lax.psum(local, "seq")
     proj = jnp.dot(tokens, qkv_weight, preferred_element_type=jnp.float32).astype(jnp.bfloat16)
     grouped = proj.reshape(tok_rows, HEADS, 3, HEAD)
-    payload = jnp.concatenate([grouped[:, :, 1], grouped[:, :, 2], grouped[:, :, 0]], axis=-1)
+    seg_col = jnp.broadcast_to(segments.astype(jnp.bfloat16)[:, None, None], (tok_rows, HEADS, 1))
+    payload = jnp.concatenate([grouped[:, :, 1], grouped[:, :, 2], grouped[:, :, 0], seg_col], axis=-1)
     payload = jnp.moveaxis(payload, 1, 0)
     mine = lax.all_to_all(payload, "seq", split_axis=0, concat_axis=0, tiled=True)
     kv_cache = mine[:, :, :2 * HEAD].reshape(groups * tok_rows, 2 * HEAD)
-    context = attention(mine.reshape(groups * tok_rows // BK, BK, 3 * HEAD), counts)
+    all_seg = mine[:, :, 3 * HEAD].astype(jnp.int32).reshape(groups * tok_rows)
+    levels = jnp.arange(SEGS + 1, dtype=jnp.int32)
+    counts = jnp.sum((all_seg[None, :] < levels[:, None]).astype(jnp.int32), axis=1)
+    context = attention(mine.reshape(groups * tok_rows // BK, BK, 3 * HEAD + 1), counts)
     ctx = lax.all_to_all(context.reshape(groups, tok_rows, HEAD), "seq", split_axis=0, concat_axis=0, tiled=True)
     mixed = (
         jnp.einsum("htc,hcd->td", ctx, out_weight.reshape(HEADS, HEAD, width), preferred_element_type=jnp.float32)

time: 136 us -> 127 us (0.934)
  starting transfers between devices: 17 us -> 4.14 us
  blocking collectives: 42.9 us -> 51.2 us
  other arithmetic: 5.82 us -> 2.92 us
  local copies, waits for them, and re-layouts: 14.7 us -> 12.7 us
    all_to_all x0 -> x1, blocking collectives: none -> 51.2 us  [shards(): lax.all_to_all(payload, 'seq', split_axis=0, concat_axis=0, tiled=True)]
    psum x1 -> x0, blocking collectives: 42.9 us -> none  [shards(): counts = lax.psum(local, 'seq')]
    all_to_all x1 -> x0, starting transfers between devices: 10.1 us -> none  [shards(): lax.all_to_all(payload, 'seq', split_axis=0, concat_axis=0, tiled=True)]
    select_n x3 -> x0, other arithmetic: 3.04 us -> none  [the longest x2 2.46 us: attention(): lo = bounds[first] // BK]
    all_to_all x1, starting transfers between devices: 6.88 us -> 4.14 us  [shards(): lax.all_to_all(context.reshape(groups, tok_rows, HEAD), 'seq', split_axis...]
  transfers between devices with their start and end apart: 2 -> 1, of which waited for: 1 -> 1; matrix products, arithmetic and copies ran while one was open for 6% -> 1% of each run, Pallas kernels for 0% -> 0%
where the time goes in v6:
time: 127 us
  blocking collectives  51.2 us (40%)
  Pallas kernels  31.2 us (25%)
  waiting for transfers between devices  16 us (13%)
  local copies, waits for them, and re-layouts  12.7 us (10%)
  matrix products  7.98 us (6%)
  starting transfers between devices  4.14 us (3%)
  other arithmetic  2.92 us (2%)
    all_to_all x1, blocking collectives, shards(): lax.all_to_all(payload, 'seq', split_axis=0, concat_axis=0, tiled=True)  51.2 us
    pallas_call x1, Pallas kernels, attention(): pl.pallas_call(attn_kernel, grid_spec=grid_spec, out_shape=jax.ShapeDtype...  31.2 us
    all_to_all x1, waiting for transfers between devices, shards(): lax.all_to_all(context.reshape(groups, tok_rows, HEAD), 'seq', split_axis...  16 us
    dot_general x1, matrix products, shards(): jnp.dot(tokens, qkv_weight, preferred_element_type=jnp.float32)  5.94 us
    all_to_all x1, starting transfers between devices, shards(): lax.all_to_all(context.reshape(groups, tok_rows, HEAD), 'seq', split_axis...  4.14 us
    all_to_all x1, local copies, waits for them, and re-layouts, shards(): lax.all_to_all(payload, 'seq', split_axis=0, concat_axis=0, tiled=True)  3.72 us
    convert_element_type x1, local copies, waits for them, and re-layouts, shards(): jnp.dot(tokens, qkv_weight, preferred_element_type=jnp.float32)  2.59 us
  transfers between devices with their start and end apart: 1, of which 1 were waited for; matrix products, arithmetic and copies ran while one was open for 1% of the time, Pallas kernels for 0%

profile of v6, /device:TPU:1, one launch (start us, length us, event | category | flops | bytes accessed | tf_op | source)
XLA Modules:
  0.0 126.8 jit_solution(120843291675745327)
XLA Ops:
  0.6 0.0 copy-start
  0.6 0.8 convert_element_type.26
  1.5 5.9 %convolution_convert_fusion = bf16[256,3072]{1,0:T(8,128)(2,1)} fusion(bf16[256,1024]{1,0:T(8,128)(2,1)} %param.7, bf16[1024,3072]{1,0:T(8,128)(2,1)} %param.9), kind=kOutput, calls=%fused_computation | convolution fusion | flops 1611399168 | bytes 8388608 | tf_op jit(solution)/shard_map/dot_general | solution.py:81
  7.4 2.6 %copy.24 = bf16[256,3072]{0,1:T(8,128)(2,1)} copy(bf16[256,3072]{1,0:T(8,128)(2,1)} %convolution_convert_fusion) | data formatting | bytes 3145728 | tf_op jit(solution)/shard_map/convert_element_type | solution.py:81
  10.0 1.5 %slice_bitcast_fusion.2 = (bf16[256,16,64]{0,2,1:T(8,128)(2,1)S(1)}, bf16[256,16,64]{0,2,1:T(8,128)(2,1)S(1)}, bf16[256,16,64]{0,2,1:T(8,128)(2,1)S(1)}) fusion(bf16[256,16,3,64]{0,3,2,1:T(8,128)(2,1)} %bitcast.31), kind=kLoop, calls=%fused_computation.9 | loop fusion | bytes 3145728 | tf_op jit(solution)/shard_map/squeeze | solution.py:84
  11.5 0.1 maximum_bitcast_fusion
  11.6 51.2 %all_to_all.10 = bf16[16,256,193]{1,2,0:T(8,128)(2,1)S(1)} all-to-all(bf16[16,256,193]{1,2,0:T(8,128)(2,1)S(1)} %maximum_bitcast_fusion), channel_id=1, replica_groups=mesh['seq'=16,'rep'=16] {'seq'}, dimensions={0} | all-to-all | bytes 3162112 | tf_op jit(solution)/shard_map/all_to_all | solution.py:86
  62.8 0.0 copy-start.1
  62.8 1.2 copy-done.1
  64.0 0.7 convert_reduce_fusion.cnt_ref
  64.6 3.7 %copy.27 = bf16[16,256,193]{2,1,0:T(8,128)(2,1)} copy(bf16[16,256,193]{1,2,0:T(8,128)(2,1)} %copy-done.1) | data formatting | bytes 3162112 | tf_op jit(solution)/shard_map/all_to_all | solution.py:86
  68.3 31.2 %shard_map.86 = bf16[4096,64]{1,0:T(8,128)(2,1)} custom-call(s32[5]{0:T(128)} %convert_reduce_fusion.cnt_ref, bf16[8,512,193]{2,1,0:T(8,128)(2,1)} %bitcast.29, bf16[8,512,193]{2,1,0:T(8,128)(2,1)} %bitcast.30), custom_call_target="tpu_custom_call" | custom-call | tf_op jit(solution)/shard_map/pallas_call | solution.py:70
  99.5 0.0 slice-start
  99.5 2.4 %copy.28 = bf16[16,256,64]{1,2,0:T(8,128)(2,1)} copy(bf16[16,256,64]{2,1,0:T(8,128)(2,1)} %bitcast.32) | data formatting | bytes 1048576 | tf_op jit(solution)/shard_map/reshape | solution.py:92
  101.9 4.1 %all-to-all-start.1 = ((bf16[16,256,64]{1,2,0:T(8,128)(2,1)}), bf16[16,256,64]{1,2,0:T(8,128)(2,1)}, u32[]{:S(2)}, u32[]{:S(2)}) async-start(bf16[16,256,64]{1,2,0:T(8,128)(2,1)} %copy.28), calls=%async_computation.1 | async-start | bytes 1048576 | tf_op jit(solution)/shard_map/all_to_all | solution.py:92
  106.1 0.0 copy-start.2
  106.1 0.0 slice-done
  106.1 1.3 %copy.29 = bf16[16,256,128]{2,1,0:T(8,128)(2,1)} copy(bf16[16,256,128]{1,2,0:T(8,128)(2,1)S(1)} %slice-done) | data formatting | bytes 2097152 | tf_op jit(solution)/shard_map/slice | solution.py:87
  107.4 16.0 %all-to-all-done.1 = bf16[16,256,64]{1,2,0:T(8,128)(2,1)} async-done(((bf16[16,256,64]{1,2,0:T(8,128)(2,1)}), bf16[16,256,64]{1,2,0:T(8,128)(2,1)}, u32[]{:S(2)}, u32[]{:S(2)}) %all-to-all-start.1) | async-done | bytes 524320 | tf_op jit(solution)/shard_map/all_to_all | solution.py:92
  123.4 0.0 copy-done
  123.4 0.0 copy-done.2
  123.4 0.0 copy-start.3
  123.4 0.0 copy-start.4
  123.5 2.0 %fusion.2 = (f32[256]{0:T(256)S(1)}, f32[256,1024]{1,0:T(8,128)S(1)}) fusion(bf16[256,1024]{1,0:T(8,128)(2,1)} %param.7, f32[1024]{0:T(1024)S(1)} %copy-done.2, bf16[16,256,64]{1,2,0:T(8,128)(2,1)} %all-to-all-done.1, bf16[16,64,1024]{2,1,0:T(8,128)(2,1)S(1)} %bitcast.28), kind=kOutput, calls=%fused_computation.15 | convolution fusion | flops 537919232 | bytes 4199424 | tf_op jit(solution)/shard_map/htc,hcd->td/dot_general | solution.py:94
  125.5 0.3 multiply_reduce_fusion
  125.8 0.0 copy-done.3
  125.8 0.0 copy-done.4
  125.8 1.0 add_convert_fusion
  (4 shorter events, 0.0 us)
Async XLA Ops:
  0.6 122.8 %copy-start = (bf16[1024,1024]{1,0:T(8,128)(2,1)S(1)}, bf16[1024,1024]{1,0:T(8,128)(2,1)}, u32[]{:S(2)}) copy-start(bf16[1024,1024]{1,0:T(8,128)(2,1)} %param.10) | copy-start | bytes 6291460
  62.8 1.2 copy-start.1
  99.5 6.6 %slice-start = ((bf16[16,256,193]{1,2,0:T(8,128)(2,1)}), bf16[16,256,128]{1,2,0:T(8,128)(2,1)S(1)}, s32[]{:S(2)}) async-start(bf16[16,256,193]{1,2,0:T(8,128)(2,1)} %copy-done.1), calls=%async_computation.2 | async-start | bytes 2097152 | tf_op jit(solution)/shard_map/slice | solution.py:87
  101.9 21.5 %all-to-all-start.1 = ((bf16[16,256,64]{1,2,0:T(8,128)(2,1)}), bf16[16,256,64]{1,2,0:T(8,128)(2,1)}, u32[]{:S(2)}, u32[]{:S(2)}) async-start(bf16[16,256,64]{1,2,0:T(8,128)(2,1)} %copy.28), calls=%async_computation.1 | async-start | bytes 1048576 | tf_op jit(solution)/shard_map/all_to_all | solution.py:92
  106.1 17.4 %copy-start.2 = (f32[1024]{0:T(1024)S(1)}, f32[1024]{0:T(1024)}, u32[]{:S(2)}) copy-start(f32[1024]{0:T(1024)} %param.11) | copy-start | bytes 12292
  123.4 2.3 %copy-start.3 = (f32[1024]{0:T(1024)S(1)}, f32[1024]{0:T(1024)}, u32[]{:S(2)}) copy-start(f32[1024]{0:T(1024)} %param.13) | copy-start | bytes 12292
  123.4 2.3 %copy-start.4 = (f32[1024]{0:T(1024)S(1)}, f32[1024]{0:T(1024)}, u32[]{:S(2)}) copy-start(f32[1024]{0:T(1024)} %param.12) | copy-start | bytes 12292

commit v7 on v6

--- a/solution.py
+++ b/solution.py
@@ -25,19 +25,25 @@
     q0 = i * BQ
     first = seg_of(q0, b1, b2, b3)
     last = seg_of(q0 + BQ - 1, b1, b2, b3)
-    lo = cnt_ref[first] // BK
-    hi = (cnt_ref[last + 1] + BK - 1) // BK
+    start = cnt_ref[first]
+    end = cnt_ref[last + 1]
+    lo = start // BK
+    hi = (end + BK - 1) // BK
+    inside = first == last
+    mid_lo = jnp.where(inside, (start + BK - 1) // BK, hi)
+    mid_hi = jnp.where(inside, jnp.maximum(end // BK, mid_lo), hi)
     scale = 1.0 / math.sqrt(HEAD)
     q = q_ref[0, :, 2 * HEAD:3 * HEAD] * jnp.asarray(scale, jnp.bfloat16)
     rows = q0 + lax.broadcasted_iota(jnp.int32, (BQ, 1), 0)
     sq = seg_of(rows, b1, b2, b3)
 
-    def body(j, carry):
+    def tile(j, carry, masked):
         m, l, acc = carry
         kv = kv_ref[j, :, :2 * HEAD]
         s = lax.dot_general(q, kv[:, :HEAD], (((1,), (1,)), ((), ())), preferred_element_type=jnp.float32)
-        cols = j * BK + lax.broadcasted_iota(jnp.int32, (1, BK), 1)
-        s = jnp.where(sq == seg_of(cols, b1, b2, b3), s, -jnp.inf)
+        if masked:
+            cols = j * BK + lax.broadcasted_iota(jnp.int32, (1, BK), 1)
+            s = jnp.where(sq == seg_of(cols, b1, b2, b3), s, -jnp.inf)
         m_new = jnp.maximum(m, jnp.max(s, axis=1, keepdims=True))
         m_safe = jnp.where(m_new == -jnp.inf, 0.0, m_new)
         p = jnp.exp(s - m_safe)
@@ -46,10 +52,18 @@
         acc = alpha * acc + jnp.dot(p.astype(jnp.bfloat16), kv, preferred_element_type=jnp.float32)
         return m_new, l, acc
 
+    def masked_tile(j, carry):
+        return tile(j, carry, True)
+
+    def plain_tile(j, carry):
+        return tile(j, carry, False)
+
     m0 = jnp.full((BQ, 1), -jnp.inf, jnp.float32)
     l0 = jnp.zeros((BQ, 1), jnp.float32)
     acc0 = jnp.zeros((BQ, 2 * HEAD), jnp.float32)
-    _, l, acc = lax.fori_loop(lo, hi, body, (m0, l0, acc0))
+    carry = lax.fori_loop(lo, mid_lo, masked_tile, (m0, l0, acc0))
+    carry = lax.fori_loop(mid_lo, mid_hi, plain_tile, carry)
+    _, l, acc = lax.fori_loop(mid_hi, hi, masked_tile, carry)
     out = pltpu.roll(acc / l, HEAD, 1)
     o_ref[...] = out[:, :HEAD].astype(o_ref.dtype)
 

time: 127 us -> 132 us (1.039)
  the two profiles are of different devices: /device:TPU:1 before, /device:TPU:7 now
where the time goes in v7:
time: 132 us; the launch traced here: 131 us
  blocking collectives  50.3 us (38%)
  Pallas kernels  36.3 us (27%)
  waiting for transfers between devices  16 us (12%)
  local copies, waits for them, and re-layouts  12.7 us (10%)
  matrix products  7.98 us (6%)
  starting transfers between devices  4.14 us (3%)
  other arithmetic  2.92 us (2%)
    all_to_all x1, blocking collectives, shards(): lax.all_to_all(payload, 'seq', split_axis=0, concat_axis=0, tiled=True)  50.3 us
    pallas_call x1, Pallas kernels, attention(): pl.pallas_call(attn_kernel, grid_spec=grid_spec, out_shape=jax.ShapeDtype...  36.3 us
    all_to_all x1, waiting for transfers between devices, shards(): lax.all_to_all(context.reshape(groups, tok_rows, HEAD), 'seq', split_axis...  16 us
    dot_general x1, matrix products, shards(): jnp.dot(tokens, qkv_weight, preferred_element_type=jnp.float32)  5.94 us
    all_to_all x1, starting transfers between devices, shards(): lax.all_to_all(context.reshape(groups, tok_rows, HEAD), 'seq', split_axis...  4.14 us
    all_to_all x1, local copies, waits for them, and re-layouts, shards(): lax.all_to_all(payload, 'seq', split_axis=0, concat_axis=0, tiled=True)  3.72 us
  transfers between devices with their start and end apart: 1, of which 1 were waited for; matrix products, arithmetic and copies ran while one was open for 1% of the time, Pallas kernels for 0%

profile of v7, /device:TPU:7, one launch (start us, length us, event | category | flops | bytes accessed | tf_op | source)
XLA Modules:
  0.0 131.1 jit_solution(6545779594042335950)
XLA Ops:
  0.6 0.0 copy-start
  0.6 0.8 convert_element_type.26
  1.5 5.9 %convolution_convert_fusion = bf16[256,3072]{1,0:T(8,128)(2,1)} fusion(bf16[256,1024]{1,0:T(8,128)(2,1)} %param.7, bf16[1024,3072]{1,0:T(8,128)(2,1)} %param.9), kind=kOutput, calls=%fused_computation | convolution fusion | flops 1611399168 | bytes 8388608 | tf_op jit(solution)/shard_map/dot_general | solution.py:95
  7.4 2.6 %copy.24 = bf16[256,3072]{0,1:T(8,128)(2,1)} copy(bf16[256,3072]{1,0:T(8,128)(2,1)} %convolution_convert_fusion) | data formatting | bytes 3145728 | tf_op jit(solution)/shard_map/convert_element_type | solution.py:95
  10.0 1.5 %slice_bitcast_fusion.2 = (bf16[256,16,64]{0,2,1:T(8,128)(2,1)S(1)}, bf16[256,16,64]{0,2,1:T(8,128)(2,1)S(1)}, bf16[256,16,64]{0,2,1:T(8,128)(2,1)S(1)}) fusion(bf16[256,16,3,64]{0,3,2,1:T(8,128)(2,1)} %bitcast.31), kind=kLoop, calls=%fused_computation.9 | loop fusion | bytes 3145728 | tf_op jit(solution)/shard_map/squeeze | solution.py:98
  11.5 0.1 maximum_bitcast_fusion
  11.6 50.3 %all_to_all.10 = bf16[16,256,193]{1,2,0:T(8,128)(2,1)S(1)} all-to-all(bf16[16,256,193]{1,2,0:T(8,128)(2,1)S(1)} %maximum_bitcast_fusion), channel_id=1, replica_groups=mesh['seq'=16,'rep'=16] {'seq'}, dimensions={0} | all-to-all | bytes 3162112 | tf_op jit(solution)/shard_map/all_to_all | solution.py:100
  62.0 0.0 copy-start.1
  62.0 1.2 copy-done.1
  63.1 0.7 convert_reduce_fusion.cnt_ref
  63.8 3.7 %copy.27 = bf16[16,256,193]{2,1,0:T(8,128)(2,1)} copy(bf16[16,256,193]{1,2,0:T(8,128)(2,1)} %copy-done.1) | data formatting | bytes 3162112 | tf_op jit(solution)/shard_map/all_to_all | solution.py:100
  67.5 36.3 %shard_map.86 = bf16[4096,64]{1,0:T(8,128)(2,1)} custom-call(s32[5]{0:T(128)} %convert_reduce_fusion.cnt_ref, bf16[8,512,193]{2,1,0:T(8,128)(2,1)} %bitcast.29, bf16[8,512,193]{2,1,0:T(8,128)(2,1)} %bitcast.30), custom_call_target="tpu_custom_call" | custom-call | tf_op jit(solution)/shard_map/pallas_call | solution.py:84
  103.8 0.0 slice-start
  103.8 2.4 %copy.28 = bf16[16,256,64]{1,2,0:T(8,128)(2,1)} copy(bf16[16,256,64]{2,1,0:T(8,128)(2,1)} %bitcast.32) | data formatting | bytes 1048576 | tf_op jit(solution)/shard_map/reshape | solution.py:106
  106.2 4.1 %all-to-all-start.1 = ((bf16[16,256,64]{1,2,0:T(8,128)(2,1)}), bf16[16,256,64]{1,2,0:T(8,128)(2,1)}, u32[]{:S(2)}, u32[]{:S(2)}) async-start(bf16[16,256,64]{1,2,0:T(8,128)(2,1)} %copy.28), calls=%async_computation.1 | async-start | bytes 1048576 | tf_op jit(solution)/shard_map/all_to_all | solution.py:106
  110.4 0.0 copy-start.2
  110.4 0.0 slice-done
  110.4 1.3 copy.29
  111.7 16.0 %all-to-all-done.1 = bf16[16,256,64]{1,2,0:T(8,128)(2,1)} async-done(((bf16[16,256,64]{1,2,0:T(8,128)(2,1)}), bf16[16,256,64]{1,2,0:T(8,128)(2,1)}, u32[]{:S(2)}, u32[]{:S(2)}) %all-to-all-start.1) | async-done | bytes 524320 | tf_op jit(solution)/shard_map/all_to_all | solution.py:106
  127.7 0.0 copy-done
  127.7 0.0 copy-done.2
  127.7 0.0 copy-start.3
  127.7 0.0 copy-start.4
  127.7 2.0 %fusion.2 = (f32[256]{0:T(256)S(1)}, f32[256,1024]{1,0:T(8,128)S(1)}) fusion(bf16[256,1024]{1,0:T(8,128)(2,1)} %param.7, f32[1024]{0:T(1024)S(1)} %copy-done.2, bf16[16,256,64]{1,2,0:T(8,128)(2,1)} %all-to-all-done.1, bf16[16,64,1024]{2,1,0:T(8,128)(2,1)S(1)} %bitcast.28), kind=kOutput, calls=%fused_computation.15 | convolution fusion | flops 537919232 | bytes 4199424 | tf_op jit(solution)/shard_map/htc,hcd->td/dot_general | solution.py:108
  129.8 0.3 multiply_reduce_fusion
  130.1 0.0 copy-done.3
  130.1 0.0 copy-done.4
  130.1 1.0 add_convert_fusion
  (4 shorter events, 0.0 us)
Async XLA Ops:
  0.6 127.1 %copy-start = (bf16[1024,1024]{1,0:T(8,128)(2,1)S(1)}, bf16[1024,1024]{1,0:T(8,128)(2,1)}, u32[]{:S(2)}) copy-start(bf16[1024,1024]{1,0:T(8,128)(2,1)} %param.10) | copy-start | bytes 6291460
  62.0 1.2 copy-start.1
  103.8 6.6 %slice-start = ((bf16[16,256,193]{1,2,0:T(8,128)(2,1)}), bf16[16,256,128]{1,2,0:T(8,128)(2,1)S(1)}, s32[]{:S(2)}) async-start(bf16[16,256,193]{1,2,0:T(8,128)(2,1)} %copy-done.1), calls=%async_computation.2 | async-start | bytes 2097152 | tf_op jit(solution)/shard_map/slice | solution.py:101
  106.2 21.5 %all-to-all-start.1 = ((bf16[16,256,64]{1,2,0:T(8,128)(2,1)}), bf16[16,256,64]{1,2,0:T(8,128)(2,1)}, u32[]{:S(2)}, u32[]{:S(2)}) async-start(bf16[16,256,64]{1,2,0:T(8,128)(2,1)} %copy.28), calls=%async_computation.1 | async-start | bytes 1048576 | tf_op jit(solution)/shard_map/all_to_all | solution.py:106
  110.4 17.4 %copy-start.2 = (f32[1024]{0:T(1024)S(1)}, f32[1024]{0:T(1024)}, u32[]{:S(2)}) copy-start(f32[1024]{0:T(1024)} %param.11) | copy-start | bytes 12292
  127.7 2.3 %copy-start.3 = (f32[1024]{0:T(1024)S(1)}, f32[1024]{0:T(1024)}, u32[]{:S(2)}) copy-start(f32[1024]{0:T(1024)} %param.13) | copy-start | bytes 12292
  127.7 2.3 %copy-start.4 = (f32[1024]{0:T(1024)S(1)}, f32[1024]{0:T(1024)}, u32[]{:S(2)}) copy-start(f32[1024]{0:T(1024)} %param.12) | copy-start | bytes 12292

commit v8 on v7

--- a/solution.py
+++ b/solution.py
@@ -11,7 +11,7 @@
 HEAD = 64
 SEGS = 4
 BQ = 512
-BK = 512
+BK = 256
 INTERPRET = False
 
 

time: 132 us -> 141 us (1.068)
  the two profiles are of different devices: /device:TPU:7 before, /device:TPU:5 now
where the time goes in v8:
time: 141 us; the launch traced here: 140 us
  blocking collectives  50.3 us (36%)
  Pallas kernels  47.2 us (33%)
  waiting for transfers between devices  15 us (11%)
  local copies, waits for them, and re-layouts  13.7 us (10%)
  matrix products  6.75 us (5%)
  starting transfers between devices  3.48 us (2%)
  other arithmetic  2.92 us (2%)
    all_to_all x1, blocking collectives, shards(): lax.all_to_all(payload, 'seq', split_axis=0, concat_axis=0, tiled=True)  50.3 us
    pallas_call x1, Pallas kernels, attention(): pl.pallas_call(attn_kernel, grid_spec=grid_spec, out_shape=jax.ShapeDtype...  47.2 us
    all_to_all x1, waiting for transfers between devices, shards(): lax.all_to_all(context.reshape(groups, tok_rows, HEAD), 'seq', split_axis...  15 us
    dot_general x1, matrix products, shards(): jnp.dot(tokens, qkv_weight, preferred_element_type=jnp.float32)  5.92 us
    all_to_all x1, local copies, waits for them, and re-layouts, shards(): lax.all_to_all(payload, 'seq', split_axis=0, concat_axis=0, tiled=True)  3.72 us
    all_to_all x1, starting transfers between devices, shards(): lax.all_to_all(context.reshape(groups, tok_rows, HEAD), 'seq', split_axis...  3.48 us
  transfers between devices with their start and end apart: 1, of which 1 were waited for; matrix products, arithmetic and copies ran while one was open for 2% of the time, Pallas kernels for 0%

profile of v8, /device:TPU:5, one launch (start us, length us, event | category | flops | bytes accessed | tf_op | source)
XLA Modules:
  0.0 140.1 jit_solution(13307588548062787022)
XLA Ops:
  0.6 0.0 copy-start
  0.6 0.8 convert_element_type.26
  1.5 5.9 %convolution_convert_fusion = bf16[256,3072]{1,0:T(8,128)(2,1)} fusion(bf16[256,1024]{1,0:T(8,128)(2,1)} %param.7, bf16[1024,3072]{1,0:T(8,128)(2,1)} %param.9), kind=kOutput, calls=%fused_computation | convolution fusion | flops 1611399168 | bytes 8388608 | tf_op jit(solution)/shard_map/dot_general | solution.py:95
  7.4 2.6 %copy.28 = bf16[256,3072]{0,1:T(8,128)(2,1)} copy(bf16[256,3072]{1,0:T(8,128)(2,1)} %convolution_convert_fusion) | data formatting | bytes 3145728 | tf_op jit(solution)/shard_map/convert_element_type | solution.py:95
  10.0 1.5 %slice_bitcast_fusion.2 = (bf16[256,16,64]{0,2,1:T(8,128)(2,1)S(1)}, bf16[256,16,64]{0,2,1:T(8,128)(2,1)S(1)}, bf16[256,16,64]{0,2,1:T(8,128)(2,1)S(1)}) fusion(bf16[256,16,3,64]{0,3,2,1:T(8,128)(2,1)} %bitcast.30), kind=kLoop, calls=%fused_computation.9 | loop fusion | bytes 3145728 | tf_op jit(solution)/shard_map/squeeze | solution.py:98
  11.5 0.1 maximum_bitcast_fusion
  11.6 50.3 %all_to_all.10 = bf16[16,256,193]{1,2,0:T(8,128)(2,1)S(1)} all-to-all(bf16[16,256,193]{1,2,0:T(8,128)(2,1)S(1)} %maximum_bitcast_fusion), channel_id=1, replica_groups=mesh['seq'=16,'rep'=16] {'seq'}, dimensions={0} | all-to-all | bytes 3162112 | tf_op jit(solution)/shard_map/all_to_all | solution.py:100
  61.9 0.0 copy-start.1
  61.9 1.2 copy-done.1
  63.1 0.7 convert_reduce_fusion.cnt_ref
  63.8 3.7 %copy.31.kv_ref = bf16[16,256,193]{2,1,0:T(8,128)(2,1)} copy(bf16[16,256,193]{1,2,0:T(8,128)(2,1)} %copy-done.1) | data formatting | bytes 3162112 | tf_op jit(solution)/shard_map/all_to_all | solution.py:100
  67.5 47.2 %shard_map.86 = bf16[4096,64]{1,0:T(8,128)(2,1)} custom-call(s32[5]{0:T(128)} %convert_reduce_fusion.cnt_ref, bf16[8,512,193]{2,1,0:T(8,128)(2,1)} %bitcast.29, bf16[16,256,193]{2,1,0:T(8,128)(2,1)} %copy.31.kv_ref), custom_call_target="tpu_custom_call" | custom-call | tf_op jit(solution)/shard_map/pallas_call | solution.py:84
  114.7 0.0 copy-start.2
  114.7 0.0 copy-start.3
  114.7 2.4 %copy.33 = bf16[16,256,64]{1,2,0:T(8,128)(2,1)} copy(bf16[16,256,64]{2,1,0:T(8,128)(2,1)} %bitcast.31) | data formatting | bytes 1048576 | tf_op jit(solution)/shard_map/reshape | solution.py:106
  117.1 3.5 %all-to-all-start.1 = ((bf16[16,256,64]{1,2,0:T(8,128)(2,1)}), bf16[16,256,64]{1,2,0:T(8,128)(2,1)S(1)}, u32[]{:S(2)}, u32[]{:S(2)}) async-start(bf16[16,256,64]{1,2,0:T(8,128)(2,1)} %copy.33), calls=%async_computation.1 | async-start | bytes 1048576 | tf_op jit(solution)/shard_map/all_to_all | solution.py:106
  120.6 2.3 %slice.24 = bf16[16,256,128]{2,1,0:T(8,128)(2,1)} slice(bf16[16,256,193]{2,1,0:T(8,128)(2,1)} %copy.31.kv_ref), slice={[0:16], [0:256], [0:128]} | slice | bytes 2097152 | tf_op jit(solution)/shard_map/slice | solution.py:101
  122.9 15.0 %all-to-all-done.1 = bf16[16,256,64]{1,2,0:T(8,128)(2,1)S(1)} async-done(((bf16[16,256,64]{1,2,0:T(8,128)(2,1)}), bf16[16,256,64]{1,2,0:T(8,128)(2,1)S(1)}, u32[]{:S(2)}, u32[]{:S(2)}) %all-to-all-start.1) | async-done | bytes 524320 | tf_op jit(solution)/shard_map/all_to_all | solution.py:106
  137.9 0.0 copy-done
  137.9 0.0 copy-done.2
  137.9 0.0 copy-done.3
  137.9 0.0 copy-start.4
  137.9 0.0 copy-start.5
  137.9 0.8 fusion.2
  138.8 0.3 multiply_reduce_fusion
  139.0 0.0 copy-done.4
  139.1 0.0 copy-done.5
  139.1 1.0 add_convert_fusion
  (4 shorter events, 0.0 us)
Async XLA Ops:
  0.6 137.3 %copy-start = (bf16[1024,1024]{1,0:T(8,128)(2,1)S(1)}, bf16[1024,1024]{1,0:T(8,128)(2,1)}, u32[]{:S(2)}) copy-start(bf16[1024,1024]{1,0:T(8,128)(2,1)} %param.10) | copy-start | bytes 6291460
  61.9 1.2 copy-start.1
  114.7 23.2 %copy-start.2 = (bf16[256,1024]{1,0:T(8,128)(2,1)S(1)}, bf16[256,1024]{1,0:T(8,128)(2,1)}, u32[]{:S(2)}) copy-start(bf16[256,1024]{1,0:T(8,128)(2,1)} %param.7) | copy-start | bytes 1572868
  114.7 23.2 %copy-start.3 = (f32[1024]{0:T(1024)S(1)}, f32[1024]{0:T(1024)}, u32[]{:S(2)}) copy-start(f32[1024]{0:T(1024)} %param.11) | copy-start | bytes 12292
  117.1 20.8 %all-to-all-start.1 = ((bf16[16,256,64]{1,2,0:T(8,128)(2,1)}), bf16[16,256,64]{1,2,0:T(8,128)(2,1)S(1)}, u32[]{:S(2)}, u32[]{:S(2)}) async-start(bf16[16,256,64]{1,2,0:T(8,128)(2,1)} %copy.33), calls=%async_computation.1 | async-start | bytes 1048576 | tf_op jit(solution)/shard_map/all_to_all | solution.py:106
  137.9 1.1 copy-start.4
  137.9 1.1 copy-start.5

commit v9 on v8

--- a/solution.py
+++ b/solution.py
@@ -11,7 +11,7 @@
 HEAD = 64
 SEGS = 4
 BQ = 512
-BK = 256
+BK = 1024
 INTERPRET = False
 
 

time: 141 us -> 129 us (0.915)
  the two profiles are of different devices: /device:TPU:5 before, /device:TPU:1 now
where the time goes in v9:
time: 129 us; the launch traced here: 128 us
  blocking collectives  51.2 us (40%)
  Pallas kernels  32.7 us (25%)
  waiting for transfers between devices  16 us (12%)
  local copies, waits for them, and re-layouts  12.7 us (10%)
  matrix products  7.98 us (6%)
  starting transfers between devices  4.14 us (3%)
  other arithmetic  2.92 us (2%)
    all_to_all x1, blocking collectives, shards(): lax.all_to_all(payload, 'seq', split_axis=0, concat_axis=0, tiled=True)  51.2 us
    pallas_call x1, Pallas kernels, attention(): pl.pallas_call(attn_kernel, grid_spec=grid_spec, out_shape=jax.ShapeDtype...  32.7 us
    all_to_all x1, waiting for transfers between devices, shards(): lax.all_to_all(context.reshape(groups, tok_rows, HEAD), 'seq', split_axis...  16 us
    dot_general x1, matrix products, shards(): jnp.dot(tokens, qkv_weight, preferred_element_type=jnp.float32)  5.94 us
    all_to_all x1, starting transfers between devices, shards(): lax.all_to_all(context.reshape(groups, tok_rows, HEAD), 'seq', split_axis...  4.14 us
    all_to_all x1, local copies, waits for them, and re-layouts, shards(): lax.all_to_all(payload, 'seq', split_axis=0, concat_axis=0, tiled=True)  3.72 us
    convert_element_type x1, local copies, waits for them, and re-layouts, shards(): jnp.dot(tokens, qkv_weight, preferred_element_type=jnp.float32)  2.59 us
  transfers between devices with their start and end apart: 1, of which 1 were waited for; matrix products, arithmetic and copies ran while one was open for 1% of the time, Pallas kernels for 0%

profile of v9, /device:TPU:1, one launch (start us, length us, event | category | flops | bytes accessed | tf_op | source)
XLA Modules:
  0.0 128.3 jit_solution(5635055903517115210)
XLA Ops:
  0.6 0.0 copy-start
  0.6 0.8 convert_element_type.26
  1.5 5.9 %convolution_convert_fusion = bf16[256,3072]{1,0:T(8,128)(2,1)} fusion(bf16[256,1024]{1,0:T(8,128)(2,1)} %param.7, bf16[1024,3072]{1,0:T(8,128)(2,1)} %param.9), kind=kOutput, calls=%fused_computation | convolution fusion | flops 1611399168 | bytes 8388608 | tf_op jit(solution)/shard_map/dot_general | solution.py:95
  7.4 2.6 %copy.26 = bf16[256,3072]{0,1:T(8,128)(2,1)} copy(bf16[256,3072]{1,0:T(8,128)(2,1)} %convolution_convert_fusion) | data formatting | bytes 3145728 | tf_op jit(solution)/shard_map/convert_element_type | solution.py:95
  10.0 1.5 %slice_bitcast_fusion.2 = (bf16[256,16,64]{0,2,1:T(8,128)(2,1)S(1)}, bf16[256,16,64]{0,2,1:T(8,128)(2,1)S(1)}, bf16[256,16,64]{0,2,1:T(8,128)(2,1)S(1)}) fusion(bf16[256,16,3,64]{0,3,2,1:T(8,128)(2,1)} %bitcast.32), kind=kLoop, calls=%fused_computation.9 | loop fusion | bytes 3145728 | tf_op jit(solution)/shard_map/squeeze | solution.py:98
  11.5 0.1 maximum_bitcast_fusion
  11.6 51.2 %all_to_all.10 = bf16[16,256,193]{1,2,0:T(8,128)(2,1)S(1)} all-to-all(bf16[16,256,193]{1,2,0:T(8,128)(2,1)S(1)} %maximum_bitcast_fusion), channel_id=1, replica_groups=mesh['seq'=16,'rep'=16] {'seq'}, dimensions={0} | all-to-all | bytes 3162112 | tf_op jit(solution)/shard_map/all_to_all | solution.py:100
  62.8 0.0 copy-start.1
  62.8 1.2 copy-done.1
  64.0 0.7 convert_reduce_fusion.cnt_ref
  64.6 3.7 %copy.29 = bf16[16,256,193]{2,1,0:T(8,128)(2,1)} copy(bf16[16,256,193]{1,2,0:T(8,128)(2,1)} %copy-done.1) | data formatting | bytes 3162112 | tf_op jit(solution)/shard_map/all_to_all | solution.py:100
  68.3 32.7 %shard_map.86 = bf16[4096,64]{1,0:T(8,128)(2,1)} custom-call(s32[5]{0:T(128)} %convert_reduce_fusion.cnt_ref, bf16[8,512,193]{2,1,0:T(8,128)(2,1)} %bitcast.30, bf16[4,1024,193]{2,1,0:T(8,128)(2,1)} %bitcast.31), custom_call_target="tpu_custom_call" | custom-call | tf_op jit(solution)/shard_map/pallas_call | solution.py:84
  101.0 0.0 slice-start
  101.0 2.4 %copy.31 = bf16[16,256,64]{1,2,0:T(8,128)(2,1)} copy(bf16[16,256,64]{2,1,0:T(8,128)(2,1)} %bitcast.33) | data formatting | bytes 1048576 | tf_op jit(solution)/shard_map/reshape | solution.py:106
  103.4 4.1 %all-to-all-start.1 = ((bf16[16,256,64]{1,2,0:T(8,128)(2,1)}), bf16[16,256,64]{1,2,0:T(8,128)(2,1)}, u32[]{:S(2)}, u32[]{:S(2)}) async-start(bf16[16,256,64]{1,2,0:T(8,128)(2,1)} %copy.31), calls=%async_computation.1 | async-start | bytes 1048576 | tf_op jit(solution)/shard_map/all_to_all | solution.py:106
  107.6 0.0 copy-start.2
  107.6 0.0 slice-done
  107.6 1.3 %copy.32 = bf16[16,256,128]{2,1,0:T(8,128)(2,1)} copy(bf16[16,256,128]{1,2,0:T(8,128)(2,1)S(1)} %slice-done) | data formatting | bytes 2097152 | tf_op jit(solution)/shard_map/slice | solution.py:101
  108.9 16.0 %all-to-all-done.1 = bf16[16,256,64]{1,2,0:T(8,128)(2,1)} async-done(((bf16[16,256,64]{1,2,0:T(8,128)(2,1)}), bf16[16,256,64]{1,2,0:T(8,128)(2,1)}, u32[]{:S(2)}, u32[]{:S(2)}) %all-to-all-start.1) | async-done | bytes 524320 | tf_op jit(solution)/shard_map/all_to_all | solution.py:106
  124.9 0.0 copy-done
  124.9 0.0 copy-done.2
  125.0 0.0 copy-start.3
  125.0 0.0 copy-start.4
  125.0 2.0 %fusion.2 = (f32[256]{0:T(256)S(1)}, f32[256,1024]{1,0:T(8,128)S(1)}) fusion(bf16[256,1024]{1,0:T(8,128)(2,1)} %param.7, f32[1024]{0:T(1024)S(1)} %copy-done.2, bf16[16,256,64]{1,2,0:T(8,128)(2,1)} %all-to-all-done.1, bf16[16,64,1024]{2,1,0:T(8,128)(2,1)S(1)} %bitcast.29), kind=kOutput, calls=%fused_computation.15 | convolution fusion | flops 537919232 | bytes 4199424 | tf_op jit(solution)/shard_map/htc,hcd->td/dot_general | solution.py:108
  127.0 0.3 multiply_reduce_fusion
  127.3 0.0 copy-done.3
  127.3 0.0 copy-done.4
  127.3 1.0 add_convert_fusion
  (4 shorter events, 0.0 us)
Async XLA Ops:
  0.6 124.3 %copy-start = (bf16[1024,1024]{1,0:T(8,128)(2,1)S(1)}, bf16[1024,1024]{1,0:T(8,128)(2,1)}, u32[]{:S(2)}) copy-start(bf16[1024,1024]{1,0:T(8,128)(2,1)} %param.10) | copy-start | bytes 6291460
  62.8 1.2 copy-start.1
  101.0 6.6 %slice-start = ((bf16[16,256,193]{1,2,0:T(8,128)(2,1)}), bf16[16,256,128]{1,2,0:T(8,128)(2,1)S(1)}, s32[]{:S(2)}) async-start(bf16[16,256,193]{1,2,0:T(8,128)(2,1)} %copy-done.1), calls=%async_computation.2 | async-start | bytes 2097152 | tf_op jit(solution)/shard_map/slice | solution.py:101
  103.4 21.5 %all-to-all-start.1 = ((bf16[16,256,64]{1,2,0:T(8,128)(2,1)}), bf16[16,256,64]{1,2,0:T(8,128)(2,1)}, u32[]{:S(2)}, u32[]{:S(2)}) async-start(bf16[16,256,64]{1,2,0:T(8,128)(2,1)} %copy.31), calls=%async_computation.1 | async-start | bytes 1048576 | tf_op jit(solution)/shard_map/all_to_all | solution.py:106
  107.6 17.4 %copy-start.2 = (f32[1024]{0:T(1024)S(1)}, f32[1024]{0:T(1024)}, u32[]{:S(2)}) copy-start(f32[1024]{0:T(1024)} %param.11) | copy-start | bytes 12292
  125.0 2.3 %copy-start.3 = (f32[1024]{0:T(1024)S(1)}, f32[1024]{0:T(1024)}, u32[]{:S(2)}) copy-start(f32[1024]{0:T(1024)} %param.13) | copy-start | bytes 12292
  125.0 2.3 %copy-start.4 = (f32[1024]{0:T(1024)S(1)}, f32[1024]{0:T(1024)}, u32[]{:S(2)}) copy-start(f32[1024]{0:T(1024)} %param.12) | copy-start | bytes 12292

commit v10 on v9

--- a/solution.py
+++ b/solution.py
@@ -92,12 +92,12 @@
 def shards(tokens, segments, qkv_weight, out_weight, out_bias, ln_gain, ln_bias):
     tok_rows, width = tokens.shape
     groups = lax.axis_size("seq")
-    proj = jnp.dot(tokens, qkv_weight, preferred_element_type=jnp.float32).astype(jnp.bfloat16)
-    grouped = proj.reshape(tok_rows, HEADS, 3, HEAD)
-    seg_col = jnp.broadcast_to(segments.astype(jnp.bfloat16)[:, None, None], (tok_rows, HEADS, 1))
-    payload = jnp.concatenate([grouped[:, :, 1], grouped[:, :, 2], grouped[:, :, 0], seg_col], axis=-1)
-    payload = jnp.moveaxis(payload, 1, 0)
-    mine = lax.all_to_all(payload, "seq", split_axis=0, concat_axis=0, tiled=True)
+    proj_t = jnp.einsum("td,dc->ct", tokens, qkv_weight, preferred_element_type=jnp.float32).astype(jnp.bfloat16)
+    grouped = proj_t.reshape(HEADS, 3, HEAD, tok_rows)
+    seg_row = jnp.broadcast_to(segments.astype(jnp.bfloat16)[None, None, :], (HEADS, 1, tok_rows))
+    payload = jnp.concatenate([grouped[:, 1], grouped[:, 2], grouped[:, 0], seg_row], axis=1)
+    mine_t = lax.all_to_all(payload, "seq", split_axis=0, concat_axis=0, tiled=True)
+    mine = jnp.swapaxes(mine_t, 1, 2)
     kv_cache = mine[:, :, :2 * HEAD].reshape(groups * tok_rows, 2 * HEAD)
     all_seg = mine[:, :, 3 * HEAD].astype(jnp.int32).reshape(groups * tok_rows)
     levels = jnp.arange(SEGS + 1, dtype=jnp.int32)

time: 129 us -> 123 us (0.953)
  local copies, waits for them, and re-layouts: 12.7 us -> 8.64 us
  matrix products: 7.98 us -> 5.57 us
  other arithmetic: 2.92 us -> 5.04 us
    convert_element_type x1 -> x0, local copies, waits for them, and re-layouts: 2.59 us -> none  [shards(): jnp.dot(tokens, qkv_weight, preferred_element_type=jnp.float32)]
    convert_element_type x1, other arithmetic: 0.02 us -> 2.14 us  [shards(): all_seg = mine[:, :, 3 * HEAD].astype(jnp.int32).reshape(groups * tok_rows)]
    squeeze x1, local copies, waits for them, and re-layouts: 1.46 us -> 0.17 us  [shards(): grouped[:, 1]]
  transfers between devices with their start and end apart: 1 -> 1, of which waited for: 1 -> 1; matrix products, arithmetic and copies ran while one was open for 1% -> 2% of each run, Pallas kernels for 0% -> 0%
where the time goes in v10:
time: 123 us; the launch traced here: 122 us
  blocking collectives  51.3 us (42%)
  Pallas kernels  32.7 us (27%)
  waiting for transfers between devices  15 us (12%)
  local copies, waits for them, and re-layouts  8.64 us (7%)
  matrix products  5.57 us (5%)
  other arithmetic  5.04 us (4%)
  starting transfers between devices  3.48 us (3%)
    all_to_all x1, blocking collectives, shards(): lax.all_to_all(payload, 'seq', split_axis=0, concat_axis=0, tiled=True)  51.3 us
    pallas_call x1, Pallas kernels, attention(): pl.pallas_call(attn_kernel, grid_spec=grid_spec, out_shape=jax.ShapeDtype...  32.7 us
    all_to_all x1, waiting for transfers between devices, shards(): lax.all_to_all(context.reshape(groups, tok_rows, HEAD), 'seq', split_axis...  15 us
    dot_general x1, matrix products, shards(): jnp.einsum('td,dc->ct', tokens, qkv_weight, preferred_element_type=jnp.fl...  4.75 us
    all_to_all x1, local copies, waits for them, and re-layouts, shards(): lax.all_to_all(payload, 'seq', split_axis=0, concat_axis=0, tiled=True)  3.73 us
    all_to_all x1, starting transfers between devices, shards(): lax.all_to_all(context.reshape(groups, tok_rows, HEAD), 'seq', split_axis...  3.48 us
  transfers between devices with their start and end apart: 1, of which 1 were waited for; matrix products, arithmetic and copies ran while one was open for 2% of the time, Pallas kernels for 0%

profile of v10, /device:TPU:1, one launch (start us, length us, event | category | flops | bytes accessed | tf_op | source)
XLA Modules:
  0.0 122.4 jit_solution(4461417381328708418)
XLA Ops:
  0.6 0.0 copy-start
  0.6 0.8 convert_element_type.26
  1.5 4.7 %convolution_convert_fusion = bf16[3072,256]{1,0:T(8,128)(2,1)S(1)} fusion(bf16[1024,3072]{1,0:T(8,128)(2,1)} %param.9, bf16[256,1024]{1,0:T(8,128)(2,1)} %param.7), kind=kOutput, calls=%fused_computation | convolution fusion | flops 1611399168 | bytes 8388608 | tf_op jit(solution)/shard_map/td,dc->ct/dot_general | solution.py:95
  6.2 0.2 slice_bitcast_fusion.2
  6.4 0.1 pad_maximum_fusion
  6.6 51.3 %all_to_all.10 = bf16[16,193,256]{2,1,0:T(8,128)(2,1)} all-to-all(bf16[16,193,256]{2,1,0:T(8,128)(2,1)S(1)} %pad_maximum_fusion), channel_id=1, replica_groups=mesh['seq'=16,'rep'=16] {'seq'}, dimensions={0} | all-to-all | bytes 3162112 | tf_op jit(solution)/shard_map/all_to_all | solution.py:99
  57.8 3.7 %copy.34 = bf16[16,193,256]{1,2,0:T(8,128)(2,1)} copy(bf16[16,193,256]{2,1,0:T(8,128)(2,1)} %all_to_all.10) | data formatting | bytes 3162112 | tf_op jit(solution)/shard_map/all_to_all | solution.py:99
  61.5 2.1 %convert_reduce_fusion = s32[16,256]{1,0:T(8,128)S(1)} fusion(bf16[16,256,193]{2,1,0:T(8,128)(2,1)} %bitcast.34), kind=kLoop, calls=%fused_computation.1 | loop fusion | flops 4096 | bytes 24576 | tf_op jit(solution)/shard_map/convert_element_type | solution.py:102
  63.7 0.7 convert_reduce_fusion.1.cnt_ref
  64.4 32.7 %shard_map.86 = bf16[4096,64]{1,0:T(8,128)(2,1)} custom-call(s32[5]{0:T(128)} %convert_reduce_fusion.1.cnt_ref, bf16[8,512,193]{2,1,0:T(8,128)(2,1)} %bitcast.35, bf16[4,1024,193]{2,1,0:T(8,128)(2,1)} %bitcast.36), custom_call_target="tpu_custom_call" | custom-call | tf_op jit(solution)/shard_map/pallas_call | solution.py:84
  97.0 0.0 copy-start.1
  97.0 0.0 copy-start.2
  97.0 2.4 %copy.35 = bf16[16,256,64]{1,2,0:T(8,128)(2,1)} copy(bf16[16,256,64]{2,1,0:T(8,128)(2,1)} %bitcast.38) | data formatting | bytes 1048576 | tf_op jit(solution)/shard_map/reshape | solution.py:106
  99.4 3.5 %all-to-all-start.1 = ((bf16[16,256,64]{1,2,0:T(8,128)(2,1)}), bf16[16,256,64]{1,2,0:T(8,128)(2,1)S(1)}, u32[]{:S(2)}, u32[]{:S(2)}) async-start(bf16[16,256,64]{1,2,0:T(8,128)(2,1)} %copy.35), calls=%async_computation.1 | async-start | bytes 1048576 | tf_op jit(solution)/shard_map/all_to_all | solution.py:106
  102.9 2.3 %slice.24 = bf16[16,256,128]{2,1,0:T(8,128)(2,1)} slice(bf16[16,256,193]{2,1,0:T(8,128)(2,1)} %bitcast.37), slice={[0:16], [0:256], [0:128]} | slice | bytes 2097152 | tf_op jit(solution)/shard_map/slice | solution.py:101
  105.2 15.0 %all-to-all-done.1 = bf16[16,256,64]{1,2,0:T(8,128)(2,1)S(1)} async-done(((bf16[16,256,64]{1,2,0:T(8,128)(2,1)}), bf16[16,256,64]{1,2,0:T(8,128)(2,1)S(1)}, u32[]{:S(2)}, u32[]{:S(2)}) %all-to-all-start.1) | async-done | bytes 524320 | tf_op jit(solution)/shard_map/all_to_all | solution.py:106
  120.2 0.0 copy-done
  120.2 0.0 copy-done.1
  120.2 0.0 copy-done.2
  120.2 0.0 copy-start.3
  120.3 0.0 copy-start.4
  120.3 0.8 fusion.2
  121.1 0.3 multiply_reduce_fusion
  121.4 0.0 copy-done.3
  121.4 0.0 copy-done.4
  121.4 1.0 add_convert_fusion
  (4 shorter events, 0.0 us)
Async XLA Ops:
  0.6 119.6 %copy-start = (bf16[1024,1024]{1,0:T(8,128)(2,1)S(1)}, bf16[1024,1024]{1,0:T(8,128)(2,1)}, u32[]{:S(2)}) copy-start(bf16[1024,1024]{1,0:T(8,128)(2,1)} %param.10) | copy-start | bytes 6291460
  97.0 23.2 %copy-start.1 = (bf16[256,1024]{1,0:T(8,128)(2,1)S(1)}, bf16[256,1024]{1,0:T(8,128)(2,1)}, u32[]{:S(2)}) copy-start(bf16[256,1024]{1,0:T(8,128)(2,1)} %param.7) | copy-start | bytes 1572868
  97.0 23.2 %copy-start.2 = (f32[1024]{0:T(1024)S(1)}, f32[1024]{0:T(1024)}, u32[]{:S(2)}) copy-start(f32[1024]{0:T(1024)} %param.11) | copy-start | bytes 12292
  99.4 20.8 %all-to-all-start.1 = ((bf16[16,256,64]{1,2,0:T(8,128)(2,1)}), bf16[16,256,64]{1,2,0:T(8,128)(2,1)S(1)}, u32[]{:S(2)}, u32[]{:S(2)}) async-start(bf16[16,256,64]{1,2,0:T(8,128)(2,1)} %copy.35), calls=%async_computation.1 | async-start | bytes 1048576 | tf_op jit(solution)/shard_map/all_to_all | solution.py:106
  120.2 1.1 copy-start.3
  120.3 1.1 copy-start.4

commit v11 on v10

--- a/solution.py
+++ b/solution.py
@@ -64,11 +64,13 @@
     carry = lax.fori_loop(lo, mid_lo, masked_tile, (m0, l0, acc0))
     carry = lax.fori_loop(mid_lo, mid_hi, plain_tile, carry)
     _, l, acc = lax.fori_loop(mid_hi, hi, masked_tile, carry)
-    out = pltpu.roll(acc / l, HEAD, 1)
-    o_ref[...] = out[:, :HEAD].astype(o_ref.dtype)
+    out = jnp.transpose(acc / l)[HEAD:, :].astype(o_ref.dtype)
+    per = o_ref.shape[2]
+    for b in range(BQ // per):
+        o_ref[b] = out[:, b * per:(b + 1) * per]
 
 
-def attention(mine, counts):
+def attention(mine, counts, tok_rows):
     nk, _, feat = mine.shape
     rows = nk * BK
     nq = rows // BQ
@@ -79,12 +81,12 @@
             pl.BlockSpec((1, BQ, feat), lambda i, cnt: (i, 0, 0)),
             pl.BlockSpec((nk, BK, feat), lambda i, cnt: (0, 0, 0)),
         ],
-        out_specs=pl.BlockSpec((BQ, HEAD), lambda i, cnt: (i, 0)),
+        out_specs=pl.BlockSpec((BQ // tok_rows, HEAD, tok_rows), lambda i, cnt: (i, 0, 0)),
     )
     return pl.pallas_call(
         attn_kernel,
         grid_spec=grid_spec,
-        out_shape=jax.ShapeDtypeStruct((rows, HEAD), jnp.bfloat16),
+        out_shape=jax.ShapeDtypeStruct((rows // tok_rows, HEAD, tok_rows), jnp.bfloat16),
         interpret=INTERPRET,
     )(counts, mine.reshape(nq, BQ, feat), mine)
 
@@ -99,13 +101,13 @@
     mine_t = lax.all_to_all(payload, "seq", split_axis=0, concat_axis=0, tiled=True)
     mine = jnp.swapaxes(mine_t, 1, 2)
     kv_cache = mine[:, :, :2 * HEAD].reshape(groups * tok_rows, 2 * HEAD)
-    all_seg = mine[:, :, 3 * HEAD].astype(jnp.int32).reshape(groups * tok_rows)
+    all_seg = mine_t[:, 3 * HEAD, :].astype(jnp.int32).reshape(groups * tok_rows)
     levels = jnp.arange(SEGS + 1, dtype=jnp.int32)
     counts = jnp.sum((all_seg[None, :] < levels[:, None]).astype(jnp.int32), axis=1)
-    context = attention(mine.reshape(groups * tok_rows // BK, BK, 3 * HEAD + 1), counts)
-    ctx = lax.all_to_all(context.reshape(groups, tok_rows, HEAD), "seq", split_axis=0, concat_axis=0, tiled=True)
+    context = attention(mine.reshape(groups * tok_rows // BK, BK, 3 * HEAD + 1), counts, tok_rows)
+    ctx = lax.all_to_all(context, "seq", split_axis=0, concat_axis=0, tiled=True)
     mixed = (
-        jnp.einsum("htc,hcd->td", ctx, out_weight.reshape(HEADS, HEAD, width), preferred_element_type=jnp.float32)
+        jnp.einsum("hct,hcd->td", ctx, out_weight.reshape(HEADS, HEAD, width), preferred_element_type=jnp.float32)
         + out_bias
         + tokens.astype(jnp.float32)
     )

time: 123 us -> 120 us (0.976)
  the two profiles are of different devices: /device:TPU:1 before, /device:TPU:27 now
where the time goes in v11:
time: 120 us
  blocking collectives  50.3 us (42%)
  Pallas kernels  34 us (28%)
  waiting for transfers between devices  15 us (12%)
  local copies, waits for them, and re-layouts  7.4 us (6%)
  matrix products  5.57 us (5%)
  starting transfers between devices  3.61 us (3%)
  other arithmetic  2.92 us (2%)
    all_to_all x1, blocking collectives, shards(): lax.all_to_all(payload, 'seq', split_axis=0, concat_axis=0, tiled=True)  50.3 us
    pallas_call x1, Pallas kernels, attention(): pl.pallas_call(attn_kernel, grid_spec=grid_spec, out_shape=jax.ShapeDtype...  34 us
    all_to_all x1, waiting for transfers between devices, shards(): lax.all_to_all(context, 'seq', split_axis=0, concat_axis=0, tiled=True)  15 us
    dot_general x1, matrix products, shards(): jnp.einsum('td,dc->ct', tokens, qkv_weight, preferred_element_type=jnp.fl...  4.75 us
    all_to_all x1, local copies, waits for them, and re-layouts, shards(): lax.all_to_all(payload, 'seq', split_axis=0, concat_axis=0, tiled=True)  3.72 us
    all_to_all x1, starting transfers between devices, shards(): lax.all_to_all(context, 'seq', split_axis=0, concat_axis=0, tiled=True)  3.61 us
  transfers between devices with their start and end apart: 1, of which 1 were waited for; matrix products, arithmetic and copies ran while one was open for 2% of the time, Pallas kernels for 0%

profile of v11, /device:TPU:27, one launch (start us, length us, event | category | flops | bytes accessed | tf_op | source)
XLA Modules:
  0.0 119.6 jit_solution(10451529225864446928)
XLA Ops:
  0.6 0.0 copy-start
  0.6 0.8 convert_element_type.26
  1.5 4.7 %convolution_convert_fusion = bf16[3072,256]{1,0:T(8,128)(2,1)S(1)} fusion(bf16[1024,3072]{1,0:T(8,128)(2,1)} %param.9, bf16[256,1024]{1,0:T(8,128)(2,1)} %param.7), kind=kOutput, calls=%fused_computation | convolution fusion | flops 1611399168 | bytes 8388608 | tf_op jit(solution)/shard_map/td,dc->ct/dot_general | solution.py:97
  6.2 0.2 slice_bitcast_fusion.2
  6.4 0.1 pad_maximum_fusion
  6.6 50.3 %all_to_all.10 = bf16[16,193,256]{2,1,0:T(8,128)(2,1)S(1)} all-to-all(bf16[16,193,256]{2,1,0:T(8,128)(2,1)S(1)} %pad_maximum_fusion), channel_id=1, replica_groups=mesh['seq'=16,'rep'=16] {'seq'}, dimensions={0} | all-to-all | bytes 3162112 | tf_op jit(solution)/shard_map/all_to_all | solution.py:101
  56.9 0.0 copy-start.1
  56.9 1.2 copy-done.1
  58.1 0.7 convert_reduce_fusion.cnt_ref
  58.8 3.7 %copy.30 = bf16[16,193,256]{1,2,0:T(8,128)(2,1)} copy(bf16[16,193,256]{2,1,0:T(8,128)(2,1)} %copy-done.1) | data formatting | bytes 3162112 | tf_op jit(solution)/shard_map/all_to_all | solution.py:101
  62.5 34.0 %shard_map.86 = bf16[16,64,256]{2,1,0:T(8,128)(2,1)} custom-call(s32[5]{0:T(128)} %convert_reduce_fusion.cnt_ref, bf16[8,512,193]{2,1,0:T(8,128)(2,1)} %bitcast.32, bf16[4,1024,193]{2,1,0:T(8,128)(2,1)} %bitcast.33), custom_call_target="tpu_custom_call" | custom-call | tf_op jit(solution)/shard_map/pallas_call | solution.py:86
  96.5 0.0 copy-start.2
  96.5 0.0 copy-start.3
  96.5 3.6 %all-to-all-start.1 = ((bf16[16,64,256]{2,1,0:T(8,128)(2,1)}), bf16[16,64,256]{2,1,0:T(8,128)(2,1)S(1)}, u32[]{:S(2)}, u32[]{:S(2)}) async-start(bf16[16,64,256]{2,1,0:T(8,128)(2,1)} %shard_map.86), calls=%async_computation.1 | async-start | bytes 1048576 | tf_op jit(solution)/shard_map/all_to_all | solution.py:108
  100.1 2.3 %slice.24 = bf16[16,256,128]{2,1,0:T(8,128)(2,1)} slice(bf16[16,256,193]{2,1,0:T(8,128)(2,1)} %bitcast.34), slice={[0:16], [0:256], [0:128]} | slice | bytes 2097152 | tf_op jit(solution)/shard_map/slice | solution.py:103
  102.4 15.0 %all-to-all-done.1 = bf16[16,64,256]{2,1,0:T(8,128)(2,1)S(1)} async-done(((bf16[16,64,256]{2,1,0:T(8,128)(2,1)}), bf16[16,64,256]{2,1,0:T(8,128)(2,1)S(1)}, u32[]{:S(2)}, u32[]{:S(2)}) %all-to-all-start.1) | async-done | bytes 524320 | tf_op jit(solution)/shard_map/all_to_all | solution.py:108
  117.4 0.0 copy-done
  117.4 0.0 copy-done.2
  117.4 0.0 copy-done.3
  117.4 0.0 copy-start.4
  117.4 0.0 copy-start.5
  117.4 0.8 fusion.2
  118.3 0.3 multiply_reduce_fusion
  118.5 0.0 copy-done.4
  118.5 0.0 copy-done.5
  118.6 1.0 add_convert_fusion
  (4 shorter events, 0.0 us)
Async XLA Ops:
  0.6 116.8 %copy-start = (bf16[1024,1024]{1,0:T(8,128)(2,1)S(1)}, bf16[1024,1024]{1,0:T(8,128)(2,1)}, u32[]{:S(2)}) copy-start(bf16[1024,1024]{1,0:T(8,128)(2,1)} %param.10) | copy-start | bytes 6291460
  56.9 1.2 copy-start.1
  96.5 20.9 %copy-start.2 = (bf16[256,1024]{1,0:T(8,128)(2,1)S(1)}, bf16[256,1024]{1,0:T(8,128)(2,1)}, u32[]{:S(2)}) copy-start(bf16[256,1024]{1,0:T(8,128)(2,1)} %param.7) | copy-start | bytes 1572868
  96.5 20.9 %copy-start.3 = (f32[1024]{0:T(1024)S(1)}, f32[1024]{0:T(1024)}, u32[]{:S(2)}) copy-start(f32[1024]{0:T(1024)} %param.11) | copy-start | bytes 12292
  96.5 20.9 %all-to-all-start.1 = ((bf16[16,64,256]{2,1,0:T(8,128)(2,1)}), bf16[16,64,256]{2,1,0:T(8,128)(2,1)S(1)}, u32[]{:S(2)}, u32[]{:S(2)}) async-start(bf16[16,64,256]{2,1,0:T(8,128)(2,1)} %shard_map.86), calls=%async_computation.1 | async-start | bytes 1048576 | tf_op jit(solution)/shard_map/all_to_all | solution.py:108
  117.4 1.1 copy-start.4
  117.4 1.1 copy-start.5

commit v12 on v11

--- a/solution.py
+++ b/solution.py
@@ -33,14 +33,15 @@
     mid_lo = jnp.where(inside, (start + BK - 1) // BK, hi)
     mid_hi = jnp.where(inside, jnp.maximum(end // BK, mid_lo), hi)
     scale = 1.0 / math.sqrt(HEAD)
-    q = q_ref[0, :, 2 * HEAD:3 * HEAD] * jnp.asarray(scale, jnp.bfloat16)
+    q = q_ref[0, :, 3 * HEAD:4 * HEAD] * jnp.asarray(scale, jnp.bfloat16)
     rows = q0 + lax.broadcasted_iota(jnp.int32, (BQ, 1), 0)
     sq = seg_of(rows, b1, b2, b3)
 
     def tile(j, carry, masked):
-        m, l, acc = carry
+        m, acc = carry
         kv = kv_ref[j, :, :2 * HEAD]
-        s = lax.dot_general(q, kv[:, :HEAD], (((1,), (1,)), ((), ())), preferred_element_type=jnp.float32)
+        k = kv_ref[j, :, 2 * HEAD:3 * HEAD]
+        s = lax.dot_general(q, k, (((1,), (1,)), ((), ())), preferred_element_type=jnp.float32)
         if masked:
             cols = j * BK + lax.broadcasted_iota(jnp.int32, (1, BK), 1)
             s = jnp.where(sq == seg_of(cols, b1, b2, b3), s, -jnp.inf)
@@ -48,9 +49,8 @@
         m_safe = jnp.where(m_new == -jnp.inf, 0.0, m_new)
         p = jnp.exp(s - m_safe)
         alpha = jnp.exp(m - m_safe)
-        l = alpha * l + jnp.sum(p, axis=1, keepdims=True)
         acc = alpha * acc + jnp.dot(p.astype(jnp.bfloat16), kv, preferred_element_type=jnp.float32)
-        return m_new, l, acc
+        return m_new, acc
 
     def masked_tile(j, carry):
         return tile(j, carry, True)
@@ -59,12 +59,11 @@
         return tile(j, carry, False)
 
     m0 = jnp.full((BQ, 1), -jnp.inf, jnp.float32)
-    l0 = jnp.zeros((BQ, 1), jnp.float32)
     acc0 = jnp.zeros((BQ, 2 * HEAD), jnp.float32)
-    carry = lax.fori_loop(lo, mid_lo, masked_tile, (m0, l0, acc0))
+    carry = lax.fori_loop(lo, mid_lo, masked_tile, (m0, acc0))
     carry = lax.fori_loop(mid_lo, mid_hi, plain_tile, carry)
-    _, l, acc = lax.fori_loop(mid_hi, hi, masked_tile, carry)
-    out = jnp.transpose(acc / l)[HEAD:, :].astype(o_ref.dtype)
+    _, acc = lax.fori_loop(mid_hi, hi, masked_tile, carry)
+    out = jnp.transpose(acc / acc[:, :1])[HEAD:, :].astype(o_ref.dtype)
     per = o_ref.shape[2]
     for b in range(BQ // per):
         o_ref[b] = out[:, b * per:(b + 1) * per]
@@ -104,7 +103,10 @@
     all_seg = mine_t[:, 3 * HEAD, :].astype(jnp.int32).reshape(groups * tok_rows)
     levels = jnp.arange(SEGS + 1, dtype=jnp.int32)
     counts = jnp.sum((all_seg[None, :] < levels[:, None]).astype(jnp.int32), axis=1)
-    context = attention(mine.reshape(groups * tok_rows // BK, BK, 3 * HEAD + 1), counts, tok_rows)
+    ones = jnp.ones((groups, HEAD, tok_rows), jnp.bfloat16)
+    kernel_t = jnp.concatenate([ones, mine_t[:, HEAD:2 * HEAD], mine_t[:, :HEAD], mine_t[:, 2 * HEAD:3 * HEAD]], axis=1)
+    kernel_in = jnp.swapaxes(kernel_t, 1, 2).reshape(groups * tok_rows // BK, BK, 4 * HEAD)
+    context = attention(kernel_in, counts, tok_rows)
     ctx = lax.all_to_all(context, "seq", split_axis=0, concat_axis=0, tiled=True)
     mixed = (
         jnp.einsum("hct,hcd->td", ctx, out_weight.reshape(HEADS, HEAD, width), preferred_element_type=jnp.float32)

time: 120 us -> 120 us (level)
  the two profiles are of different devices: /device:TPU:27 before, /device:TPU:1 now
where the time goes in v12:
time: 120 us
  waiting for transfers between devices  51.1 us (43%)
  Pallas kernels  29.4 us (24%)
  starting transfers between devices  14.2 us (12%)
  local copies, waits for them, and re-layouts  11.7 us (10%)
  other arithmetic  6.87 us (6%)
  matrix products  5.58 us (5%)
    all_to_all x1, waiting for transfers between devices, shards(): lax.all_to_all(payload, 'seq', split_axis=0, concat_axis=0, tiled=True)  39.9 us
    pallas_call x1, Pallas kernels, attention(): pl.pallas_call(attn_kernel, grid_spec=grid_spec, out_shape=jax.ShapeDtype...  29.4 us
    all_to_all x1, waiting for transfers between devices, shards(): lax.all_to_all(context, 'seq', split_axis=0, concat_axis=0, tiled=True)  11.1 us
    all_to_all x1, starting transfers between devices, shards(): lax.all_to_all(payload, 'seq', split_axis=0, concat_axis=0, tiled=True)  9.97 us
    dot_general x1, matrix products, shards(): jnp.einsum('td,dc->ct', tokens, qkv_weight, preferred_element_type=jnp.fl...  4.75 us
    all_to_all x1, starting transfers between devices, shards(): lax.all_to_all(context, 'seq', split_axis=0, concat_axis=0, tiled=True)  4.23 us
    transpose x1, local copies, waits for them, and re-layouts, shards(): jnp.swapaxes(kernel_t, 1, 2).reshape(groups * tok_rows // BK, BK, 4 * HEAD)  3.9 us
    all_to_all x1, local copies, waits for them, and re-layouts, shards(): lax.all_to_all(payload, 'seq', split_axis=0, concat_axis=0, tiled=True)  3.77 us
  transfers between devices with their start and end apart: 2, of which 2 were waited for; matrix products, arithmetic and copies ran while one was open for 5% of the time, Pallas kernels for 0%

profile of v12, /device:TPU:1, one launch (start us, length us, event | category | flops | bytes accessed | tf_op | source)
XLA Modules:
  0.0 119.6 jit_solution(9364691445164094001)
XLA Ops:
  0.6 0.0 copy-start
  0.6 0.8 convert_element_type.26
  1.5 4.7 %convolution_convert_fusion = bf16[3072,256]{1,0:T(8,128)(2,1)S(1)} fusion(bf16[1024,3072]{1,0:T(8,128)(2,1)} %param.9, bf16[256,1024]{1,0:T(8,128)(2,1)} %param.7), kind=kOutput, calls=%fused_computation | convolution fusion | flops 1611399168 | bytes 8388608 | tf_op jit(solution)/shard_map/td,dc->ct/dot_general | solution.py:96
  6.2 0.2 slice_bitcast_fusion.2
  6.4 1.3 %pad_maximum_fusion = bf16[16,193,256]{2,1,0:T(8,128)(2,1)} fusion(bf16[16,1,256]{2,1,0:T(2,128)(2,1)S(1)} %broadcast_in_dim.4, bf16[16,64,256]{2,1,0:T(8,128)(2,1)S(1)} %get-tuple-element.7, bf16[16,64,256]{2,1,0:T(8,128)(2,1)S(1)} %get-tuple-element.6, bf16[16,64,256]{2,1,0:T(8,128)(2,1)S(1)} %get-tuple-element.5), kind=kLoop, calls=%fused_computation.2 | loop fusion | flops 6324224 | bytes 3162112 | tf_op jit(solution)/shard_map/concatenate | solution.py:99
  7.7 10.0 %all-to-all-start = ((bf16[16,193,256]{2,1,0:T(8,128)(2,1)}), bf16[16,193,256]{2,1,0:T(8,128)(2,1)}, u32[]{:S(2)}, u32[]{:S(2)}) async-start(bf16[16,193,256]{2,1,0:T(8,128)(2,1)} %pad_maximum_fusion), calls=%async_computation | async-start | bytes 3276800 | tf_op jit(solution)/shard_map/all_to_all | solution.py:100
  17.7 39.9 %all-to-all-done = bf16[16,193,256]{2,1,0:T(8,128)(2,1)} async-done(((bf16[16,193,256]{2,1,0:T(8,128)(2,1)}), bf16[16,193,256]{2,1,0:T(8,128)(2,1)}, u32[]{:S(2)}, u32[]{:S(2)}) %all-to-all-start) | async-done | bytes 1581088 | tf_op jit(solution)/shard_map/all_to_all | solution.py:100
  57.6 0.9 slice_convert_fusion
  58.5 0.7 convert_reduce_fusion.cnt_ref
  59.2 1.5 %fusion.2 = (bf16[16,64,256]{2,1,0:T(8,128)(2,1)S(1)}, bf16[16,64,256]{2,1,0:T(8,128)(2,1)S(1)}, bf16[16,64,256]{2,1,0:T(8,128)(2,1)S(1)}) fusion(bf16[16,193,256]{2,1,0:T(8,128)(2,1)} %all-to-all-done), kind=kLoop, calls=%fused_computation.16 | loop fusion | bytes 3145728 | tf_op jit(solution)/shard_map/slice | solution.py:107
  60.7 1.9 %maximum_bitcast_fusion = bf16[16,256,256]{1,2,0:T(8,128)(2,1)} fusion(bf16[16,64,256]{2,1,0:T(8,128)(2,1)S(1)} %get-tuple-element.3, bf16[16,64,256]{2,1,0:T(8,128)(2,1)S(1)} %get-tuple-element.4, bf16[16,64,256]{2,1,0:T(8,128)(2,1)S(1)} %get-tuple-element.2, bf16[256]{0:T(256)(128)(2,1)S(1)} %pad.clone), kind=kLoop, calls=%fused_computation.1 | loop fusion | flops 8388608 | bytes 3670528 | tf_op jit(solution)/shard_map/transpose | solution.py:108
  62.6 3.9 %copy.32 = bf16[16,256,256]{2,1,0:T(8,128)(2,1)} copy(bf16[16,256,256]{1,2,0:T(8,128)(2,1)} %maximum_bitcast_fusion) | data formatting | bytes 4194304 | tf_op jit(solution)/shard_map/transpose | solution.py:108
  66.5 29.4 %shard_map.86 = bf16[16,64,256]{2,1,0:T(8,128)(2,1)} custom-call(s32[5]{0:T(128)} %convert_reduce_fusion.cnt_ref, bf16[8,512,256]{2,1,0:T(8,128)(2,1)} %bitcast.32, bf16[4,1024,256]{2,1,0:T(8,128)(2,1)} %bitcast.33), custom_call_target="tpu_custom_call" | custom-call | tf_op jit(solution)/shard_map/pallas_call | solution.py:85
  96.0 4.2 %all-to-all-start.1 = ((bf16[16,64,256]{2,1,0:T(8,128)(2,1)}), bf16[16,64,256]{2,1,0:T(8,128)(2,1)S(1)}, u32[]{:S(2)}, u32[]{:S(2)}) async-start(bf16[16,64,256]{2,1,0:T(8,128)(2,1)} %shard_map.86), calls=%async_computation.1 | async-start | bytes 1048576 | tf_op jit(solution)/shard_map/all_to_all | solution.py:110
  100.2 0.0 copy-start.1
  100.2 0.0 copy-start.2
  100.2 3.8 %copy.34 = bf16[16,193,256]{1,2,0:T(8,128)(2,1)} copy(bf16[16,193,256]{2,1,0:T(8,128)(2,1)} %all-to-all-done) | data formatting | bytes 3162112 | tf_op jit(solution)/shard_map/all_to_all | solution.py:100
  104.0 2.3 %slice.39 = bf16[16,256,128]{2,1,0:T(8,128)(2,1)} slice(bf16[16,256,193]{2,1,0:T(8,128)(2,1)} %bitcast.34), slice={[0:16], [0:256], [0:128]} | slice | bytes 2097152 | tf_op jit(solution)/shard_map/slice | solution.py:102
  106.3 11.1 %all-to-all-done.1 = bf16[16,64,256]{2,1,0:T(8,128)(2,1)S(1)} async-done(((bf16[16,64,256]{2,1,0:T(8,128)(2,1)}), bf16[16,64,256]{2,1,0:T(8,128)(2,1)S(1)}, u32[]{:S(2)}, u32[]{:S(2)}) %all-to-all-start.1) | async-done | bytes 524320 | tf_op jit(solution)/shard_map/all_to_all | solution.py:110
  117.4 0.0 copy-done
  117.4 0.0 copy-done.1
  117.4 0.0 copy-done.2
  117.4 0.0 copy-start.3
  117.4 0.0 copy-start.4
  117.4 0.8 fusion.3
  118.3 0.3 multiply_reduce_fusion
  118.5 0.0 copy-done.3
  118.6 0.0 copy-done.4
  118.6 1.0 add_convert_fusion
  (5 shorter events, 0.0 us)
Async XLA Ops:
  0.6 116.8 %copy-start = (bf16[1024,1024]{1,0:T(8,128)(2,1)S(1)}, bf16[1024,1024]{1,0:T(8,128)(2,1)}, u32[]{:S(2)}) copy-start(bf16[1024,1024]{1,0:T(8,128)(2,1)} %param.10) | copy-start | bytes 6291460
  7.7 49.9 %all-to-all-start = ((bf16[16,193,256]{2,1,0:T(8,128)(2,1)}), bf16[16,193,256]{2,1,0:T(8,128)(2,1)}, u32[]{:S(2)}, u32[]{:S(2)}) async-start(bf16[16,193,256]{2,1,0:T(8,128)(2,1)} %pad_maximum_fusion), calls=%async_computation | async-start | bytes 3276800 | tf_op jit(solution)/shard_map/all_to_all | solution.py:100
  96.0 21.4 %all-to-all-start.1 = ((bf16[16,64,256]{2,1,0:T(8,128)(2,1)}), bf16[16,64,256]{2,1,0:T(8,128)(2,1)S(1)}, u32[]{:S(2)}, u32[]{:S(2)}) async-start(bf16[16,64,256]{2,1,0:T(8,128)(2,1)} %shard_map.86), calls=%async_computation.1 | async-start | bytes 1048576 | tf_op jit(solution)/shard_map/all_to_all | solution.py:110
  100.2 17.2 %copy-start.1 = (bf16[256,1024]{1,0:T(8,128)(2,1)S(1)}, bf16[256,1024]{1,0:T(8,128)(2,1)}, u32[]{:S(2)}) copy-start(bf16[256,1024]{1,0:T(8,128)(2,1)} %param.7) | copy-start | bytes 1572868
  100.2 17.2 %copy-start.2 = (f32[1024]{0:T(1024)S(1)}, f32[1024]{0:T(1024)}, u32[]{:S(2)}) copy-start(f32[1024]{0:T(1024)} %param.11) | copy-start | bytes 12292
  117.4 1.1 copy-start.3
  117.4 1.1 copy-start.4

commit v13 on v12

--- a/solution.py
+++ b/solution.py
@@ -33,15 +33,16 @@
     mid_lo = jnp.where(inside, (start + BK - 1) // BK, hi)
     mid_hi = jnp.where(inside, jnp.maximum(end // BK, mid_lo), hi)
     scale = 1.0 / math.sqrt(HEAD)
-    q = q_ref[0, :, 3 * HEAD:4 * HEAD] * jnp.asarray(scale, jnp.bfloat16)
+    q = q_ref[0, :, 2 * HEAD:3 * HEAD] * jnp.asarray(scale, jnp.bfloat16)
     rows = q0 + lax.broadcasted_iota(jnp.int32, (BQ, 1), 0)
     sq = seg_of(rows, b1, b2, b3)
+
+    key_lanes = lax.broadcasted_iota(jnp.int32, (BK, 2 * HEAD), 1) < HEAD
 
     def tile(j, carry, masked):
         m, acc = carry
         kv = kv_ref[j, :, :2 * HEAD]
-        k = kv_ref[j, :, 2 * HEAD:3 * HEAD]
-        s = lax.dot_general(q, k, (((1,), (1,)), ((), ())), preferred_element_type=jnp.float32)
+        s = lax.dot_general(q, kv[:, :HEAD], (((1,), (1,)), ((), ())), preferred_element_type=jnp.float32)
         if masked:
             cols = j * BK + lax.broadcasted_iota(jnp.int32, (1, BK), 1)
             s = jnp.where(sq == seg_of(cols, b1, b2, b3), s, -jnp.inf)
@@ -49,7 +50,8 @@
         m_safe = jnp.where(m_new == -jnp.inf, 0.0, m_new)
         p = jnp.exp(s - m_safe)
         alpha = jnp.exp(m - m_safe)
-        acc = alpha * acc + jnp.dot(p.astype(jnp.bfloat16), kv, preferred_element_type=jnp.float32)
+        rhs = jnp.where(key_lanes, jnp.ones_like(kv), kv)
+        acc = alpha * acc + jnp.dot(p.astype(jnp.bfloat16), rhs, preferred_element_type=jnp.float32)
         return m_new, acc
 
     def masked_tile(j, carry):
@@ -103,10 +105,7 @@
     all_seg = mine_t[:, 3 * HEAD, :].astype(jnp.int32).reshape(groups * tok_rows)
     levels = jnp.arange(SEGS + 1, dtype=jnp.int32)
     counts = jnp.sum((all_seg[None, :] < levels[:, None]).astype(jnp.int32), axis=1)
-    ones = jnp.ones((groups, HEAD, tok_rows), jnp.bfloat16)
-    kernel_t = jnp.concatenate([ones, mine_t[:, HEAD:2 * HEAD], mine_t[:, :HEAD], mine_t[:, 2 * HEAD:3 * HEAD]], axis=1)
-    kernel_in = jnp.swapaxes(kernel_t, 1, 2).reshape(groups * tok_rows // BK, BK, 4 * HEAD)
-    context = attention(kernel_in, counts, tok_rows)
+    context = attention(mine.reshape(groups * tok_rows // BK, BK, 3 * HEAD + 1), counts, tok_rows)
     ctx = lax.all_to_all(context, "seq", split_axis=0, concat_axis=0, tiled=True)
     mixed = (
         jnp.einsum("hct,hcd->td", ctx, out_weight.reshape(HEADS, HEAD, width), preferred_element_type=jnp.float32)

time: 120 us -> 115 us (0.958)
  the two profiles are of different devices: /device:TPU:1 before, /device:TPU:5 now
where the time goes in v13:
time: 115 us; the launch traced here: 114 us
  blocking collectives  50.3 us (44%)
  Pallas kernels  28.7 us (25%)
  waiting for transfers between devices  15 us (13%)
  local copies, waits for them, and re-layouts  7.4 us (6%)
  matrix products  5.58 us (5%)
  starting transfers between devices  3.61 us (3%)
  other arithmetic  2.92 us (3%)
    all_to_all x1, blocking collectives, shards(): lax.all_to_all(payload, 'seq', split_axis=0, concat_axis=0, tiled=True)  50.3 us
    pallas_call x1, Pallas kernels, attention(): pl.pallas_call(attn_kernel, grid_spec=grid_spec, out_shape=jax.ShapeDtype...  28.7 us
    all_to_all x1, waiting for transfers between devices, shards(): lax.all_to_all(context, 'seq', split_axis=0, concat_axis=0, tiled=True)  15 us
    dot_general x1, matrix products, shards(): jnp.einsum('td,dc->ct', tokens, qkv_weight, preferred_element_type=jnp.fl...  4.75 us
    all_to_all x1, local copies, waits for them, and re-layouts, shards(): lax.all_to_all(payload, 'seq', split_axis=0, concat_axis=0, tiled=True)  3.72 us
    all_to_all x1, starting transfers between devices, shards(): lax.all_to_all(context, 'seq', split_axis=0, concat_axis=0, tiled=True)  3.61 us
  transfers between devices with their start and end apart: 1, of which 1 were waited for; matrix products, arithmetic and copies ran while one was open for 2% of the time, Pallas kernels for 0%

profile of v13, /device:TPU:5, one launch (start us, length us, event | category | flops | bytes accessed | tf_op | source)
XLA Modules:
  0.0 114.3 jit_solution(2429926558246473093)
XLA Ops:
  0.6 0.0 copy-start
  0.6 0.8 convert_element_type.26
  1.5 4.8 %convolution_convert_fusion = bf16[3072,256]{1,0:T(8,128)(2,1)S(1)} fusion(bf16[1024,3072]{1,0:T(8,128)(2,1)} %param.9, bf16[256,1024]{1,0:T(8,128)(2,1)} %param.7), kind=kOutput, calls=%fused_computation | convolution fusion | flops 1611399168 | bytes 8388608 | tf_op jit(solution)/shard_map/td,dc->ct/dot_general | solution.py:98
  6.2 0.2 slice_bitcast_fusion.2
  6.4 0.1 pad_maximum_fusion
  6.6 50.3 %all_to_all.10 = bf16[16,193,256]{2,1,0:T(8,128)(2,1)S(1)} all-to-all(bf16[16,193,256]{2,1,0:T(8,128)(2,1)S(1)} %pad_maximum_fusion), channel_id=1, replica_groups=mesh['seq'=16,'rep'=16] {'seq'}, dimensions={0} | all-to-all | bytes 3162112 | tf_op jit(solution)/shard_map/all_to_all | solution.py:102
  56.9 0.0 copy-start.1
  56.9 1.2 %copy-done.1 = bf16[16,193,256]{2,1,0:T(8,128)(2,1)} copy-done((bf16[16,193,256]{2,1,0:T(8,128)(2,1)}, bf16[16,193,256]{2,1,0:T(8,128)(2,1)S(1)}, u32[]{:S(2)}) %copy-start.1) | copy-done | bytes 1581080
  58.1 0.7 convert_reduce_fusion.cnt_ref
  58.7 3.7 %copy.30 = bf16[16,193,256]{1,2,0:T(8,128)(2,1)} copy(bf16[16,193,256]{2,1,0:T(8,128)(2,1)} %copy-done.1) | data formatting | bytes 3162112 | tf_op jit(solution)/shard_map/all_to_all | solution.py:102
  62.5 28.7 %shard_map.86 = bf16[16,64,256]{2,1,0:T(8,128)(2,1)} custom-call(s32[5]{0:T(128)} %convert_reduce_fusion.cnt_ref, bf16[8,512,193]{2,1,0:T(8,128)(2,1)} %bitcast.32, bf16[4,1024,193]{2,1,0:T(8,128)(2,1)} %bitcast.33), custom_call_target="tpu_custom_call" | custom-call | tf_op jit(solution)/shard_map/pallas_call | solution.py:87
  91.2 0.0 copy-start.2
  91.2 0.0 copy-start.3
  91.2 3.6 %all-to-all-start.1 = ((bf16[16,64,256]{2,1,0:T(8,128)(2,1)}), bf16[16,64,256]{2,1,0:T(8,128)(2,1)S(1)}, u32[]{:S(2)}, u32[]{:S(2)}) async-start(bf16[16,64,256]{2,1,0:T(8,128)(2,1)} %shard_map.86), calls=%async_computation.1 | async-start | bytes 1048576 | tf_op jit(solution)/shard_map/all_to_all | solution.py:109
  94.8 2.3 %slice.24 = bf16[16,256,128]{2,1,0:T(8,128)(2,1)} slice(bf16[16,256,193]{2,1,0:T(8,128)(2,1)} %bitcast.34), slice={[0:16], [0:256], [0:128]} | slice | bytes 2097152 | tf_op jit(solution)/shard_map/slice | solution.py:104
  97.1 15.0 %all-to-all-done.1 = bf16[16,64,256]{2,1,0:T(8,128)(2,1)S(1)} async-done(((bf16[16,64,256]{2,1,0:T(8,128)(2,1)}), bf16[16,64,256]{2,1,0:T(8,128)(2,1)S(1)}, u32[]{:S(2)}, u32[]{:S(2)}) %all-to-all-start.1) | async-done | bytes 524320 | tf_op jit(solution)/shard_map/all_to_all | solution.py:109
  112.1 0.0 copy-done
  112.1 0.0 copy-done.2
  112.1 0.0 copy-done.3
  112.1 0.0 copy-start.4
  112.1 0.0 copy-start.5
  112.1 0.8 fusion.2
  113.0 0.3 multiply_reduce_fusion
  113.2 0.0 copy-done.4
  113.3 0.0 copy-done.5
  113.3 1.0 add_convert_fusion
  (4 shorter events, 0.0 us)
Async XLA Ops:
  0.6 111.5 %copy-start = (bf16[1024,1024]{1,0:T(8,128)(2,1)S(1)}, bf16[1024,1024]{1,0:T(8,128)(2,1)}, u32[]{:S(2)}) copy-start(bf16[1024,1024]{1,0:T(8,128)(2,1)} %param.10) | copy-start | bytes 6291460
  56.9 1.2 %copy-start.1 = (bf16[16,193,256]{2,1,0:T(8,128)(2,1)}, bf16[16,193,256]{2,1,0:T(8,128)(2,1)S(1)}, u32[]{:S(2)}) copy-start(bf16[16,193,256]{2,1,0:T(8,128)(2,1)S(1)} %all_to_all.10) | copy-start | bytes 4743172
  91.2 20.9 %copy-start.2 = (bf16[256,1024]{1,0:T(8,128)(2,1)S(1)}, bf16[256,1024]{1,0:T(8,128)(2,1)}, u32[]{:S(2)}) copy-start(bf16[256,1024]{1,0:T(8,128)(2,1)} %param.7) | copy-start | bytes 1572868
  91.2 20.9 %copy-start.3 = (f32[1024]{0:T(1024)S(1)}, f32[1024]{0:T(1024)}, u32[]{:S(2)}) copy-start(f32[1024]{0:T(1024)} %param.11) | copy-start | bytes 12292
  91.2 20.9 %all-to-all-start.1 = ((bf16[16,64,256]{2,1,0:T(8,128)(2,1)}), bf16[16,64,256]{2,1,0:T(8,128)(2,1)S(1)}, u32[]{:S(2)}, u32[]{:S(2)}) async-start(bf16[16,64,256]{2,1,0:T(8,128)(2,1)} %shard_map.86), calls=%async_computation.1 | async-start | bytes 1048576 | tf_op jit(solution)/shard_map/all_to_all | solution.py:109
  112.1 1.1 copy-start.4
  112.1 1.1 copy-start.5

commit v14 on v13

--- a/solution.py
+++ b/solution.py
@@ -47,9 +47,8 @@
             cols = j * BK + lax.broadcasted_iota(jnp.int32, (1, BK), 1)
             s = jnp.where(sq == seg_of(cols, b1, b2, b3), s, -jnp.inf)
         m_new = jnp.maximum(m, jnp.max(s, axis=1, keepdims=True))
-        m_safe = jnp.where(m_new == -jnp.inf, 0.0, m_new)
-        p = jnp.exp(s - m_safe)
-        alpha = jnp.exp(m - m_safe)
+        p = jnp.exp(s - m_new)
+        alpha = jnp.exp(m - m_new)
         rhs = jnp.where(key_lanes, jnp.ones_like(kv), kv)
         acc = alpha * acc + jnp.dot(p.astype(jnp.bfloat16), rhs, preferred_element_type=jnp.float32)
         return m_new, acc
@@ -60,7 +59,7 @@
     def plain_tile(j, carry):
         return tile(j, carry, False)
 
-    m0 = jnp.full((BQ, 1), -jnp.inf, jnp.float32)
+    m0 = jnp.full((BQ, 1), -1e30, jnp.float32)
     acc0 = jnp.zeros((BQ, 2 * HEAD), jnp.float32)
     carry = lax.fori_loop(lo, mid_lo, masked_tile, (m0, acc0))
     carry = lax.fori_loop(mid_lo, mid_hi, plain_tile, carry)

time: 115 us -> 114 us (level)
  the two profiles are of different devices: /device:TPU:5 before, /device:TPU:1 now
where the time goes in v14:
time: 114 us
  blocking collectives  51.2 us (45%)
  Pallas kernels  27.6 us (24%)
  waiting for transfers between devices  15 us (13%)
  local copies, waits for them, and re-layouts  7.4 us (6%)
  matrix products  5.58 us (5%)
  starting transfers between devices  3.6 us (3%)
  other arithmetic  2.92 us (3%)
    all_to_all x1, blocking collectives, shards(): lax.all_to_all(payload, 'seq', split_axis=0, concat_axis=0, tiled=True)  51.2 us
    pallas_call x1, Pallas kernels, attention(): pl.pallas_call(attn_kernel, grid_spec=grid_spec, out_shape=jax.ShapeDtype...  27.6 us
    all_to_all x1, waiting for transfers between devices, shards(): lax.all_to_all(context, 'seq', split_axis=0, concat_axis=0, tiled=True)  15 us
    dot_general x1, matrix products, shards(): jnp.einsum('td,dc->ct', tokens, qkv_weight, preferred_element_type=jnp.fl...  4.75 us
    all_to_all x1, local copies, waits for them, and re-layouts, shards(): lax.all_to_all(payload, 'seq', split_axis=0, concat_axis=0, tiled=True)  3.72 us
    all_to_all x1, starting transfers between devices, shards(): lax.all_to_all(context, 'seq', split_axis=0, concat_axis=0, tiled=True)  3.6 us
    slice x1, local copies, waits for them, and re-layouts, shards(): kv_cache = mine[:, :, :2 * HEAD].reshape(groups * tok_rows, 2 * HEAD)  2.3 us
  transfers between devices with their start and end apart: 1, of which 1 were waited for; matrix products, arithmetic and copies ran while one was open for 2% of the time, Pallas kernels for 0%

profile of v14, /device:TPU:1, one launch (start us, length us, event | category | flops | bytes accessed | tf_op | source)
XLA Modules:
  0.0 114.0 jit_solution(1471964396416680253)
XLA Ops:
  0.6 0.0 copy-start
  0.6 0.8 convert_element_type.26
  1.5 4.7 %convolution_convert_fusion = bf16[3072,256]{1,0:T(8,128)(2,1)S(1)} fusion(bf16[1024,3072]{1,0:T(8,128)(2,1)} %param.9, bf16[256,1024]{1,0:T(8,128)(2,1)} %param.7), kind=kOutput, calls=%fused_computation | convolution fusion | flops 1611399168 | bytes 8388608 | tf_op jit(solution)/shard_map/td,dc->ct/dot_general | solution.py:97
  6.2 0.2 slice_bitcast_fusion.2
  6.4 0.1 pad_maximum_fusion
  6.6 51.2 %all_to_all.10 = bf16[16,193,256]{2,1,0:T(8,128)(2,1)S(1)} all-to-all(bf16[16,193,256]{2,1,0:T(8,128)(2,1)S(1)} %pad_maximum_fusion), channel_id=1, replica_groups=mesh['seq'=16,'rep'=16] {'seq'}, dimensions={0} | all-to-all | bytes 3162112 | tf_op jit(solution)/shard_map/all_to_all | solution.py:101
  57.7 0.0 copy-start.1
  57.7 1.2 %copy-done.1 = bf16[16,193,256]{2,1,0:T(8,128)(2,1)} copy-done((bf16[16,193,256]{2,1,0:T(8,128)(2,1)}, bf16[16,193,256]{2,1,0:T(8,128)(2,1)S(1)}, u32[]{:S(2)}) %copy-start.1) | copy-done | bytes 1581080
  58.9 0.7 convert_reduce_fusion.cnt_ref
  59.6 3.7 %copy.30 = bf16[16,193,256]{1,2,0:T(8,128)(2,1)} copy(bf16[16,193,256]{2,1,0:T(8,128)(2,1)} %copy-done.1) | data formatting | bytes 3162112 | tf_op jit(solution)/shard_map/all_to_all | solution.py:101
  63.3 27.6 %shard_map.86 = bf16[16,64,256]{2,1,0:T(8,128)(2,1)} custom-call(s32[5]{0:T(128)} %convert_reduce_fusion.cnt_ref, bf16[8,512,193]{2,1,0:T(8,128)(2,1)} %bitcast.32, bf16[4,1024,193]{2,1,0:T(8,128)(2,1)} %bitcast.33), custom_call_target="tpu_custom_call" | custom-call | tf_op jit(solution)/shard_map/pallas_call | solution.py:86
  90.9 0.0 copy-start.2
  90.9 0.0 copy-start.3
  90.9 3.6 %all-to-all-start.1 = ((bf16[16,64,256]{2,1,0:T(8,128)(2,1)}), bf16[16,64,256]{2,1,0:T(8,128)(2,1)S(1)}, u32[]{:S(2)}, u32[]{:S(2)}) async-start(bf16[16,64,256]{2,1,0:T(8,128)(2,1)} %shard_map.86), calls=%async_computation.1 | async-start | bytes 1048576 | tf_op jit(solution)/shard_map/all_to_all | solution.py:108
  94.5 2.3 %slice.24 = bf16[16,256,128]{2,1,0:T(8,128)(2,1)} slice(bf16[16,256,193]{2,1,0:T(8,128)(2,1)} %bitcast.34), slice={[0:16], [0:256], [0:128]} | slice | bytes 2097152 | tf_op jit(solution)/shard_map/slice | solution.py:103
  96.8 15.0 %all-to-all-done.1 = bf16[16,64,256]{2,1,0:T(8,128)(2,1)S(1)} async-done(((bf16[16,64,256]{2,1,0:T(8,128)(2,1)}), bf16[16,64,256]{2,1,0:T(8,128)(2,1)S(1)}, u32[]{:S(2)}, u32[]{:S(2)}) %all-to-all-start.1) | async-done | bytes 524320 | tf_op jit(solution)/shard_map/all_to_all | solution.py:108
  111.9 0.0 copy-done
  111.9 0.0 copy-done.2
  111.9 0.0 copy-done.3
  111.9 0.0 copy-start.4
  111.9 0.0 copy-start.5
  111.9 0.8 fusion.2
  112.7 0.3 multiply_reduce_fusion
  113.0 0.0 copy-done.4
  113.0 0.0 copy-done.5
  113.0 1.0 add_convert_fusion
  (4 shorter events, 0.0 us)
Async XLA Ops:
  0.6 111.2 %copy-start = (bf16[1024,1024]{1,0:T(8,128)(2,1)S(1)}, bf16[1024,1024]{1,0:T(8,128)(2,1)}, u32[]{:S(2)}) copy-start(bf16[1024,1024]{1,0:T(8,128)(2,1)} %param.10) | copy-start | bytes 6291460
  57.7 1.2 %copy-start.1 = (bf16[16,193,256]{2,1,0:T(8,128)(2,1)}, bf16[16,193,256]{2,1,0:T(8,128)(2,1)S(1)}, u32[]{:S(2)}) copy-start(bf16[16,193,256]{2,1,0:T(8,128)(2,1)S(1)} %all_to_all.10) | copy-start | bytes 4743172
  90.9 20.9 %copy-start.2 = (bf16[256,1024]{1,0:T(8,128)(2,1)S(1)}, bf16[256,1024]{1,0:T(8,128)(2,1)}, u32[]{:S(2)}) copy-start(bf16[256,1024]{1,0:T(8,128)(2,1)} %param.7) | copy-start | bytes 1572868
  90.9 20.9 %copy-start.3 = (f32[1024]{0:T(1024)S(1)}, f32[1024]{0:T(1024)}, u32[]{:S(2)}) copy-start(f32[1024]{0:T(1024)} %param.11) | copy-start | bytes 12292
  90.9 20.9 %all-to-all-start.1 = ((bf16[16,64,256]{2,1,0:T(8,128)(2,1)}), bf16[16,64,256]{2,1,0:T(8,128)(2,1)S(1)}, u32[]{:S(2)}, u32[]{:S(2)}) async-start(bf16[16,64,256]{2,1,0:T(8,128)(2,1)} %shard_map.86), calls=%async_computation.1 | async-start | bytes 1048576 | tf_op jit(solution)/shard_map/all_to_all | solution.py:108
  111.9 1.1 copy-start.4
  111.9 1.1 copy-start.5

commit v15 on v14

--- a/solution.py
+++ b/solution.py
@@ -19,7 +19,7 @@
     return (x >= b1).astype(jnp.int32) + (x >= b2).astype(jnp.int32) + (x >= b3).astype(jnp.int32)
 
 
-def attn_kernel(cnt_ref, q_ref, kv_ref, o_ref):
+def attn_kernel(cnt_ref, q_ref, kv_ref, o_ref, pv_ref):
     i = pl.program_id(0)
     b1, b2, b3 = cnt_ref[1], cnt_ref[2], cnt_ref[3]
     q0 = i * BQ
@@ -37,20 +37,24 @@
     rows = q0 + lax.broadcasted_iota(jnp.int32, (BQ, 1), 0)
     sq = seg_of(rows, b1, b2, b3)
 
-    key_lanes = lax.broadcasted_iota(jnp.int32, (BK, 2 * HEAD), 1) < HEAD
+    @pl.when(i == 0)
+    def _():
+        key_lanes = lax.broadcasted_iota(jnp.int32, (BK, 2 * HEAD), 1) < HEAD
+        for b in range(pv_ref.shape[0]):
+            block = kv_ref[b, :, :2 * HEAD]
+            pv_ref[b] = jnp.where(key_lanes, jnp.ones_like(block), block)
 
     def tile(j, carry, masked):
         m, acc = carry
-        kv = kv_ref[j, :, :2 * HEAD]
-        s = lax.dot_general(q, kv[:, :HEAD], (((1,), (1,)), ((), ())), preferred_element_type=jnp.float32)
+        k = kv_ref[j, :, :HEAD]
+        s = lax.dot_general(q, k, (((1,), (1,)), ((), ())), preferred_element_type=jnp.float32)
         if masked:
             cols = j * BK + lax.broadcasted_iota(jnp.int32, (1, BK), 1)
             s = jnp.where(sq == seg_of(cols, b1, b2, b3), s, -jnp.inf)
         m_new = jnp.maximum(m, jnp.max(s, axis=1, keepdims=True))
         p = jnp.exp(s - m_new)
         alpha = jnp.exp(m - m_new)
-        rhs = jnp.where(key_lanes, jnp.ones_like(kv), kv)
-        acc = alpha * acc + jnp.dot(p.astype(jnp.bfloat16), rhs, preferred_element_type=jnp.float32)
+        acc = alpha * acc + jnp.dot(p.astype(jnp.bfloat16), pv_ref[j], preferred_element_type=jnp.float32)
         return m_new, acc
 
     def masked_tile(j, carry):
@@ -82,6 +86,7 @@
             pl.BlockSpec((nk, BK, feat), lambda i, cnt: (0, 0, 0)),
         ],
         out_specs=pl.BlockSpec((BQ // tok_rows, HEAD, tok_rows), lambda i, cnt: (i, 0, 0)),
+        scratch_shapes=[pltpu.VMEM((nk, BK, 2 * HEAD), jnp.bfloat16)],
     )
     return pl.pallas_call(
         attn_kernel,

time: 114 us -> 115 us (level)
  no operation moved by 1% of the time
where the time goes in v15:
time: 115 us; the launch traced here: 114 us
  blocking collectives  51.2 us (45%)
  Pallas kernels  27.8 us (24%)
  waiting for transfers between devices  15 us (13%)
  local copies, waits for them, and re-layouts  7.4 us (6%)
  matrix products  5.58 us (5%)
  starting transfers between devices  3.6 us (3%)
  other arithmetic  2.92 us (3%)
    all_to_all x1, blocking collectives, shards(): lax.all_to_all(payload, 'seq', split_axis=0, concat_axis=0, tiled=True)  51.2 us
    pallas_call x1, Pallas kernels, attention(): pl.pallas_call(attn_kernel, grid_spec=grid_spec, out_shape=jax.ShapeDtype...  27.8 us
    all_to_all x1, waiting for transfers between devices, shards(): lax.all_to_all(context, 'seq', split_axis=0, concat_axis=0, tiled=True)  15 us
    dot_general x1, matrix products, shards(): jnp.einsum('td,dc->ct', tokens, qkv_weight, preferred_element_type=jnp.fl...  4.75 us
    all_to_all x1, local copies, waits for them, and re-layouts, shards(): lax.all_to_all(payload, 'seq', split_axis=0, concat_axis=0, tiled=True)  3.72 us
    all_to_all x1, starting transfers between devices, shards(): lax.all_to_all(context, 'seq', split_axis=0, concat_axis=0, tiled=True)  3.6 us
  transfers between devices with their start and end apart: 1, of which 1 were waited for; matrix products, arithmetic and copies ran while one was open for 2% of the time, Pallas kernels for 0%

profile of v15, /device:TPU:1, one launch (start us, length us, event | category | flops | bytes accessed | tf_op | source)
XLA Modules:
  0.0 114.2 jit_solution(7712645471138583889)
XLA Ops:
  0.6 0.0 copy-start
  0.6 0.8 convert_element_type.26
  1.5 4.7 %convolution_convert_fusion = bf16[3072,256]{1,0:T(8,128)(2,1)S(1)} fusion(bf16[1024,3072]{1,0:T(8,128)(2,1)} %param.9, bf16[256,1024]{1,0:T(8,128)(2,1)} %param.7), kind=kOutput, calls=%fused_computation | convolution fusion | flops 1611399168 | bytes 8388608 | tf_op jit(solution)/shard_map/td,dc->ct/dot_general | solution.py:102
  6.2 0.2 slice_bitcast_fusion.2
  6.4 0.1 pad_maximum_fusion
  6.6 51.2 %all_to_all.10 = bf16[16,193,256]{2,1,0:T(8,128)(2,1)S(1)} all-to-all(bf16[16,193,256]{2,1,0:T(8,128)(2,1)S(1)} %pad_maximum_fusion), channel_id=1, replica_groups=mesh['seq'=16,'rep'=16] {'seq'}, dimensions={0} | all-to-all | bytes 3162112 | tf_op jit(solution)/shard_map/all_to_all | solution.py:106
  57.7 0.0 copy-start.1
  57.7 1.2 %copy-done.1 = bf16[16,193,256]{2,1,0:T(8,128)(2,1)} copy-done((bf16[16,193,256]{2,1,0:T(8,128)(2,1)}, bf16[16,193,256]{2,1,0:T(8,128)(2,1)S(1)}, u32[]{:S(2)}) %copy-start.1) | copy-done | bytes 1581080
  58.9 0.7 convert_reduce_fusion.cnt_ref
  59.6 3.7 %copy.30 = bf16[16,193,256]{1,2,0:T(8,128)(2,1)} copy(bf16[16,193,256]{2,1,0:T(8,128)(2,1)} %copy-done.1) | data formatting | bytes 3162112 | tf_op jit(solution)/shard_map/all_to_all | solution.py:106
  63.3 27.8 %shard_map.86 = bf16[16,64,256]{2,1,0:T(8,128)(2,1)} custom-call(s32[5]{0:T(128)} %convert_reduce_fusion.cnt_ref, bf16[8,512,193]{2,1,0:T(8,128)(2,1)} %bitcast.32, bf16[4,1024,193]{2,1,0:T(8,128)(2,1)} %bitcast.33), custom_call_target="tpu_custom_call" | custom-call | tf_op jit(solution)/shard_map/pallas_call | solution.py:91
  91.1 0.0 copy-start.2
  91.1 0.0 copy-start.3
  91.1 3.6 %all-to-all-start.1 = ((bf16[16,64,256]{2,1,0:T(8,128)(2,1)}), bf16[16,64,256]{2,1,0:T(8,128)(2,1)S(1)}, u32[]{:S(2)}, u32[]{:S(2)}) async-start(bf16[16,64,256]{2,1,0:T(8,128)(2,1)} %shard_map.86), calls=%async_computation.1 | async-start | bytes 1048576 | tf_op jit(solution)/shard_map/all_to_all | solution.py:113
  94.7 2.3 %slice.24 = bf16[16,256,128]{2,1,0:T(8,128)(2,1)} slice(bf16[16,256,193]{2,1,0:T(8,128)(2,1)} %bitcast.34), slice={[0:16], [0:256], [0:128]} | slice | bytes 2097152 | tf_op jit(solution)/shard_map/slice | solution.py:108
  97.0 15.0 %all-to-all-done.1 = bf16[16,64,256]{2,1,0:T(8,128)(2,1)S(1)} async-done(((bf16[16,64,256]{2,1,0:T(8,128)(2,1)}), bf16[16,64,256]{2,1,0:T(8,128)(2,1)S(1)}, u32[]{:S(2)}, u32[]{:S(2)}) %all-to-all-start.1) | async-done | bytes 524320 | tf_op jit(solution)/shard_map/all_to_all | solution.py:113
  112.0 0.0 copy-done
  112.0 0.0 copy-done.2
  112.0 0.0 copy-done.3
  112.0 0.0 copy-start.4
  112.0 0.0 copy-start.5
  112.0 0.8 fusion.2
  112.9 0.3 multiply_reduce_fusion
  113.1 0.0 copy-done.4
  113.1 0.0 copy-done.5
  113.2 1.0 add_convert_fusion
  (4 shorter events, 0.0 us)
Async XLA Ops:
  0.6 111.4 %copy-start = (bf16[1024,1024]{1,0:T(8,128)(2,1)S(1)}, bf16[1024,1024]{1,0:T(8,128)(2,1)}, u32[]{:S(2)}) copy-start(bf16[1024,1024]{1,0:T(8,128)(2,1)} %param.10) | copy-start | bytes 6291460
  57.7 1.2 %copy-start.1 = (bf16[16,193,256]{2,1,0:T(8,128)(2,1)}, bf16[16,193,256]{2,1,0:T(8,128)(2,1)S(1)}, u32[]{:S(2)}) copy-start(bf16[16,193,256]{2,1,0:T(8,128)(2,1)S(1)} %all_to_all.10) | copy-start | bytes 4743172
  91.1 20.9 %copy-start.2 = (bf16[256,1024]{1,0:T(8,128)(2,1)S(1)}, bf16[256,1024]{1,0:T(8,128)(2,1)}, u32[]{:S(2)}) copy-start(bf16[256,1024]{1,0:T(8,128)(2,1)} %param.7) | copy-start | bytes 1572868
  91.1 20.9 %copy-start.3 = (f32[1024]{0:T(1024)S(1)}, f32[1024]{0:T(1024)}, u32[]{:S(2)}) copy-start(f32[1024]{0:T(1024)} %param.11) | copy-start | bytes 12292
  91.1 20.9 %all-to-all-start.1 = ((bf16[16,64,256]{2,1,0:T(8,128)(2,1)}), bf16[16,64,256]{2,1,0:T(8,128)(2,1)S(1)}, u32[]{:S(2)}, u32[]{:S(2)}) async-start(bf16[16,64,256]{2,1,0:T(8,128)(2,1)} %shard_map.86), calls=%async_computation.1 | async-start | bytes 1048576 | tf_op jit(solution)/shard_map/all_to_all | solution.py:113
  112.0 1.1 copy-start.4
  112.0 1.1 copy-start.5

commit v16 on v14

--- a/solution.py
+++ b/solution.py
@@ -10,7 +10,7 @@
 HEADS = 16
 HEAD = 64
 SEGS = 4
-BQ = 512
+BQ = 1024
 BK = 1024
 INTERPRET = False
 

time: 114 us -> 114 us (level)
  the two profiles are of different devices: /device:TPU:1 before, /device:TPU:27 now
where the time goes in v16:
time: 114 us; the launch traced here: 113 us
  blocking collectives  50.3 us (44%)
  Pallas kernels  27.8 us (24%)
  waiting for transfers between devices  15 us (13%)
  local copies, waits for them, and re-layouts  7.4 us (6%)
  matrix products  5.57 us (5%)
  starting transfers between devices  3.61 us (3%)
  other arithmetic  2.92 us (3%)
    all_to_all x1, blocking collectives, shards(): lax.all_to_all(payload, 'seq', split_axis=0, concat_axis=0, tiled=True)  50.3 us
    pallas_call x1, Pallas kernels, attention(): pl.pallas_call(attn_kernel, grid_spec=grid_spec, out_shape=jax.ShapeDtype...  27.8 us
    all_to_all x1, waiting for transfers between devices, shards(): lax.all_to_all(context, 'seq', split_axis=0, concat_axis=0, tiled=True)  15 us
    dot_general x1, matrix products, shards(): jnp.einsum('td,dc->ct', tokens, qkv_weight, preferred_element_type=jnp.fl...  4.75 us
    all_to_all x1, local copies, waits for them, and re-layouts, shards(): lax.all_to_all(payload, 'seq', split_axis=0, concat_axis=0, tiled=True)  3.72 us
    all_to_all x1, starting transfers between devices, shards(): lax.all_to_all(context, 'seq', split_axis=0, concat_axis=0, tiled=True)  3.61 us
    slice x1, local copies, waits for them, and re-layouts, shards(): kv_cache = mine[:, :, :2 * HEAD].reshape(groups * tok_rows, 2 * HEAD)  2.3 us
  transfers between devices with their start and end apart: 1, of which 1 were waited for; matrix products, arithmetic and copies ran while one was open for 2% of the time, Pallas kernels for 0%

profile of v16, /device:TPU:27, one launch (start us, length us, event | category | flops | bytes accessed | tf_op | source)
XLA Modules:
  0.0 113.4 jit_solution(16776746406543371809)
XLA Ops:
  0.6 0.0 copy-start
  0.6 0.8 convert_element_type.26
  1.5 4.7 %convolution_convert_fusion = bf16[3072,256]{1,0:T(8,128)(2,1)S(1)} fusion(bf16[1024,3072]{1,0:T(8,128)(2,1)} %param.9, bf16[256,1024]{1,0:T(8,128)(2,1)} %param.7), kind=kOutput, calls=%fused_computation | convolution fusion | flops 1611399168 | bytes 8388608 | tf_op jit(solution)/shard_map/td,dc->ct/dot_general | solution.py:97
  6.2 0.2 slice_bitcast_fusion.2
  6.4 0.1 pad_maximum_fusion
  6.6 50.3 %all_to_all.10 = bf16[16,193,256]{2,1,0:T(8,128)(2,1)S(1)} all-to-all(bf16[16,193,256]{2,1,0:T(8,128)(2,1)S(1)} %pad_maximum_fusion), channel_id=1, replica_groups=mesh['seq'=16,'rep'=16] {'seq'}, dimensions={0} | all-to-all | bytes 3162112 | tf_op jit(solution)/shard_map/all_to_all | solution.py:101
  56.9 0.0 copy-start.1
  56.9 1.2 %copy-done.1 = bf16[16,193,256]{2,1,0:T(8,128)(2,1)} copy-done((bf16[16,193,256]{2,1,0:T(8,128)(2,1)}, bf16[16,193,256]{2,1,0:T(8,128)(2,1)S(1)}, u32[]{:S(2)}) %copy-start.1) | copy-done | bytes 1581080
  58.1 0.7 convert_reduce_fusion.cnt_ref
  58.8 3.7 %copy.28 = bf16[16,193,256]{1,2,0:T(8,128)(2,1)} copy(bf16[16,193,256]{2,1,0:T(8,128)(2,1)} %copy-done.1) | data formatting | bytes 3162112 | tf_op jit(solution)/shard_map/all_to_all | solution.py:101
  62.5 27.8 %shard_map.86 = bf16[16,64,256]{2,1,0:T(8,128)(2,1)} custom-call(s32[5]{0:T(128)} %convert_reduce_fusion.cnt_ref, bf16[4,1024,193]{2,1,0:T(8,128)(2,1)} %bitcast.30, bf16[4,1024,193]{2,1,0:T(8,128)(2,1)} %bitcast.31), custom_call_target="tpu_custom_call" | custom-call | tf_op jit(solution)/shard_map/pallas_call | solution.py:86
  90.3 0.0 copy-start.2
  90.3 0.0 copy-start.3
  90.3 3.6 %all-to-all-start.1 = ((bf16[16,64,256]{2,1,0:T(8,128)(2,1)}), bf16[16,64,256]{2,1,0:T(8,128)(2,1)S(1)}, u32[]{:S(2)}, u32[]{:S(2)}) async-start(bf16[16,64,256]{2,1,0:T(8,128)(2,1)} %shard_map.86), calls=%async_computation.1 | async-start | bytes 1048576 | tf_op jit(solution)/shard_map/all_to_all | solution.py:108
  93.9 2.3 %slice.24 = bf16[16,256,128]{2,1,0:T(8,128)(2,1)} slice(bf16[16,256,193]{2,1,0:T(8,128)(2,1)} %bitcast.32), slice={[0:16], [0:256], [0:128]} | slice | bytes 2097152 | tf_op jit(solution)/shard_map/slice | solution.py:103
  96.2 15.0 %all-to-all-done.1 = bf16[16,64,256]{2,1,0:T(8,128)(2,1)S(1)} async-done(((bf16[16,64,256]{2,1,0:T(8,128)(2,1)}), bf16[16,64,256]{2,1,0:T(8,128)(2,1)S(1)}, u32[]{:S(2)}, u32[]{:S(2)}) %all-to-all-start.1) | async-done | bytes 524320 | tf_op jit(solution)/shard_map/all_to_all | solution.py:108
  111.2 0.0 copy-done
  111.2 0.0 copy-done.2
  111.2 0.0 copy-done.3
  111.2 0.0 copy-start.4
  111.2 0.0 copy-start.5
  111.2 0.8 fusion.2
  112.1 0.3 multiply_reduce_fusion
  112.4 0.0 copy-done.4
  112.4 0.0 copy-done.5
  112.4 1.0 add_convert_fusion
  (4 shorter events, 0.0 us)
Async XLA Ops:
  0.6 110.6 %copy-start = (bf16[1024,1024]{1,0:T(8,128)(2,1)S(1)}, bf16[1024,1024]{1,0:T(8,128)(2,1)}, u32[]{:S(2)}) copy-start(bf16[1024,1024]{1,0:T(8,128)(2,1)} %param.10) | copy-start | bytes 6291460
  56.9 1.2 %copy-start.1 = (bf16[16,193,256]{2,1,0:T(8,128)(2,1)}, bf16[16,193,256]{2,1,0:T(8,128)(2,1)S(1)}, u32[]{:S(2)}) copy-start(bf16[16,193,256]{2,1,0:T(8,128)(2,1)S(1)} %all_to_all.10) | copy-start | bytes 4743172
  90.3 20.9 %copy-start.2 = (bf16[256,1024]{1,0:T(8,128)(2,1)S(1)}, bf16[256,1024]{1,0:T(8,128)(2,1)}, u32[]{:S(2)}) copy-start(bf16[256,1024]{1,0:T(8,128)(2,1)} %param.7) | copy-start | bytes 1572868
  90.3 20.9 %copy-start.3 = (f32[1024]{0:T(1024)S(1)}, f32[1024]{0:T(1024)}, u32[]{:S(2)}) copy-start(f32[1024]{0:T(1024)} %param.11) | copy-start | bytes 12292
  90.3 20.9 %all-to-all-start.1 = ((bf16[16,64,256]{2,1,0:T(8,128)(2,1)}), bf16[16,64,256]{2,1,0:T(8,128)(2,1)S(1)}, u32[]{:S(2)}, u32[]{:S(2)}) async-start(bf16[16,64,256]{2,1,0:T(8,128)(2,1)} %shard_map.86), calls=%async_computation.1 | async-start | bytes 1048576 | tf_op jit(solution)/shard_map/all_to_all | solution.py:108
  111.2 1.1 copy-start.4
  111.2 1.1 copy-start.5

commit v17 on v16

--- a/solution.py
+++ b/solution.py
@@ -11,7 +11,7 @@
 HEAD = 64
 SEGS = 4
 BQ = 1024
-BK = 1024
+BK = 512
 INTERPRET = False
 
 

time: 114 us -> 116 us (1.018)
  the two profiles are of different devices: /device:TPU:27 before, /device:TPU:1 now
where the time goes in v17:
time: 116 us
  blocking collectives  51.2 us (44%)
  Pallas kernels  29.8 us (26%)
  waiting for transfers between devices  15 us (13%)
  local copies, waits for them, and re-layouts  7.4 us (6%)
  matrix products  5.58 us (5%)
  starting transfers between devices  3.61 us (3%)
  other arithmetic  2.92 us (3%)
    all_to_all x1, blocking collectives, shards(): lax.all_to_all(payload, 'seq', split_axis=0, concat_axis=0, tiled=True)  51.2 us
    pallas_call x1, Pallas kernels, attention(): pl.pallas_call(attn_kernel, grid_spec=grid_spec, out_shape=jax.ShapeDtype...  29.8 us
    all_to_all x1, waiting for transfers between devices, shards(): lax.all_to_all(context, 'seq', split_axis=0, concat_axis=0, tiled=True)  15 us
    dot_general x1, matrix products, shards(): jnp.einsum('td,dc->ct', tokens, qkv_weight, preferred_element_type=jnp.fl...  4.75 us
    all_to_all x1, local copies, waits for them, and re-layouts, shards(): lax.all_to_all(payload, 'seq', split_axis=0, concat_axis=0, tiled=True)  3.72 us
    all_to_all x1, starting transfers between devices, shards(): lax.all_to_all(context, 'seq', split_axis=0, concat_axis=0, tiled=True)  3.61 us
  transfers between devices with their start and end apart: 1, of which 1 were waited for; matrix products, arithmetic and copies ran while one was open for 2% of the time, Pallas kernels for 0%

profile of v17, /device:TPU:1, one launch (start us, length us, event | category | flops | bytes accessed | tf_op | source)
XLA Modules:
  0.0 116.3 jit_solution(12085407102483009841)
XLA Ops:
  0.6 0.0 copy-start
  0.6 0.8 convert_element_type.26
  1.5 4.7 %convolution_convert_fusion = bf16[3072,256]{1,0:T(8,128)(2,1)S(1)} fusion(bf16[1024,3072]{1,0:T(8,128)(2,1)} %param.9, bf16[256,1024]{1,0:T(8,128)(2,1)} %param.7), kind=kOutput, calls=%fused_computation | convolution fusion | flops 1611399168 | bytes 8388608 | tf_op jit(solution)/shard_map/td,dc->ct/dot_general | solution.py:97
  6.2 0.2 slice_bitcast_fusion.2
  6.4 0.1 pad_maximum_fusion
  6.6 51.2 %all_to_all.10 = bf16[16,193,256]{2,1,0:T(8,128)(2,1)S(1)} all-to-all(bf16[16,193,256]{2,1,0:T(8,128)(2,1)S(1)} %pad_maximum_fusion), channel_id=1, replica_groups=mesh['seq'=16,'rep'=16] {'seq'}, dimensions={0} | all-to-all | bytes 3162112 | tf_op jit(solution)/shard_map/all_to_all | solution.py:101
  57.7 0.0 copy-start.1
  57.7 1.2 %copy-done.1 = bf16[16,193,256]{2,1,0:T(8,128)(2,1)} copy-done((bf16[16,193,256]{2,1,0:T(8,128)(2,1)}, bf16[16,193,256]{2,1,0:T(8,128)(2,1)S(1)}, u32[]{:S(2)}) %copy-start.1) | copy-done | bytes 1581080
  58.9 0.7 convert_reduce_fusion.cnt_ref
  59.6 3.7 %copy.30 = bf16[16,193,256]{1,2,0:T(8,128)(2,1)} copy(bf16[16,193,256]{2,1,0:T(8,128)(2,1)} %copy-done.1) | data formatting | bytes 3162112 | tf_op jit(solution)/shard_map/all_to_all | solution.py:101
  63.3 29.8 %shard_map.86 = bf16[16,64,256]{2,1,0:T(8,128)(2,1)} custom-call(s32[5]{0:T(128)} %convert_reduce_fusion.cnt_ref, bf16[4,1024,193]{2,1,0:T(8,128)(2,1)} %bitcast.32, bf16[8,512,193]{2,1,0:T(8,128)(2,1)} %bitcast.33), custom_call_target="tpu_custom_call" | custom-call | tf_op jit(solution)/shard_map/pallas_call | solution.py:86
  93.1 0.0 copy-start.2
  93.1 0.0 copy-start.3
  93.1 3.6 %all-to-all-start.1 = ((bf16[16,64,256]{2,1,0:T(8,128)(2,1)}), bf16[16,64,256]{2,1,0:T(8,128)(2,1)S(1)}, u32[]{:S(2)}, u32[]{:S(2)}) async-start(bf16[16,64,256]{2,1,0:T(8,128)(2,1)} %shard_map.86), calls=%async_computation.1 | async-start | bytes 1048576 | tf_op jit(solution)/shard_map/all_to_all | solution.py:108
  96.8 2.3 %slice.24 = bf16[16,256,128]{2,1,0:T(8,128)(2,1)} slice(bf16[16,256,193]{2,1,0:T(8,128)(2,1)} %bitcast.34), slice={[0:16], [0:256], [0:128]} | slice | bytes 2097152 | tf_op jit(solution)/shard_map/slice | solution.py:103
  99.0 15.0 %all-to-all-done.1 = bf16[16,64,256]{2,1,0:T(8,128)(2,1)S(1)} async-done(((bf16[16,64,256]{2,1,0:T(8,128)(2,1)}), bf16[16,64,256]{2,1,0:T(8,128)(2,1)S(1)}, u32[]{:S(2)}, u32[]{:S(2)}) %all-to-all-start.1) | async-done | bytes 524320 | tf_op jit(solution)/shard_map/all_to_all | solution.py:108
  114.1 0.0 copy-done
  114.1 0.0 copy-done.2
  114.1 0.0 copy-done.3
  114.1 0.0 copy-start.4
  114.1 0.0 copy-start.5
  114.1 0.8 fusion.2
  114.9 0.3 multiply_reduce_fusion
  115.2 0.0 copy-done.4
  115.2 0.0 copy-done.5
  115.2 1.0 add_convert_fusion
  (4 shorter events, 0.0 us)
Async XLA Ops:
  0.6 113.4 %copy-start = (bf16[1024,1024]{1,0:T(8,128)(2,1)S(1)}, bf16[1024,1024]{1,0:T(8,128)(2,1)}, u32[]{:S(2)}) copy-start(bf16[1024,1024]{1,0:T(8,128)(2,1)} %param.10) | copy-start | bytes 6291460
  57.7 1.2 %copy-start.1 = (bf16[16,193,256]{2,1,0:T(8,128)(2,1)}, bf16[16,193,256]{2,1,0:T(8,128)(2,1)S(1)}, u32[]{:S(2)}) copy-start(bf16[16,193,256]{2,1,0:T(8,128)(2,1)S(1)} %all_to_all.10) | copy-start | bytes 4743172
  93.1 20.9 %copy-start.2 = (bf16[256,1024]{1,0:T(8,128)(2,1)S(1)}, bf16[256,1024]{1,0:T(8,128)(2,1)}, u32[]{:S(2)}) copy-start(bf16[256,1024]{1,0:T(8,128)(2,1)} %param.7) | copy-start | bytes 1572868
  93.1 20.9 %copy-start.3 = (f32[1024]{0:T(1024)S(1)}, f32[1024]{0:T(1024)}, u32[]{:S(2)}) copy-start(f32[1024]{0:T(1024)} %param.11) | copy-start | bytes 12292
  93.1 20.9 %all-to-all-start.1 = ((bf16[16,64,256]{2,1,0:T(8,128)(2,1)}), bf16[16,64,256]{2,1,0:T(8,128)(2,1)S(1)}, u32[]{:S(2)}, u32[]{:S(2)}) async-start(bf16[16,64,256]{2,1,0:T(8,128)(2,1)} %shard_map.86), calls=%async_computation.1 | async-start | bytes 1048576 | tf_op jit(solution)/shard_map/all_to_all | solution.py:108
  114.1 1.1 copy-start.4
  114.1 1.1 copy-start.5
